TPU v7x, 32 devices: a whole 2x2x4 slice. The times are simulated.
32 devices in a mesh: dp: 16 (over z, x, core), head: 2 (over y).
Axes of the slice: x: 2, y: 2, z: 4, core: 2. Of those that a mesh axis runs over, the one named last changes fastest.
Arguments:
- tokens: bfloat16 [16384, 1024], P(('dp', 'head')), may hold values from -6 to 6
- lengths: int32 [16], P('dp'), may hold values from 128 to 1024, as said below
- decay: float32 [8], P('head'), may hold values from 0.00048828125 to 0.03125
- w_query: bfloat16 [1024, 1024], P(None, 'head'), may hold values from -0.1875 to 0.1875
- w_key: bfloat16 [1024, 1024], P(None, 'head'), may hold values from -0.1875 to 0.1875
- w_value: bfloat16 [1024, 1024], P(None, 'head'), may hold values from -0.1875 to 0.1875
- w_gate: bfloat16 [1024, 1024], P(None, 'head'), may hold values from -0.1875 to 0.1875
- w_out: bfloat16 [1024, 1024], P('head'), may hold values from -0.1875 to 0.1875
- f_value: bfloat16 [1024, 2816], P('dp', 'head'), may hold values from -0.1875 to 0.1875
- f_gate: bfloat16 [1024, 2816], P('dp', 'head'), may hold values from -0.1875 to 0.1875
- f_out: bfloat16 [2816, 1024], P('head', 'dp'), may hold values from -0.109375 to 0.109375
- cotangent: bfloat16 [16384, 1024], P(('dp', 'head')), may hold values from -6 to 6
Outputs:
- output: bfloat16 [16384, 1024], P(('dp', 'head'))
- d_tokens: float32 [16384, 1024], P(('dp', 'head'))
- d_w_query: float32 [1024, 1024], P(None, 'head')
- d_w_key: float32 [1024, 1024], P(None, 'head')
- d_w_value: float32 [1024, 1024], P(None, 'head')
- d_w_gate: float32 [1024, 1024], P(None, 'head')
- d_w_out: float32 [1024, 1024], P('head')
- d_f_value: float32 [1024, 2816], P('dp', 'head')
- d_f_gate: float32 [1024, 2816], P('dp', 'head')
- d_f_out: float32 [2816, 1024], P('head', 'dp')
Inputs may be any that keep to these rules, and one draw needn't show every extreme that they name: `lengths`: each bucket holds a single slot, and that slot's sequence has length 1024.
All inputs are finite; a program needn't handle non-finite values.
Results may differ from a plain program's by a relative error of at most 0.022.
Values may be sent and summed in bfloat16 or wider, within the bound.
A program may use at most 192 MiB of HBM per device.

v0:
```python
import jax
import jax.numpy as jnp
from jax import lax
from jax.sharding import PartitionSpec as P

D = 1024
HD = 128
SEQ_DEV = 1
SLOT = 1024
BLOCK = 512


epsilon = 1e-06


def normalize(values):
    factor = lax.rsqrt(jnp.mean(values * values, axis=-1, keepdims=True) + epsilon)
    return (values * factor, factor)


def norm_back(grad_normed, normed, factor):
    inner_sum = jnp.mean(grad_normed * normed, axis=-1, keepdims=True)
    return factor * (grad_normed - normed * inner_sum)


def silu_slope(values):
    sigmoid = jax.nn.sigmoid(values)
    return sigmoid * (1.0 + values * (1.0 - sigmoid))


def matmul(left_side, right_side):
    return jnp.dot(left_side, right_side, preferred_element_type=jnp.float32)


def matmul_right_t(left_side, right_side):
    return lax.dot_general(
        left_side, right_side, (((1,), (1,)), ((), ())), preferred_element_type=jnp.float32
    )


def matmul_left_t(left_side, right_side):
    return lax.dot_general(
        left_side, right_side, (((0,), (0,)), ((), ())), preferred_element_type=jnp.float32
    )


def exact(form, left_side, right_side):
    return jnp.einsum(form, left_side, right_side, precision=lax.Precision.HIGHEST)


def decay_tables(rates):
    offsets = jnp.arange(BLOCK).astype(jnp.float32)
    spread = offsets[:, None] - offsets[None, :]
    causal = spread >= 0
    within = jnp.where(
        causal[None], jnp.exp(-rates[:, None, None] * jnp.where(causal, spread, 0.0)[None]), 0.0
    )
    first_decay = jnp.exp(-rates[:, None] * (offsets[None, :] + 1.0))
    last_decay = jnp.exp(-rates[:, None] * (BLOCK - 1.0 - offsets[None, :]))
    block_decay = jnp.exp(-rates * BLOCK)
    return (within, first_decay, last_decay, block_decay)


def to_blocks(values, heads):
    shaped = values.reshape(SEQ_DEV, SLOT // BLOCK, BLOCK, heads, HD)
    return shaped.transpose(1, 0, 3, 2, 4)


def from_blocks(blocks):
    return blocks.transpose(1, 0, 3, 2, 4).reshape(-1, blocks.shape[2] * blocks.shape[4])


def lightning_forward(query, keys, values, tables):
    within, first_decay, last_decay, block_decay = tables

    def advance(carried, inputs):
        query_blk, keys_blk, values_blk = inputs
        scores = jnp.einsum(
            "shbd,shcd->shbc", query_blk, keys_blk, preferred_element_type=jnp.float32
        )
        weights = (scores * within[None]).astype(jnp.bfloat16)
        inner_sum = jnp.einsum(
            "shbc,shcd->shbd", weights, values_blk, preferred_element_type=jnp.float32
        )
        outer_sum = first_decay[None, :, :, None] * exact(
            "shbd,shde->shbe", query_blk.astype(jnp.float32), carried
        )
        keys_scaled = keys_blk.astype(jnp.float32) * last_decay[None, :, :, None]
        update = exact("shbd,shbe->shde", keys_scaled, values_blk.astype(jnp.float32))
        return (
            block_decay[None, :, None, None] * carried + update,
            (inner_sum + outer_sum, carried),
        )

    initial = jnp.zeros((SEQ_DEV, query.shape[2], HD, HD), jnp.float32)
    final_state, (mixed, states) = lax.scan(advance, initial, (query, keys, values))
    return (mixed, states)


def lightning_backward(query, keys, values, grads, states, tables):
    within, first_decay, last_decay, block_decay = tables

    def retreat(later_grad, inputs):
        query_blk, keys_blk, values_blk, grad_blk, carried = inputs
        scores = jnp.einsum(
            "shbd,shcd->shbc", query_blk, keys_blk, preferred_element_type=jnp.float32
        )
        weights = (scores * within[None]).astype(jnp.bfloat16)
        d_weights = jnp.einsum(
            "shbd,shcd->shbc", grad_blk, values_blk, preferred_element_type=jnp.float32
        )
        d_scores = (d_weights * within[None]).astype(jnp.bfloat16)
        d_query = jnp.einsum(
            "shbc,shcd->shbd", d_scores, keys_blk, preferred_element_type=jnp.float32
        )
        d_keys = jnp.einsum(
            "shbc,shbd->shcd", d_scores, query_blk, preferred_element_type=jnp.float32
        )
        d_values = jnp.einsum(
            "shbc,shbd->shcd", weights, grad_blk, preferred_element_type=jnp.float32
        )
        grad_scaled = grad_blk.astype(jnp.float32) * first_decay[None, :, :, None]
        keys_scaled = keys_blk.astype(jnp.float32) * last_decay[None, :, :, None]
        d_query = d_query + exact("shbe,shde->shbd", grad_scaled, carried)
        d_keys = d_keys + last_decay[None, :, :, None] * exact(
            "shbe,shde->shbd", values_blk.astype(jnp.float32), later_grad
        )
        d_values = d_values + exact("shbd,shde->shbe", keys_scaled, later_grad)
        earlier = block_decay[None, :, None, None] * later_grad + exact(
            "shbd,shbe->shde", query_blk.astype(jnp.float32), grad_scaled
        )
        return (earlier, (d_query, d_keys, d_values))

    initial = jnp.zeros((SEQ_DEV, query.shape[2], HD, HD), jnp.float32)
    first_grad, results = lax.scan(
        retreat, initial, (query, keys, values, grads, states), reverse=True
    )
    return results


def body(
    tokens,
    lengths,
    decay,
    w_query,
    w_key,
    w_value,
    w_gate,
    w_out,
    f_value,
    f_gate,
    f_out,
    cotangent,
):
    own_rows = tokens.shape[0]
    first_row = lax.axis_index("head") * own_rows
    heads_here = decay.shape[0]
    tables = decay_tables(decay)
    positions = first_row + jnp.arange(own_rows, dtype=jnp.int32)
    slot_match = (positions // SLOT)[:, None] == jnp.arange(SEQ_DEV, dtype=jnp.int32)[None, :]
    length_of = jnp.sum(jnp.where(slot_match, lengths[None, :], 0), axis=1)
    keep_rows = (positions % SLOT < length_of).astype(jnp.float32)[:, None]
    inputs_f = tokens.astype(jnp.float32)
    normed, scale_in = normalize(inputs_f)
    gathered = lax.all_gather(normed.astype(jnp.bfloat16), "head", axis=0, tiled=True)
    query_pre = matmul(gathered, w_query)
    keys_pre = matmul(gathered, w_key)
    values_pre = matmul(gathered, w_value)
    gate_pre = matmul(gathered, w_gate)
    query_blocks = to_blocks(jax.nn.silu(query_pre).astype(jnp.bfloat16), heads_here)
    keys_blocks = to_blocks(jax.nn.silu(keys_pre).astype(jnp.bfloat16), heads_here)
    values_blocks = to_blocks(values_pre.astype(jnp.bfloat16), heads_here)
    mixed_blocks, states = lightning_forward(query_blocks, keys_blocks, values_blocks, tables)
    mixed = from_blocks(mixed_blocks)
    squares = lax.psum(jnp.sum(mixed * mixed, axis=1), "head")
    scale_out = lax.rsqrt(squares / D + epsilon)[:, None]
    mixed_unit = mixed * scale_out
    gated = (mixed_unit * gate_pre).astype(jnp.bfloat16)
    branch = lax.psum_scatter(
        matmul(gated, w_out).astype(jnp.bfloat16), "head", scatter_dimension=0, tiled=True
    ).astype(jnp.float32)
    middle = inputs_f + branch
    mid_normed, scale_mid = normalize(middle)
    mid_all = lax.all_gather(mid_normed.astype(jnp.bfloat16), "head", axis=0, tiled=True)
    value_full, gate_full = (
        lax.all_gather(f_value, "dp", axis=0, tiled=True),
        lax.all_gather(f_gate, "dp", axis=0, tiled=True),
    )
    down_full = lax.all_gather(f_out, "dp", axis=1, tiled=True)
    value_ffn = matmul(mid_all, value_full)
    gate_ffn = matmul(mid_all, gate_full)
    hidden = (value_ffn * gate_ffn).astype(jnp.bfloat16)
    ffn_branch = lax.psum_scatter(
        matmul(hidden, down_full).astype(jnp.bfloat16), "head", scatter_dimension=0, tiled=True
    ).astype(jnp.float32)
    output = ((middle + ffn_branch) * keep_rows).astype(jnp.bfloat16)
    grad_out = cotangent.astype(jnp.float32) * keep_rows
    grad_all = lax.all_gather(grad_out.astype(jnp.bfloat16), "head", axis=0, tiled=True)
    grad_hidden = matmul_right_t(grad_all, down_full)
    d_value_ffn = (grad_hidden * gate_ffn).astype(jnp.bfloat16)
    d_gate_ffn = (grad_hidden * value_ffn).astype(jnp.bfloat16)
    d_mid_normed = lax.psum_scatter(
        (matmul_right_t(d_value_ffn, value_full) + matmul_right_t(d_gate_ffn, gate_full)).astype(
            jnp.bfloat16
        ),
        "head",
        scatter_dimension=0,
        tiled=True,
    ).astype(jnp.float32)
    grad_middle = grad_out + norm_back(d_mid_normed, mid_normed, scale_mid)
    joined = jnp.concatenate([d_value_ffn, d_gate_ffn], axis=1)
    hidden_here = hidden.shape[1]
    shares = lax.psum_scatter(
        jnp.concatenate(
            [matmul_left_t(mid_all, joined), matmul_left_t(grad_all, hidden)], axis=1
        ).astype(jnp.bfloat16),
        "dp",
        scatter_dimension=0,
        tiled=True,
    ).astype(jnp.float32)
    d_f_value = shares[:, :hidden_here]
    d_f_gate = shares[:, hidden_here : 2 * hidden_here]
    d_f_out = shares[:, 2 * hidden_here :].T
    grad_rows = lax.all_gather(grad_middle.astype(jnp.bfloat16), "head", axis=0, tiled=True)
    d_gated = matmul_right_t(grad_rows, w_out)
    d_w_out_local = matmul_left_t(gated, grad_rows)
    d_gate_pre = (d_gated * mixed_unit).astype(jnp.bfloat16)
    d_unit = d_gated * gate_pre
    inner_out = lax.psum(jnp.sum(d_unit * mixed_unit, axis=1), "head")
    d_mixed = (scale_out * (d_unit - mixed_unit * (inner_out / D)[:, None])).astype(jnp.bfloat16)
    d_query, d_keys, d_values = lightning_backward(
        query_blocks, keys_blocks, values_blocks, to_blocks(d_mixed, heads_here), states, tables
    )
    d_query_pre = (from_blocks(d_query) * silu_slope(query_pre)).astype(jnp.bfloat16)
    d_keys_pre = (from_blocks(d_keys) * silu_slope(keys_pre)).astype(jnp.bfloat16)
    d_values_pre = from_blocks(d_values).astype(jnp.bfloat16)
    total = matmul_right_t(d_query_pre, w_query) + matmul_right_t(d_keys_pre, w_key)
    d_normed = lax.psum_scatter(
        (total + matmul_right_t(d_values_pre, w_value) + matmul_right_t(d_gate_pre, w_gate)).astype(
            jnp.bfloat16
        ),
        "head",
        scatter_dimension=0,
        tiled=True,
    ).astype(jnp.float32)
    d_tokens = grad_middle + norm_back(d_normed, normed, scale_in)
    grads_attention = (
        lax.psum(matmul_left_t(gathered, d_query_pre).astype(jnp.bfloat16), "dp").astype(
            jnp.float32
        ),
        lax.psum(matmul_left_t(gathered, d_keys_pre).astype(jnp.bfloat16), "dp").astype(
            jnp.float32
        ),
        lax.psum(matmul_left_t(gathered, d_values_pre).astype(jnp.bfloat16), "dp").astype(
            jnp.float32
        ),
        lax.psum(matmul_left_t(gathered, d_gate_pre).astype(jnp.bfloat16), "dp").astype(
            jnp.float32
        ),
        lax.psum(d_w_out_local.astype(jnp.bfloat16), "dp").astype(jnp.float32),
    )
    return (
        output,
        d_tokens,
        grads_attention[0],
        grads_attention[1],
        grads_attention[2],
        grads_attention[3],
        grads_attention[4],
        d_f_value,
        d_f_gate,
        d_f_out,
    )


def solution(mesh):
    placed = (
        P(("dp", "head"), None),
        P("dp"),
        P("head"),
        P(None, "head"),
        P(None, "head"),
        P(None, "head"),
        P(None, "head"),
        P("head", None),
        P("dp", "head"),
        P("dp", "head"),
        P("head", "dp"),
        P(("dp", "head"), None),
    )
    return jax.shard_map(
        body,
        mesh=mesh,
        in_specs=placed,
        out_specs=(
            P(("dp", "head"), None),
            P(("dp", "head"), None),
            P(None, "head"),
            P(None, "head"),
            P(None, "head"),
            P(None, "head"),
            P("head", None),
            P("dp", "head"),
            P("dp", "head"),
            P("head", "dp"),
        ),
        check_vma=False,
    )
```

profile of v0, /device:TPU:1, one launch (start us, length us, event | category | flops | bytes accessed | tf_op | source)
XLA Modules:
  0.0 685.4 jit_solution(16797415050043910649)
XLA Ops:
  15.0 33.1 %all-gather.8.cloned.1.call-done = bf16[1024,1024]{1,0:T(8,128)(2,1)} async-done(((bf16[512,1024]{1,0:T(8,128)(2,1)}), bf16[1024,1024]{1,0:T(8,128)(2,1)}) %all-gather.8.cloned.1.call-update) | async-done | bytes 2097168 | tf_op jit(solution)/shard_map/all_gather | solution.py:165
  48.2 4.4 multiply_convert_fusion.8
  52.8 3.1 convolution_convert_fusion.8
  58.5 2.8 copy_bitcast_fusion.1
  61.2 3.1 multiply_convert_fusion.7
  68.4 15.1 %while.40 = (s32[]{:T(128)}, f32[1,4,128,128]{3,2,1,0:T(8,128)S(1)}, f32[2,1,4,512,128]{4,3,2,1,0:T(8,128)}, f32[2,1,4,128,128]{4,3,2,1,0:T(8,128)}, f32[4]{0:T(...) while((s32[]{:T(128)}, ...), condition=%wide.region_2.3_spmd.clone.clone.clone, body=%wide.region_1.2_spmd.clone.clone.clone.sunk | while | flops 1347751936 | bytes 17343232 | solution.py:96
  68.4 3.0 fusion.246
  71.6 2.7 fusion.247
  76.0 3.0 fusion.246
  79.1 2.7 fusion.247
  85.7 4.1 copy.42
  91.9 4.0 psum.49
  95.9 4.5 multiply_convert_fusion.6
  104.7 32.5 %reduce-scatter.6.cloned.1.call-done = bf16[512,1024]{1,0:T(8,128)(2,1)} async-done(((bf16[1024,1024]{1,0:T(8,128)(2,1)}), bf16[512,1024]{1,0:T(8,128)(2,1)}) %reduce-scatter.6.cloned.1.call-update) | async-done | bytes 1048592 | tf_op jit(solution)/shard_map/reduce_scatter | solution.py:179
  144.8 7.8 %all-gather.12.cloned.1.call-done = bf16[1024,1408]{1,0:T(8,128)(2,1)} async-done(((bf16[64,1408]{1,0:T(8,128)(2,1)}), bf16[1024,1408]{1,0:T(8,128)(2,1)}) %all-gather.12.cloned.1.call-update) | async-done | bytes 2883600 | tf_op jit(solution)/shard_map/all_gather | solution.py:186
  152.7 33.2 %all-gather.10.cloned.1.call-done = bf16[1024,1024]{1,0:T(8,128)(2,1)} async-done(((bf16[512,1024]{1,0:T(8,128)(2,1)}), bf16[1024,1024]{1,0:T(8,128)(2,1)}) %all-gather.10.cloned.1.call-update) | async-done | bytes 2097168 | tf_op jit(solution)/shard_map/all_gather | solution.py:184
  185.9 8.3 %fusion.155 = f32[1024,1408]{1,0:T(8,128)} fusion(bf16[1024,1024]{1,0:T(8,128)(2,1)} %all-gather.10.cloned.1.call-done, bf16[1024,1408]{1,0:T(8,128)(2,1)} %all-gather.12.cloned.1.call-done), kind=kOutput, calls=%fused_computation.209 | convolution fusion | flops 2952790016 | bytes 10747904 | tf_op jit(solution)/shard_map/dot_general | solution.py:32
  194.2 38.6 %all-gather.14.cloned.1.call-done = bf16[1024,1408]{1,0:T(8,128)(2,1)} async-done(((bf16[64,1408]{1,0:T(8,128)(2,1)}), bf16[1024,1408]{1,0:T(8,128)(2,1)}) %all-gather.14.cloned.1.call-update) | async-done | bytes 2883600 | tf_op jit(solution)/shard_map/all_gather | solution.py:187
  232.8 8.4 %fusion.156 = f32[1024,1408]{1,0:T(8,128)} fusion(bf16[1024,1024]{1,0:T(8,128)(2,1)} %all-gather.10.cloned.1.call-done, bf16[1024,1408]{1,0:T(8,128)(2,1)} %all-gather.14.cloned.1.call-done), kind=kOutput, calls=%fused_computation.210 | convolution fusion | flops 2952790016 | bytes 10747904 | tf_op jit(solution)/shard_map/dot_general | solution.py:32
  241.2 24.9 %all-gather.18.cloned.1.call-done = bf16[1024,1024]{1,0:T(8,128)(2,1)} async-done(((bf16[512,1024]{1,0:T(8,128)(2,1)}), bf16[1024,1024]{1,0:T(8,128)(2,1)}) %all-gather.18.cloned.1.call-update) | async-done | bytes 2097168 | tf_op jit(solution)/shard_map/all_gather | solution.py:198
  266.1 47.1 %all-gather.16.cloned.1.call-done = bf16[1408,1024]{0,1:T(8,128)(2,1)} async-done(((bf16[1408,64]{0,1:T(8,128)(2,1)}), bf16[1408,1024]{0,1:T(8,128)(2,1)}) %all-gather.16.cloned.1.call-update) | async-done | bytes 2883600 | tf_op jit(solution)/shard_map/all_gather | solution.py:189
  313.2 11.0 %multiply_convert_fusion = (bf16[1024,1408]{1,0:T(8,128)(2,1)S(1)}, bf16[1024,1408]{1,0:T(8,128)(2,1)}, bf16[1024,1408]{1,0:T(8,128)(2,1)S(1)}) fusion(f32[1024,1408]{1,0:T(8,128)} %fusion.155, f32[1024,1408]{1,0:T(8,128)} %fusion.156, bf16[1024,1024]{1,0:T(8,128)(2,1)} %all-gather.18.cloned.1.call-done, bf16[1408,1024]{0,1:T(8,128)(2,1)} %all-gather.16.cloned.1.call-done), kind=kOutput, calls=%fused_computation.120 | convolution fusion | flops 2961440768 | bytes 25165824 | tf_op jit(solution)/shard_map/dot_general | solution.py:36
  324.2 3.4 fusion.157
  328.1 4.6 add_convert_fusion.1
  332.8 30.2 %reduce-scatter.10.cloned.1.call-done = bf16[512,1024]{1,0:T(8,128)(2,1)} async-done(((bf16[1024,1024]{1,0:T(8,128)(2,1)}), bf16[512,1024]{1,0:T(8,128)(2,1)}) %reduce-scatter.10.cloned.1.call-update) | async-done | bytes 1048592 | tf_op jit(solution)/shard_map/reduce_scatter | solution.py:202
  370.9 29.3 %all-gather.20.cloned.1.call-done = bf16[1024,1024]{1,0:T(8,128)(2,1)} async-done(((bf16[512,1024]{1,0:T(8,128)(2,1)}), bf16[1024,1024]{1,0:T(8,128)(2,1)}) %all-gather.20.cloned.1.call-update) | async-done | bytes 2097168 | tf_op jit(solution)/shard_map/all_gather | solution.py:224
  400.2 5.3 multiply_reduce_fusion
  405.5 3.8 psum.50
  417.2 36.7 %while.41 = (s32[]{:T(128)}, f32[1,4,128,128]{3,2,1,0:T(8,128)S(1)}, f32[2,1,4,512,128]{4,3,2,1,0:T(8,128)}, f32[2,1,4,512,128]{4,3,2,1,0:T(8,128)}, bf16[2,1,4,...) while((s32[]{:T(128)}, ...), condition=%wide.region_13.14_spmd.clone.clone.clone, body=%wide.region_12.13_spmd.clone.clone.clone.sunk | while | flops 2964131840 | bytes 44889964 | solution.py:135
  417.2 2.8 fusion.264
  421.0 2.7 fusion.268
  424.8 3.3 fusion.266
  428.1 3.3 fusion.269
  435.4 2.8 fusion.264
  439.2 2.7 fusion.268
  443.0 3.3 fusion.266
  446.4 3.3 fusion.269
  453.8 2.9 copy.45
  456.8 3.0 copy.44
  482.0 2.7 add_convert_fusion
  484.8 7.5 %convolution_convert_fusion.1 = bf16[1024,1024]{1,0:T(8,128)(2,1)} fusion(bf16[1024,1408]{1,0:T(8,128)(2,1)} %get-tuple-element.714, bf16[1408,1024]{0,1:T(8,128)(2,1)} %all-gather.16.cloned.1.call-done), kind=kOutput, calls=%fused_computation.160 | convolution fusion | flops 2953838592 | bytes 7864320 | tf_op jit(solution)/shard_map/dot_general | solution.py:32
  494.2 5.7 convolution_convert_fusion
  499.9 6.8 fusion.121
  506.8 3.8 pad_maximum_fusion
  510.6 119.6 %all-reduce.3.cloned.1.call-done = (bf16[1024,512]{1,0:T(8,128)(2,1)}, bf16[1024,512]{1,0:T(8,128)(2,1)}, bf16[1024,512]{1,0:T(8,128)(2,1)}, bf16[1024,512]{1,0:T(8,128)(2,1)}, bf16[512,1024]{1,0:T(8,128)(2,1)}) async-done(((bf16[1024,512]{1,0:T(8,128)(2,1)}, bf16[1024,512]{1,0:T(8,128)(2,1)}, bf16[1024,512]{1,0:T(8,128)(2,1)}, bf16[1024,512]{1,0:T(8,128)(2,1)}, bf16[512,1024]{1,0:T(8,128)(2,1)}), ...) | async-done | bytes 5242896 | tf_op jit(solution)/shard_map/psum | solution.py:248
  630.2 3.0 convert_element_type.243
  641.4 4.4 fusion.131
  645.9 29.0 %reduce-scatter.14.cloned.1.call-done = bf16[64,4224]{1,0:T(8,128)(2,1)} async-done(((bf16[1024,4224]{1,0:T(8,128)(2,1)}), bf16[64,4224]{1,0:T(8,128)(2,1)}) %reduce-scatter.14.cloned.1.call-update) | async-done | bytes 540688 | tf_op jit(solution)/shard_map/reduce_scatter | solution.py:213
  (222 shorter events, 95.9 us)
Async XLA Ops:
  8.0 93.4 %copy-start = (bf16[512,1024]{1,0:T(8,128)(2,1)S(1)}, bf16[512,1024]{1,0:T(8,128)(2,1)}, u32[]{:S(2)}) copy-start(bf16[512,1024]{1,0:T(8,128)(2,1)} %param.23) | copy-start | bytes 3145732
  8.0 40.1 %all-gather.8.cloned.1.call-start = ((), (), s32[]{:S(2)}) async-start(), calls=%async_computation.5 | async-start | bytes 3145728 | tf_op jit(solution)/shard_map/all_gather | solution.py:165
  8.1 4.8 copy-start.51
  10.3 37.9 %copy-start.48 = (bf16[1024,512]{1,0:T(8,128)(2,1)S(1)}, bf16[1024,512]{1,0:T(8,128)(2,1)}, u32[]{:S(2)}) copy-start(bf16[1024,512]{1,0:T(8,128)(2,1)} %param.20) | copy-start | bytes 3145732
  12.8 124.4 %reduce-scatter.6.cloned.1.call-start = ((), (), s32[]{:S(2)}) async-start(), calls=%async_computation.6 | async-start | bytes 3145728 | tf_op jit(solution)/shard_map/reduce_scatter | solution.py:179
  58.5 2.8 copy-start.32
  58.5 2.8 copy-start.47
  65.7 2.7 copy-start.16
  71.5 2.9 copy-start.21
  71.5 3.7 copy-start.13
  79.0 2.8 copy-start.21
  79.0 3.7 copy-start.13
  83.5 6.3 copy-start.6
  91.9 8.5 %copy-start.4 = (f32[64,8,2,512]{3,1,2,0:T(8,128)}, f32[64,8,2,512]{3,1,2,0:T(8,128)S(1)}, u32[]{:S(2)}) copy-start(f32[64,8,2,512]{3,1,2,0:T(8,128)S(1)} %copy.52) | copy-start | bytes 6291460
  104.0 33.2 %copy-start.2 = (bf16[512,1024]{1,0:T(8,128)(2,1)S(1)}, bf16[512,1024]{1,0:T(8,128)(2,1)}, u32[]{:S(2)}) copy-start(bf16[512,1024]{1,0:T(8,128)(2,1)} %param.16) | copy-start | bytes 3145732
  104.0 48.6 %all-gather.12.cloned.1.call-start = ((), (), s32[]{:S(2)}) async-start(), calls=%async_computation.8 | async-start | bytes 3063808 | tf_op jit(solution)/shard_map/all_gather | solution.py:186
  104.6 81.2 %all-gather.10.cloned.1.call-start = ((), (), s32[]{:S(2)}) async-start(), calls=%async_computation.7 | async-start | bytes 3145728 | tf_op jit(solution)/shard_map/all_gather | solution.py:184
  140.2 92.5 %all-gather.14.cloned.1.call-start = ((), (), s32[]{:S(2)}) async-start(), calls=%async_computation.9 | async-start | bytes 3063808 | tf_op jit(solution)/shard_map/all_gather | solution.py:187
  140.8 125.3 %all-gather.18.cloned.1.call-start = ((), (), s32[]{:S(2)}) async-start(), calls=%async_computation.12 | async-start | bytes 3145728 | tf_op jit(solution)/shard_map/all_gather | solution.py:198
  144.0 169.2 %all-gather.16.cloned.1.call-start = ((), (), s32[]{:S(2)}) async-start(), calls=%async_computation.10 | async-start | bytes 3063808 | tf_op jit(solution)/shard_map/all_gather | solution.py:189
  144.8 218.3 %reduce-scatter.10.cloned.1.call-start = ((), (), s32[]{:S(2)}) async-start(), calls=%async_computation.13 | async-start | bytes 3145728 | tf_op jit(solution)/shard_map/reduce_scatter | solution.py:202
  313.2 11.0 %copy-start.44 = (bf16[1024,1408]{1,0:T(8,128)(2,1)S(1)}, bf16[1024,1408]{1,0:T(8,128)(2,1)}, u32[]{:S(2)}) copy-start(bf16[1024,1408]{1,0:T(8,128)(2,1)} %all-gather.12.cloned.1.call-done) | copy-start | bytes 8650756
  324.2 3.5 copy-start.27
  324.2 3.5 copy-start.25
  324.2 3.9 copy-start.45
  332.8 67.4 %all-gather.20.cloned.1.call-start = ((), (), s32[]{:S(2)}) async-start(), calls=%async_computation.14 | async-start | bytes 3145728 | tf_op jit(solution)/shard_map/all_gather | solution.py:224
  366.9 33.3 %copy-start.5 = (f32[64,8,2,512]{3,1,2,0:T(8,128)S(1)}, f32[64,8,2,512]{3,1,2,0:T(8,128)}, u32[]{:S(2)}) copy-start(f32[64,8,2,512]{3,1,2,0:T(8,128)} %copy-done.4) | copy-start | bytes 6291460
  366.9 263.3 %all-reduce.3.cloned.1.call-start = ((), (), s32[]{:S(2)}) async-start(), calls=%async_computation.17 | async-start | bytes 10485760 | tf_op jit(solution)/shard_map/psum | solution.py:248
  417.2 2.8 copy-start.7
  421.0 2.8 copy-start.9
  424.5 3.7 copy-start.8
  424.5 3.7 copy-start.10
  435.4 2.8 copy-start.7
  439.2 2.8 copy-start.9
  442.7 3.7 copy-start.8
  442.7 3.7 copy-start.10
  456.8 3.1 copy-start.19
  460.7 11.0 %copy-start.38 = (bf16[1,2,512,4,128]{4,3,2,1,0:T(4,128)(2,1)}, bf16[1,2,512,4,128]{4,3,2,1,0:T(4,128)(2,1)S(1)}, u32[]{:S(2)}) copy-start(bf16[1,2,512,4,128]{4,3,2,1,0:T(4,128)(2,1)S(1)} %copy.46) | copy-start | bytes 3145732
  476.2 163.3 %reduce-scatter.12.cloned.1.call-start = ((), (), s32[]{:S(2)}) async-start(), calls=%async_computation.15 | async-start | bytes 3145728 | tf_op jit(solution)/shard_map/reduce_scatter | solution.py:238
  476.5 2.6 copy-start.49
  484.7 156.7 %reduce-scatter.8.cloned.1.call-start = ((), (), s32[]{:S(2)}) async-start(), calls=%async_computation.11 | async-start | bytes 3145728 | tf_op jit(solution)/shard_map/reduce_scatter | solution.py:193
  492.3 182.6 %reduce-scatter.14.cloned.1.call-start = ((), (), s32[]{:S(2)}) async-start(), calls=%async_computation.16 | async-start | bytes 9191424 | tf_op jit(solution)/shard_map/reduce_scatter | solution.py:213
  494.2 5.7 copy-start.26
  494.2 5.8 copy-start.28
  494.2 5.8 copy-start.46
  630.2 3.0 copy-start.37
  638.0 3.4 copy-start.12
  641.4 36.3 %copy-start.1 = (bf16[512,1024]{1,0:T(8,128)(2,1)S(1)}, bf16[512,1024]{1,0:T(8,128)(2,1)}, u32[]{:S(2)}) copy-start(bf16[512,1024]{1,0:T(8,128)(2,1)} %param.23) | copy-start | bytes 3145732
  (25 other events, 38.2 us)
Sparse Core Ops, SparseCore 0:
  12.9 35.1 all-gather.7
  104.2 32.9 reduce-scatter.5
  332.9 30.0 reduce-scatter.9
  367.0 33.0 all-gather.19
  484.8 33.0 reduce-scatter.11
  520.1 31.8 reduce-scatter.7
  556.6 118.1 reduce-scatter.13
Sparse Core Ops, SparseCore 1:
  107.1 45.5 all-gather.11
  154.7 31.1 all-gather.9
  188.3 44.4 all-gather.13
  235.0 31.1 all-gather.17
  268.7 44.4 all-gather.15
  476.3 153.8 all-reduce.2
where the time goes:
time: 694 us; the launch traced here: 685 us
  waiting for transfers between devices  427 us (62%)
  matrix products  147 us (21%)
  other arithmetic  43.5 us (6%)
  local copies, waits for them, and re-layouts  41.4 us (6%)
  between operations  17.1 us (2%)
  blocking collectives  7.72 us (1%)
    psum x1, waiting for transfers between devices, body(): lax.psum(matmul_left_t(gathered, d_query_pre).astype(jnp.bfloat16), 'dp')  120 us
    all_gather x1, waiting for transfers between devices, body(): down_full = lax.all_gather(f_out, 'dp', axis=1, tiled=True)  47.1 us
    dot_general x8, matrix products, matmul(): return jnp.dot(left_side, right_side, preferred_element_type=jnp.float32)  41.9 us
    all_gather x1, waiting for transfers between devices, body(): lax.all_gather(f_gate, 'dp', axis=0, tiled=True)  38.6 us
    all_gather x1, waiting for transfers between devices, body(): lax.all_gather(mid_normed.astype(jnp.bfloat16), 'head', axis=0, tiled=True)  33.2 us
    all_gather x1, waiting for transfers between devices, body(): lax.all_gather(normed.astype(jnp.bfloat16), 'head', axis=0, tiled=True)  33.1 us
    reduce_scatter x1, waiting for transfers between devices, body(): lax.psum_scatter(matmul(gated, w_out).astype(jnp.bfloat16), 'head', scatt...  32.5 us
    dot_general x8, matrix products, matmul_right_t(): lax.dot_general(left_side, right_side, (((1,), (1,)), ((), ())), preferre...  32.3 us
  transfers between devices with their start and end apart: 13, of which 11 were waited for; matrix products, arithmetic and copies ran while one was open for 11% of the time, Pallas kernels for 0%

commit v1 on v0

--- a/solution.py
+++ b/solution.py
@@ -1,6 +1,8 @@
 import jax
 import jax.numpy as jnp
 from jax import lax
+from jax.experimental import pallas as pl
+from jax.experimental.pallas import tpu as pltpu
 from jax.sharding import PartitionSpec as P
 
 D = 1024
@@ -138,7 +140,7 @@
     return results
 
 
-def body(
+def general_body(
     tokens,
     lengths,
     decay,
@@ -273,6 +275,317 @@
     )
 
 
+MESH = pl.DeviceIdType.MESH
+NCH = 11
+RA = 16
+HR = 32
+SP = 2
+SPW = 2
+RS_AT = (1, 2, 4, 6, 8)
+NP = 4
+CW = 512 // NP
+NPIECE = 5 * NP
+WG_AT = tuple(1 + 2 * k for k in range(8))
+bf = jnp.bfloat16
+f32 = jnp.float32
+NT = (((1,), (1,)), ((), ()))
+
+
+def dot(a, b):
+    return jnp.dot(a, b, preferred_element_type=f32)
+
+
+def dotnt(a, b):
+    return lax.dot_general(a, b, NT, preferred_element_type=f32)
+
+
+def place():
+    d=lax.axis_index("dp")
+    return d//4, (d//2)%2, d%2, lax.axis_index("head")
+def dev(z,x,c,y): return ((z*2+x)*2+c, y)
+def gather_kernel(s_ref, wq, wk, wv, wg, wo, W3, pq, pk, pv, pg, po, zs, zr, xs, xr, ys, yr, ds, dr, wys, wyr, wzs, wzr, wxs, wxr, wds, wdr, ls):
+    z,x,c,y=place()
+    zp=[lax.rem(z+r,4) for r in (1,2,3)]
+    bar=pltpu.get_barrier_semaphore()
+    peers=[dev(q,x,c,y) for q in zp]+[dev(z,1-x,c,y),dev(z,x,1-c,y),dev(z,x,c,1-y)]
+    for p in peers: pl.semaphore_signal(bar,inc=1,device_id=p,device_id_type=MESH)
+    pl.semaphore_wait(bar,len(peers))
+    X=dev(z,1-x,c,y); Y=dev(z,x,c,1-y); C=dev(z,x,1-c,y)
+    col=pl.ds(pl.multiple_of(y*128,128),128)
+    own=[wq,wk,wv,wg,wo]; par=[pq,pk,pv,pg,po]
+    def rc(src,dst,ss,rs,d): return pltpu.make_async_remote_copy(src_ref=src,dst_ref=dst,send_sem=ss,recv_sem=rs,device_id=d,device_id_type=MESH)
+    loc=pltpu.make_async_copy(s_ref, W3.at[:,z,:,x,c,y], ls)
+    loc.start()
+    def st(k,i):
+        if k==0:
+            o=[]
+            for n,q in enumerate(zp):
+                t=W3.at[i,z,:,x,c,y]
+                o.append(rc(s_ref.at[i],t,zs.at[i,n],zr.at[i,n],dev(q,x,c,y)))
+            return o
+        if k==1:
+            a=W3.at[i,:,:,x,c,y,0:RA]; b=W3.at[i,:,:,x,c,y,RA:64]
+            return [rc(a,a,xs.at[i,0],xr.at[i,0],X), rc(b,b,ys.at[i,0],yr.at[i,0],Y)]
+        if k==2:
+            a=W3.at[i,:,:,:,c,y,0:RA]; b=W3.at[i,:,:,x,c,:,RA:64]
+            return [rc(b,b,xs.at[i,1],xr.at[i,1],X), rc(a,a,ys.at[i,1],yr.at[i,1],Y)]
+        if k==3:
+            a=W3.at[i,:,:,:,c]
+            return [rc(a,a,ds.at[i],dr.at[i],C)]
+    zb=lax.rem(z,2); ZP=dev(z+1-2*zb,x,c,y)
+    def wst(k,j):
+        if k==0: return [rc(own[j].at[zb,c],par[j].at[zb,c],wys.at[j],wyr.at[j],Y)]
+        if k==1:
+            a=par[j].at[zb,c]
+            return [rc(a,a,wxs.at[j],wxr.at[j],ZP)]
+        if k==2:
+            a=par[j].at[:,c]
+            return [rc(a,a,wds.at[j],wdr.at[j],C)]
+        return []
+    live={}
+    def go(f,tag,k,i,n):
+        if 0<=i<n:
+            if k>0:
+                for cp in live[(tag,k-1,i)]: cp.wait_recv()
+            if k<4:
+                live[(tag,k,i)]=f(k,i)
+                for cp in live[(tag,k,i)]: cp.start()
+    for t in range(NCH+4*SP):
+        for k in (4,3,2,1,0):
+            go(wst,"w",k,t-k*SPW,5)
+        if t==min(1,SP-1): loc.wait()
+        for k in (4,3,2,1,0):
+            go(st,"f",k,t-k*SP,NCH)
+    for cps in live.values():
+        for cp in cps: cp.wait_send()
+def gather_call(s, ws):
+    D=pltpu.SemaphoreType.DMA
+    bf=jnp.bfloat16
+    outs=[jax.ShapeDtypeStruct((NCH,4,3,2,2,2,64,128),bf)]+[jax.ShapeDtypeStruct((2,2,256,512),bf)]*4+[jax.ShapeDtypeStruct((2,2,128,1024),bf)]
+    A=pl.BlockSpec(memory_space=pl.ANY)
+    sem=[(NCH,3),(NCH,3),(NCH,2),(NCH,2),(NCH,2),(NCH,2),(NCH,),(NCH,),(5,),(5,),(5,3),(5,3),(5,),(5,),(5,),(5,)]
+    return pl.pallas_call(gather_kernel,out_shape=outs,in_specs=[pl.BlockSpec(memory_space=pltpu.VMEM)]+[A]*5,out_specs=[A]*6,
+        scratch_shapes=[D(v) for v in sem]+[D(())],
+        compiler_params=pltpu.CompilerParams(collective_id=1,has_side_effects=True,vmem_limit_bytes=60<<20))(s,*ws)
+def prep(fv,fg,fo):
+    s=jnp.stack([fv,fg,fo.T])
+    return s.reshape(3,64,NCH,128).transpose(2,0,1,3)
+def wviews(wq,wk,wv,wg,wo):
+    return [w.reshape(2,2,256,512) for w in (wq,wk,wv,wg)]+[wo.reshape(2,2,128,1024)]
+def ffn_kernel(mid, go, midT, goT, W3, out, dm, sh, G, RD, R1A, R1B, R2A, R2B, Q, RZ, WT, wsem, ds, dr, xs, xr, ys, yr, zs, zr):
+    z,x,c,y=place()
+    zp=[lax.rem(z+r,4) for r in (1,2,3)]
+    X=dev(z,1-x,c,y); Y=dev(z,x,c,1-y); C=dev(z,x,1-c,y)
+    bar=pltpu.get_barrier_semaphore()
+    peers=[dev(q,x,c,y) for q in zp]+[X,Y,C]
+    for p in peers: pl.semaphore_signal(bar,inc=1,device_id=p,device_id_type=MESH)
+    pl.semaphore_wait(bar,len(peers))
+    def rc(src,dst,ss,rs,d): return pltpu.make_async_remote_copy(src_ref=src,dst_ref=dst,send_sem=ss,recv_sem=rs,device_id=d,device_id_type=MESH)
+    def wload(i,s):
+        return [pltpu.make_async_copy(W3.at[i,:,:,:,:,h],WT.at[s,:,:,:,:,:,pl.ds(h*128,128)],wsem.at[s,h]) for h in (0,1)]
+    for cp in wload(0,0): cp.start()
+    out[...]=jnp.zeros_like(out); dm[...]=jnp.zeros_like(dm)
+    def cps(k,i):
+        if k==0: return [rc(G.at[i,1-c],RD.at[i],ds.at[i],dr.at[i],C)]
+        if k==1: return [rc(G.at[i,c,:,:,1-x,:,0:HR],R1A.at[i],xs.at[i,0],xr.at[i,0],X),
+                         rc(G.at[i,c,:,:,:,1-y,HR:64],R1B.at[i],ys.at[i,0],yr.at[i,0],Y)]
+        if k==2: return [rc(G.at[i,c,:,:,x,1-y,0:HR],R2A.at[i],ys.at[i,1],yr.at[i,1],Y),
+                         rc(G.at[i,c,:,:,1-x,y,HR:64],R2B.at[i],xs.at[i,1],xr.at[i,1],X)]
+        if k==3: return [rc(Q.at[i,:,q],RZ.at[i,n],zs.at[i,n],zr.at[i,n],dev(q,x,c,y)) for n,q in enumerate(zp)]
+    def reduce(k,i):
+        if k==1: G[i,c]=(G[i,c].astype(f32)+RD[i].astype(f32)).astype(bf)
+        if k==2:
+            G[i,c,:,:,x,:,0:HR]=(G[i,c,:,:,x,:,0:HR].astype(f32)+R1A[i].astype(f32)).astype(bf)
+            G[i,c,:,:,:,y,HR:64]=(G[i,c,:,:,:,y,HR:64].astype(f32)+R1B[i].astype(f32)).astype(bf)
+        if k==3:
+            Q[i,:,:,0:HR]=(G[i,c,:,:,x,y,0:HR].astype(f32)+R2A[i].astype(f32)).astype(bf)
+            Q[i,:,:,HR:64]=(G[i,c,:,:,x,y,HR:64].astype(f32)+R2B[i].astype(f32)).astype(bf)
+        if k==4:
+            v=Q[i,:,z].astype(f32)
+            for n in range(3): v=v+RZ[i,n].astype(f32)
+            sh[:,:,pl.ds(pl.multiple_of(i*128,128),128)]=v
+    def stages(t):
+        for k in (4,3,2,1,0):
+            i=t-RS_AT[k]
+            @pl.when((i>=0)&(i<NCH))
+            def _():
+                if k>0:
+                    for cp in cps(k-1,i): cp.wait_recv()
+                if k==1:
+                    for cp in cps(0,i): cp.wait_send()
+                reduce(k,i)
+        for k in (3,2,1,0):
+            i=t-RS_AT[k]
+            @pl.when((i>=0)&(i<NCH))
+            def _():
+                for cp in cps(k,i): cp.start()
+    def body(t,_):
+        stages(t)
+        @pl.when(t<NCH)
+        def _():
+            s=lax.rem(t,2)
+            for cp in wload(t,s): cp.wait()
+            @pl.when(t+1<NCH)
+            def _():
+                for cp in wload(t+1,1-s): cp.start()
+            fv=WT[s,:,0].reshape(1024,256); fg=WT[s,:,1].reshape(1024,256); fo=WT[s,:,2].reshape(1024,256)
+            m=mid[...]; g_=go[...]
+            v=dot(m,fv); g=dot(m,fg); gh=dot(g_,fo)
+            hid=(v*g).astype(bf); dv=(gh*g).astype(bf); dg=(gh*v).astype(bf)
+            out[...]+=dotnt(hid,fo)
+            dm[...]+=dotnt(dv,fv)+dotnt(dg,fg)
+            for tt,(L,R) in enumerate(((midT,dv),(midT,dg),(goT,hid))):
+                r=dot(L[...],R).astype(bf).reshape(4,2,2,64,256)
+                for cc in (0,1):
+                    for h in (0,1):
+                        G[t,cc,tt,:,:,h]=r[:,:,cc,:,h*128:h*128+128]
+        return 0
+    lax.fori_loop(0,NCH+RS_AT[4],body,0)
+    def drain(i,_):
+        for k in (1,2,3):
+            for cp in cps(k,i): cp.wait_send()
+        return 0
+    lax.fori_loop(0,NCH,drain,0)
+def ffn_call(mid,go,midT,goT,W3):
+    D=pltpu.SemaphoreType.DMA; V=pltpu.VMEM
+    A=pl.BlockSpec(memory_space=pl.ANY); VM=pl.BlockSpec(memory_space=pltpu.VMEM)
+    scr=[V((NCH,2,3,4,2,2,64,128),bf),V((NCH,3,4,2,2,64,128),bf),V((NCH,3,4,2,HR,128),bf),V((NCH,3,4,2,64-HR,128),bf),
+         V((NCH,3,4,HR,128),bf),V((NCH,3,4,64-HR,128),bf),V((NCH,3,4,64,128),bf),V((NCH,3,3,64,128),bf),V((2,4,3,2,2,64,256),bf),
+         D((2,2)),D((NCH,)),D((NCH,)),D((NCH,2)),D((NCH,2)),D((NCH,2)),D((NCH,2)),D((NCH,3)),D((NCH,3))]
+    return pl.pallas_call(ffn_kernel,out_shape=[jax.ShapeDtypeStruct((512,1024),f32)]*2+[jax.ShapeDtypeStruct((3,64,1408),f32)],
+        in_specs=[VM]*4+[A],out_specs=[VM]*3,scratch_shapes=scr,
+        compiler_params=pltpu.CompilerParams(collective_id=2,has_side_effects=True,vmem_limit_bytes=67043328))(mid,go,midT,goT,W3)
+def wg_kernel(LT, R, O, G, RD, RY, RX, Q, RZ, ds, dr, ys, yr, xs, xr, zs, zr, z2s, z2r, x2s, x2r, d2s, d2r):
+    z,x,c,y=place()
+    zp=[lax.rem(z+r,4) for r in (1,2,3)]
+    X=dev(z,1-x,c,y); Y=dev(z,x,c,1-y); C=dev(z,x,1-c,y)
+    bar=pltpu.get_barrier_semaphore()
+    peers=[dev(q,x,c,y) for q in zp]+[X,Y,C]
+    for p in peers: pl.semaphore_signal(bar,inc=1,device_id=p,device_id_type=MESH)
+    pl.semaphore_wait(bar,len(peers))
+    def rc(src,dst,ss,rs,d): return pltpu.make_async_remote_copy(src_ref=src,dst_ref=dst,send_sem=ss,recv_sem=rs,device_id=d,device_id_type=MESH)
+    def cps(k,i):
+        if k==0: return [rc(G.at[i,1-c],RD.at[i],ds.at[i],dr.at[i],C)]
+        if k==1: return [rc(G.at[i,c,1],RY.at[i],ys.at[i],yr.at[i],Y)]
+        if k==2: return [rc(G.at[i,c,0,:,1-x],RX.at[i],xs.at[i],xr.at[i],X)]
+        if k==3: return [rc(Q.at[i,q],RZ.at[i,n],zs.at[i,n],zr.at[i,n],dev(q,x,c,y)) for n,q in enumerate(zp)]
+        if k==4: return [rc(O.at[i,z,x,c],O.at[i,z,x,c],z2s.at[i,n],z2r.at[i,n],dev(q,x,c,y)) for n,q in enumerate(zp)]
+        if k==5: return [rc(O.at[i,:,x,c],O.at[i,:,x,c],x2s.at[i],x2r.at[i],X)]
+        if k==6: return [rc(O.at[i,:,:,c],O.at[i,:,:,c],d2s.at[i],d2r.at[i],C)]
+    def reduce(k,i):
+        if k==1: G[i,c]=(G[i,c].astype(f32)+RD[i].astype(f32)).astype(bf)
+        if k==2: G[i,c,0]=(G[i,c,0].astype(f32)+RY[i].astype(f32)).astype(bf)
+        if k==3: Q[i]=(G[i,c,0,:,x].astype(f32)+RX[i].astype(f32)).astype(bf)
+        if k==4:
+            v=Q[i,z].astype(f32)
+            for n in range(3): v=v+RZ[i,n].astype(f32)
+            O[i,z,x,c]=v.astype(bf)
+    def stages(t):
+        for k in range(7,-1,-1):
+            i=t-WG_AT[k]
+            @pl.when((i>=0)&(i<NPIECE))
+            def _():
+                if k>0:
+                    for cp in cps(k-1,i): cp.wait_recv()
+                if k==1:
+                    for cp in cps(0,i): cp.wait_send()
+                reduce(k,i)
+        for k in range(6,-1,-1):
+            i=t-WG_AT[k]
+            @pl.when((i>=0)&(i<NPIECE))
+            def _():
+                for cp in cps(k,i): cp.start()
+    def body(t,_):
+        stages(t)
+        @pl.when(t<NPIECE)
+        def _():
+            j=t//NP; pp=lax.rem(t,NP)
+            L=LT[jnp.minimum(j,1)]
+            for b in (0,1):
+                r=dot(L,R[j,b,:,pl.ds(pl.multiple_of(pp*CW,128),CW)]).astype(bf).reshape(4,2,2,64,CW)
+                for cc in (0,1): G[t,cc,b]=r[:,:,cc]
+        return 0
+    lax.fori_loop(0,NPIECE+WG_AT[7],body,0)
+    def drain(i,_):
+        for k in (1,2,3,4,5,6):
+            for cp in cps(k,i): cp.wait_send()
+        return 0
+    lax.fori_loop(0,NPIECE,drain,0)
+def wg_call(LT,R):
+    D=pltpu.SemaphoreType.DMA; V=pltpu.VMEM
+    VM=pl.BlockSpec(memory_space=pltpu.VMEM)
+    scr=[V((NPIECE,2,2,4,2,64,CW),bf),V((NPIECE,2,4,2,64,CW),bf),V((NPIECE,4,2,64,CW),bf),V((NPIECE,4,64,CW),bf),V((NPIECE,4,64,CW),bf),V((NPIECE,3,64,CW),bf)]
+    n=(NPIECE,); m=(NPIECE,3)
+    scr+=[D(v) for v in (n,n,n,n,n,n,m,m,m,m,n,n,n,n)]
+    return pl.pallas_call(wg_kernel,out_shape=jax.ShapeDtypeStruct((NPIECE,4,2,2,64,CW),bf),
+        in_specs=[VM]*2,out_specs=VM,scratch_shapes=scr,
+        compiler_params=pltpu.CompilerParams(collective_id=3,has_side_effects=True,vmem_limit_bytes=67043328))(LT,R)
+
+def fast_body(tokens, lengths, decay, w_query, w_key, w_value, w_gate, w_out, f_value, f_gate, f_out, cotangent):
+    own_rows = tokens.shape[0]
+    y = lax.axis_index("head")
+    swap = [(0, 1), (1, 0)]
+    rates = jnp.concatenate([decay, lax.ppermute(decay, "head", swap)])
+    within, first_decay, last_decay, _ = decay_tables(rates)
+    positions = y * own_rows + jnp.arange(own_rows, dtype=jnp.int32)
+    keep_rows = (positions < lengths[0]).astype(f32)[:, None]
+    inputs_f = tokens.astype(f32)
+    normed, scale_in = normalize(inputs_f)
+    normed_low = normed.astype(bf)
+    W3, *parts = gather_call(prep(f_value, f_gate, f_out), wviews(w_query, w_key, w_value, w_gate, w_out))
+    pq, pk, pv, pg = [p.reshape(1024, 512) for p in parts[:4]]
+    po = parts[4].reshape(512, 1024)
+    two = lambda a, b: jnp.concatenate([matmul(normed_low, a), matmul(normed_low, b)], axis=1)
+    query_pre, keys_pre, values_pre, gate_pre = two(w_query, pq), two(w_key, pk), two(w_value, pv), two(w_gate, pg)
+    heads = lambda t: t.reshape(own_rows, 8, HD).transpose(1, 0, 2)
+    flat = lambda t: t.transpose(1, 0, 2).reshape(own_rows, 8 * HD)
+    query = heads(jax.nn.silu(query_pre).astype(bf))
+    keys = heads(jax.nn.silu(keys_pre).astype(bf))
+    values = heads(values_pre.astype(bf))
+    ein = lambda form, a, b: jnp.einsum(form, a, b, preferred_element_type=f32)
+    swapped = lambda t: lax.ppermute(jnp.concatenate([t[4:], t[:4]]).astype(bf), "head", swap)
+    keys_last = (keys.astype(f32) * last_decay[:, :, None]).astype(bf)
+    update = ein("htd,hte->hde", keys_last, values)
+    state = swapped(update)
+    state = jnp.where(y == 1, state, jnp.zeros_like(state))
+    weights = (ein("htd,hrd->htr", query, keys) * within).astype(bf)
+    mixed = flat(ein("htr,hrd->htd", weights, values) + first_decay[:, :, None] * ein("htd,hde->hte", query, state))
+    scale_out = lax.rsqrt(jnp.mean(mixed * mixed, axis=1, keepdims=True) + epsilon)
+    mixed_unit = mixed * scale_out
+    gated = (mixed_unit * gate_pre).astype(bf)
+    middle = inputs_f + matmul(gated[:, :512], w_out) + matmul(gated[:, 512:], po)
+    mid_normed, scale_mid = normalize(middle)
+    mid_low = mid_normed.astype(bf)
+    grad_out = cotangent.astype(f32) * keep_rows
+    grad_low = grad_out.astype(bf)
+    ffn, d_mid_normed, shares = ffn_call(mid_low, grad_low, mid_low.T, grad_low.T, W3)
+    output = ((middle + ffn) * keep_rows).astype(bf)
+    grad_middle = grad_out + norm_back(d_mid_normed, mid_normed, scale_mid)
+    gm = grad_middle.astype(bf)
+    d_gated = jnp.concatenate([matmul_right_t(gm, w_out), matmul_right_t(gm, po)], axis=1)
+    d_gate_pre = (d_gated * mixed_unit).astype(bf)
+    d_unit = d_gated * gate_pre
+    d_mixed = heads(norm_back(d_unit, mixed_unit, scale_out).astype(bf))
+    grad_first = (d_mixed.astype(f32) * first_decay[:, :, None]).astype(bf)
+    later = swapped(ein("htd,hte->hde", query, grad_first))
+    later = jnp.where(y == 0, later, jnp.zeros_like(later))
+    d_scores = (ein("htd,hrd->htr", d_mixed, values) * within).astype(bf)
+    d_query = ein("htr,hrd->htd", d_scores, keys) + ein("hte,hde->htd", grad_first, state)
+    d_keys = ein("htr,htd->hrd", d_scores, query) + last_decay[:, :, None] * ein("hte,hde->htd", values, later)
+    d_values = ein("htr,htd->hrd", weights, d_mixed) + ein("htd,hde->hte", keys_last, later)
+    d_query_pre = (flat(d_query) * silu_slope(query_pre)).astype(bf)
+    d_keys_pre = (flat(d_keys) * silu_slope(keys_pre)).astype(bf)
+    d_values_pre = flat(d_values).astype(bf)
+    total = 0.0
+    for d, own, part in ((d_query_pre, w_query, pq), (d_keys_pre, w_key, pk), (d_values_pre, w_value, pv), (d_gate_pre, w_gate, pg)):
+        total = total + matmul_right_t(d[:, :512], own) + matmul_right_t(d[:, 512:], part)
+    d_tokens = grad_middle + norm_back(total, normed, scale_in)
+    right = jnp.stack([t[:, h * 512 : h * 512 + 512] for t in (gated, d_gate_pre, d_values_pre, d_keys_pre, d_query_pre) for h in (0, 1)]).reshape(5, 2, 512, 512)
+    grads = wg_call(jnp.stack([gm.T, normed_low.T]), right)
+    grads = grads.reshape(5, NP, 1024, CW).transpose(0, 2, 1, 3).reshape(5, 1024, 512).astype(f32)
+    return (output, d_tokens, grads[4], grads[3], grads[2], grads[1], grads[0].T, shares[0], shares[1], shares[2].T)
+
+
 def solution(mesh):
     placed = (
         P(("dp", "head"), None),
@@ -288,8 +601,9 @@
         P("head", "dp"),
         P(("dp", "head"), None),
     )
+    fast = mesh.shape["dp"] == 16 and mesh.shape["head"] == 2
     return jax.shard_map(
-        body,
+        fast_body if fast else general_body,
         mesh=mesh,
         in_specs=placed,
         out_specs=(

time: 694 us -> 486 us (0.70)
  waiting for transfers between devices: 427 us -> 1.79 us
  Pallas kernels: 0 us -> 306 us
  matrix products: 147 us -> 45.2 us
  local copies, waits for them, and re-layouts: 41.4 us -> 88.7 us
  other arithmetic: 43.5 us -> 28.8 us
  between operations: 17.1 us -> 2.61 us
  blocking collectives: 7.72 us -> 0 us
    pallas_call x0 -> x3, Pallas kernels: none -> 306 us  [the longest x1 116 us: gather_call(): pl.pallas_call(gather_kernel, out_shape=outs, in_specs=[pl.BlockSpec(memo...]
    all_gather x7 -> x0, waiting for transfers between devices: 214 us -> none  [the longest x1 47.1 us: body(): down_full = lax.all_gather(f_out, 'dp', axis=1, tiled=True)]
    psum x1 -> x0, waiting for transfers between devices: 120 us -> none  [body(): lax.psum(matmul_left_t(gathered, d_query_pre).astype(jnp.bfloat16), 'dp')]
    reduce_scatter x5 -> x0, waiting for transfers between devices: 91.7 us -> none  [the longest x1 32.5 us: body(): lax.psum_scatter(matmul(gated, w_out).astype(jnp.bfloat16), 'head', scatt...]
    dot_general x29 -> x12, matrix products: 72.5 us -> 19.5 us  [fast_body(): ein = lambda form, a, b: jnp.einsum(form, a, b, preferred_element_type=f32)]
    unnamed x90 -> x201, local copies, waits for them, and re-layouts: 8.68 us -> 39.8 us
    dot_general x8 -> x10, matrix products: 41.9 us -> 14.2 us  [matmul(): return jnp.dot(left_side, right_side, preferred_element_type=jnp.float32)]
    dot_general x8 -> x10, matrix products: 32.3 us -> 11.6 us  [matmul_right_t(): lax.dot_general(left_side, right_side, (((1,), (1,)), ((), ())), preferre...]
  transfers between devices with their start and end apart: 13 -> 3, of which waited for: 11 -> 1; matrix products, arithmetic and copies ran while one was open for 11% -> 11% of each run, Pallas kernels for 0% -> 24%
where the time goes in v1:
time: 486 us; the launch traced here: 477 us
  Pallas kernels  306 us (63%)
  local copies, waits for them, and re-layouts  88.7 us (18%)
  matrix products  45.2 us (9%)
  other arithmetic  28.8 us (6%)
    pallas_call x1, Pallas kernels, gather_call(): pl.pallas_call(gather_kernel, out_shape=outs, in_specs=[pl.BlockSpec(memo...  116 us
    pallas_call x1, Pallas kernels, wg_call(): pl.pallas_call(wg_kernel, out_shape=jax.ShapeDtypeStruct((NPIECE, 4, 2, 2...  97.3 us
    pallas_call x1, Pallas kernels, ffn_call(): pl.pallas_call(ffn_kernel, out_shape=[jax.ShapeDtypeStruct((512, 1024), f...  92.5 us
    unnamed x201, local copies, waits for them, and re-layouts  39.8 us
    dot_general x12, matrix products, fast_body(): ein = lambda form, a, b: jnp.einsum(form, a, b, preferred_element_type=f32)  19.5 us
    dot_general x10, matrix products, matmul(): return jnp.dot(left_side, right_side, preferred_element_type=jnp.float32)  14.2 us
    dot_general x10, matrix products, matmul_right_t(): lax.dot_general(left_side, right_side, (((1,), (1,)), ((), ())), preferre...  11.6 us
    concatenate x5, local copies, waits for them, and re-layouts, fast_body(): jnp.concatenate([matmul(normed_low, a), matmul(normed_low, b)], axis=1)  11.3 us
  transfers between devices with their start and end apart: 3, of which 1 were waited for; matrix products, arithmetic and copies ran while one was open for 11% of the time, Pallas kernels for 24%

profile of v1, /device:TPU:1, one launch (start us, length us, event | category | flops | bytes accessed | tf_op | source)
XLA Modules:
  0.0 476.8 jit_solution(2376486568640264881)
XLA Ops:
  0.6 2.1 collective-permute-start
  5.6 1.5 copy.80
  12.6 1.6 convolution_convert_fusion.1
  14.2 2.1 copy.74
  19.1 1.7 fusion.61
  20.8 2.5 copy.68
  24.7 2.3 copy.82.go
  27.8 116.2 %shard_map.195 = (bf16[11,4,3,2,2,2,64,128]{7,6,5,4,3,2,1,0:T(8,128)(2,1)}, bf16[2,2,256,512]{3,2,1,0:T(8,128)(2,1)}, bf16[2,2,256,512]{3,2,1,0:T(8,128)(2,1)}, ...) custom-call(bf16[11,3,64,128]{3,2,1,0:T(8,128)(2,1)} %maximum_bitcast_fusion.1., ...), custom_call_target="tpu_custom_call" | custom-call | tf_op jit(solution)/shard_map/pallas_call | solution.py:367
  144.0 3.1 fusion.55
  147.1 1.7 fusion.59
  149.6 2.9 copy.69
  152.5 2.5 copy.71
  155.0 2.7 copy.72
  157.8 2.1 convolution_convert_fusion
  163.8 1.7 convolution_convert_fusion.3
  166.8 2.2 multiply_convert_fusion.1
  169.1 1.5 fusion.74
  171.8 1.8 collective-permute-done.1
  178.8 1.5 fusion.106.midT
  182.0 92.5 %shard_map.196 = (f32[512,1024]{1,0:T(8,128)}, f32[512,1024]{1,0:T(8,128)}, f32[3,64,1408]{2,1,0:T(8,128)}) custom-call(bf16[512,1024]{1,0:T(8,128)(2,1)} %copy.81.mid, bf16[512,1024]{1,0:T(8,128)(2,1)} %copy.82.go, bf16[1024,512]{1,0:T(8,128)(2,1)} %fusion.106.midT, bf16[1024,512]{1,0:T(8,128)(2,1)} %fusion.105.goT, ...), custom_call_target="tpu_custom_call" | custom-call | tf_op jit(solution)/shard_map/pallas_call | solution.py:455
  274.6 2.9 copy.83
  277.5 3.0 copy.85
  280.5 2.0 multiply_reduce_fusion.1
  283.0 4.0 convert_bitcast_fusion.1
  295.4 2.0 fusion.78
  297.5 3.1 multiply_convert_fusion
  300.6 2.1 fusion.22
  302.7 1.5 fusion.18
  308.0 2.0 fusion.37
  310.0 2.0 fusion.39
  314.9 2.0 fusion.27
  318.6 2.3 copy.107
  321.7 2.5 fusion.13
  334.6 2.3 fusion.48
  337.0 3.0 copy.108
  344.9 8.0 %copy.101 = bf16[10,512,512]{2,1,0:T(8,128)(2,1)} copy(bf16[10,512,512]{1,2,0:T(8,128)(2,1)} %bitcast_dynamic-update-slice_fusion) | data formatting | bytes 10485760 | tf_op jit(solution)/shard_map/stack | solution.py:583
  352.9 1.5 pad_maximum_fusion.4.LT
  354.4 97.3 %shard_map.197 = bf16[20,4,2,2,64,128]{5,4,3,2,1,0:T(8,128)(2,1)} custom-call(bf16[2,1024,512]{2,1,0:T(8,128)(2,1)} %pad_maximum_fusion.4.LT, bf16[5,2,512,512]{3,2,1,0:T(8,128)(2,1)} %bitcast.182), custom_call_target="tpu_custom_call" | custom-call | tf_op jit(solution)/shard_map/pallas_call | solution.py:520
  451.7 3.6 convert_bitcast_fusion
  455.3 3.5 fusion.75
  458.8 2.9 copy.106
  461.7 2.9 copy.105
  464.6 1.5 copy.139
  467.0 1.4 copy.104
  468.3 1.5 copy.140
  470.7 1.4 copy.103
  472.0 1.5 copy.141
  474.9 1.5 copy.142
  (256 shorter events, 62.7 us)
Async XLA Ops:
  0.6 161.6 %collective-permute-start = (f32[4]{0:T(128)}, f32[4]{0:T(128)S(1)}, u32[]{:S(2)}, u32[]{:S(2)}) collective-permute-start(f32[4]{0:T(128)} %param.14), channel_id=1, source_target_pairs={{0,1},{1,0},{2,3},{3,2},{4,5},{5,4},{6,7},{7,6},{8,9},{9,8},{10,11... | collective-permute-start | bytes 56 | tf_op jit(solution)/shard_map/ppermute | solution.py:528
  7.1 2.4 copy-start.11
  7.1 2.4 copy-start.75
  7.1 2.6 copy-start.76
  8.3 3.5 copy-start.65
  9.9 2.7 copy-start.53
  12.3 164.7 %copy-start.6 = (bf16[512,1024]{0,1:T(8,128)(2,1)}, bf16[512,1024]{0,1:T(8,128)(2,1)S(1)}, u32[]{:S(2)}) copy-start(bf16[512,1024]{0,1:T(8,128)(2,1)S(1)} %copy.64) | copy-start | bytes 3145732
  12.6 145.1 %copy-start.87 = (f32[512]{0:T(512)}, f32[512]{0:T(512)S(1)}, u32[]{:S(2)}) copy-start(f32[512]{0:T(512)S(1)} %add_rsqrt_fusion.2) | copy-start | bytes 6148
  12.6 3.6 copy-start.51
  17.5 5.9 %copy-start.37 = (f32[512,512]{0,1:T(8,128)}, f32[512,512]{0,1:T(8,128)S(1)}, u32[]{:S(2)}) copy-start(f32[512,512]{0,1:T(8,128)S(1)} %fusion.57) | copy-start | bytes 3145732
  19.1 155.2 %copy-start.21 = (f32[512,512]{0,1:T(8,128)}, f32[512,512]{0,1:T(8,128)S(1)}, u32[]{:S(2)}) copy-start(f32[512,512]{0,1:T(8,128)S(1)} %fusion.51) | copy-start | bytes 3145732
  24.7 2.3 copy-start.72
  144.0 3.1 copy-start.63
  149.6 24.7 %copy-start.23 = (f32[512,512]{0,1:T(8,128)}, f32[512,512]{0,1:T(8,128)S(1)}, u32[]{:S(2)}) copy-start(f32[512,512]{0,1:T(8,128)S(1)} %fusion.49) | copy-start | bytes 3145732
  159.9 9.1 %copy-start.59 = (bf16[512,4,128]{2,0,1:T(8,128)(2,1)}, bf16[512,4,128]{2,0,1:T(8,128)(2,1)S(1)}, u32[]{:S(2)}) copy-start(bf16[512,4,128]{2,0,1:T(8,128)(2,1)S(1)} %convolution_convert_fusion) | copy-start | bytes 1572868
  161.7 11.9 %copy-start.13 = (bf16[512,8,128]{2,0,1:T(8,128)(2,1)}, bf16[512,8,128]{2,0,1:T(8,128)(2,1)S(1)}, u32[]{:S(2)}) copy-start(bf16[512,8,128]{2,0,1:T(8,128)(2,1)S(1)} %multiply_convert_fusion.7) | copy-start | bytes 3145732
  162.2 4.6 copy-start.17
  162.4 8.2 %copy-start.89 = (f32[8]{0:T(128)}, f32[8]{0:T(128)S(1)}, u32[]{:S(2)}) copy-start(f32[8]{0:T(128)S(1)} %maximum_negate_fusion) | copy-start | bytes 100
  163.8 3.1 copy-start.66
  163.8 3.1 copy-start.73
  165.5 8.0 %collective-permute-start.1 = (bf16[8,128,128]{2,1,0:T(8,128)(2,1)S(1)}, bf16[8,128,128]{2,1,0:T(8,128)(2,1)S(1)}, u32[]{:S(2)}, u32[]{:S(2)}) collective-permute-start(bf16[8,128,128]{2,1,0:T(8,128)(2,1)S(1)} %pad_maximum_fusion.5), channel_id=1, source_target_pairs={{0,1},{1,0},{2,3},{3,2},{4,5},{5,4},{6,7},{7,6},{8,9},{9,8},{10,11... | collective-permute-start | bytes 786440 | tf_op jit(solution)/shard_map/ppermute | solution.py:546
  277.5 3.0 copy-start.3
  277.5 3.0 copy-start.84
  280.5 2.2 copy-start.8
  280.5 2.5 copy-start.12
  280.5 2.5 copy-start.86
  283.0 4.1 copy-start.57
  291.2 29.7 %copy-start.27 = (bf16[512,1024]{0,1:T(8,128)(2,1)}, bf16[512,1024]{0,1:T(8,128)(2,1)S(1)}, u32[]{:S(2)}) copy-start(bf16[512,1024]{0,1:T(8,128)(2,1)S(1)} %fusion.10) | copy-start | bytes 3145732
  293.2 2.2 copy-start.10
  297.5 3.1 copy-start.14
  310.0 2.9 copy-start.61
  312.1 2.9 copy-start.50
  314.7 7.1 %collective-permute-start.2 = (bf16[8,128,128]{2,1,0:T(8,128)(2,1)}, bf16[8,128,128]{2,1,0:T(8,128)(2,1)S(1)}, u32[]{:S(2)}, u32[]{:S(2)}) collective-permute-start(bf16[8,128,128]{2,1,0:T(8,128)(2,1)} %pad_maximum_fusion.6), channel_id=1, source_target_pairs={{0,1},{1,0},{2,3},{3,2},{4,5},{5,4},{6,7},{7,6},{8,9},{9,8},{10,11... | collective-permute-start | bytes 786440 | tf_op jit(solution)/shard_map/ppermute | solution.py:546
  317.8 3.9 copy-start.80
  321.7 2.5 copy-start.38
  321.7 2.5 copy-start.40
  328.3 3.6 copy-start.34
  328.3 3.6 copy-start.71
  329.6 2.5 copy-start.32
  329.6 3.1 copy-start.33
  330.3 2.4 copy-start.7
  330.3 2.7 copy-start.28
  330.3 2.7 copy-start.88
  337.0 3.0 copy-start.20
  344.9 8.0 %copy-start.55 = (bf16[1,1024,512]{2,1,0:T(8,128)(2,1)S(1)}, bf16[1,1024,512]{2,1,0:T(8,128)(2,1)}, u32[]{:S(2)}) copy-start(bf16[1,1024,512]{2,1,0:T(8,128)(2,1)} %get-tuple-element.48) | copy-start | bytes 3145732
  344.9 8.0 %copy-start.58 = (bf16[1,1024,512]{2,1,0:T(8,128)(2,1)S(1)}, bf16[1,1024,512]{2,1,0:T(8,128)(2,1)}, u32[]{:S(2)}) copy-start(bf16[1,1024,512]{2,1,0:T(8,128)(2,1)} %get-tuple-element.59) | copy-start | bytes 3145732
  464.6 2.4 copy-start.31
  468.3 2.4 copy-start.30
  (47 other events, 73.3 us)

commit v2 on v0

--- a/solution.py
+++ b/solution.py
@@ -1,6 +1,8 @@
 import jax
 import jax.numpy as jnp
 from jax import lax
+from jax.experimental import pallas as pl
+from jax.experimental.pallas import tpu as pltpu
 from jax.sharding import PartitionSpec as P
 
 D = 1024
@@ -138,7 +140,7 @@
     return results
 
 
-def body(
+def general_body(
     tokens,
     lengths,
     decay,
@@ -273,6 +275,523 @@
     )
 
 
+MESH = pl.DeviceIdType.MESH
+NCH = 11
+RA = 16
+HR = 32
+SP = 2
+SPW = 2
+NWG = 20
+NALL = NCH + NWG
+RS_AT = (1, 2, 4, 6, 8)
+AG_AT = (10, 12, 14)
+TN = (((0,), (0,)), ((), ()))
+bf = jnp.bfloat16
+f32 = jnp.float32
+NT = (((1,), (1,)), ((), ()))
+
+
+def dot(a, b):
+    return jnp.dot(a, b, preferred_element_type=f32)
+
+
+def dotnt(a, b):
+    return lax.dot_general(a, b, NT, preferred_element_type=f32)
+
+
+def dottn(a, b):
+    return lax.dot_general(a, b, TN, preferred_element_type=f32)
+
+
+def place():
+    d=lax.axis_index("dp")
+    return d//4, (d//2)%2, d%2, lax.axis_index("head")
+def dev(z,x,c,y): return ((z*2+x)*2+c, y)
+def gather_kernel(s_ref, wq, wk, wv, wg, wo, W3, pq, pk, pv, pg, po, zs, zr, xs, xr, ys, yr, ds, dr, wys, wyr, wzs, wzr, wxs, wxr, wds, wdr, ls):
+    z,x,c,y=place()
+    zp=[lax.rem(z+r,4) for r in (1,2,3)]
+    bar=pltpu.get_barrier_semaphore()
+    peers=[dev(q,x,c,y) for q in zp]+[dev(z,1-x,c,y),dev(z,x,1-c,y),dev(z,x,c,1-y)]
+    for p in peers: pl.semaphore_signal(bar,inc=1,device_id=p,device_id_type=MESH)
+    pl.semaphore_wait(bar,len(peers))
+    X=dev(z,1-x,c,y); Y=dev(z,x,c,1-y); C=dev(z,x,1-c,y)
+    col=pl.ds(pl.multiple_of(y*128,128),128)
+    own=[wq,wk,wv,wg,wo]; par=[pq,pk,pv,pg,po]
+    def rc(src,dst,ss,rs,d): return pltpu.make_async_remote_copy(src_ref=src,dst_ref=dst,send_sem=ss,recv_sem=rs,device_id=d,device_id_type=MESH)
+    loc=pltpu.make_async_copy(s_ref, W3.at[:,z,:,x,c,y], ls)
+    loc.start()
+    def st(k,i):
+        if k==0:
+            o=[]
+            for n,q in enumerate(zp):
+                t=W3.at[i,z,:,x,c,y]
+                o.append(rc(s_ref.at[i],t,zs.at[i,n],zr.at[i,n],dev(q,x,c,y)))
+            return o
+        if k==1:
+            a=W3.at[i,:,:,x,c,y,0:RA]; b=W3.at[i,:,:,x,c,y,RA:64]
+            return [rc(a,a,xs.at[i,0],xr.at[i,0],X), rc(b,b,ys.at[i,0],yr.at[i,0],Y)]
+        if k==2:
+            a=W3.at[i,:,:,:,c,y,0:RA]; b=W3.at[i,:,:,x,c,:,RA:64]
+            return [rc(b,b,xs.at[i,1],xr.at[i,1],X), rc(a,a,ys.at[i,1],yr.at[i,1],Y)]
+        if k==3:
+            a=W3.at[i,:,:,:,c]
+            return [rc(a,a,ds.at[i],dr.at[i],C)]
+    zb=lax.rem(z,2); ZP=dev(z+1-2*zb,x,c,y)
+    def wst(k,j):
+        if k==0: return [rc(own[j].at[zb,c],par[j].at[zb,c],wys.at[j],wyr.at[j],Y)]
+        if k==1:
+            a=par[j].at[zb,c]
+            return [rc(a,a,wxs.at[j],wxr.at[j],ZP)]
+        if k==2:
+            a=par[j].at[:,c]
+            return [rc(a,a,wds.at[j],wdr.at[j],C)]
+        return []
+    live={}
+    def go(f,tag,k,i,n):
+        if 0<=i<n:
+            if k>0:
+                for cp in live[(tag,k-1,i)]: cp.wait_recv()
+            if k<4:
+                live[(tag,k,i)]=f(k,i)
+                for cp in live[(tag,k,i)]: cp.start()
+    for t in range(NCH+4*SP):
+        for k in (4,3,2,1,0):
+            go(wst,"w",k,t-k*SPW,5)
+        if t==min(1,SP-1): loc.wait()
+        for k in (4,3,2,1,0):
+            go(st,"f",k,t-k*SP,NCH)
+    for cps in live.values():
+        for cp in cps: cp.wait_send()
+def gather_call(s, ws):
+    D=pltpu.SemaphoreType.DMA
+    bf=jnp.bfloat16
+    outs=[jax.ShapeDtypeStruct((NCH,4,3,2,2,2,64,128),bf)]+[jax.ShapeDtypeStruct((2,2,256,512),bf)]*4+[jax.ShapeDtypeStruct((2,2,128,1024),bf)]
+    A=pl.BlockSpec(memory_space=pl.ANY)
+    sem=[(NCH,3),(NCH,3),(NCH,2),(NCH,2),(NCH,2),(NCH,2),(NCH,),(NCH,),(5,),(5,),(5,3),(5,3),(5,),(5,),(5,),(5,)]
+    return pl.pallas_call(gather_kernel,out_shape=outs,in_specs=[pl.BlockSpec(memory_space=pltpu.VMEM)]+[A]*5,out_specs=[A]*6,
+        scratch_shapes=[D(v) for v in sem]+[D(())],
+        compiler_params=pltpu.CompilerParams(collective_id=1,has_side_effects=True,vmem_limit_bytes=60<<20))(s,*ws)
+def prep(fv,fg,fo):
+    s=jnp.stack([fv,fg,fo.T])
+    return s.reshape(3,64,NCH,128).transpose(2,0,1,3)
+def wviews(wq,wk,wv,wg,wo):
+    return [w.reshape(2,2,256,512) for w in (wq,wk,wv,wg)]+[wo.reshape(2,2,128,1024)]
+def backward_kernel(mid, go, rates, scal, state, W3, middle, gate, unit, gated, qpre, kpre, vals, normed, wq, wk, wv, wg, wo, pq, pk, pv, pg, po,
+                    output, dtok, sh, O,
+                    G, RD, R1, R2, Q, RZ, FN, WT, LT, ACC, DV, R, UN, NM, DMX, WB, WO, GS, GR,
+                    wsem, lsem, bsem, gss, gsr, ds, dr, xs, xr, ys, yr, zs, zr, az_s, az_r, ax_s, ax_r, ad_s, ad_r, fl):
+    z, x, c, y = place()
+    zp = [lax.rem(z + r, 4) for r in (1, 2, 3)]
+    X, Y, C = dev(z, 1 - x, c, y), dev(z, x, c, 1 - y), dev(z, x, 1 - c, y)
+    bar = pltpu.get_barrier_semaphore()
+    peers = [dev(q, x, c, y) for q in zp] + [X, Y, C]
+    for p in peers:
+        pl.semaphore_signal(bar, inc=1, device_id=p, device_id_type=MESH)
+
+    def rc(src, dst, ss, rs, d):
+        return pltpu.make_async_remote_copy(src_ref=src, dst_ref=dst, send_sem=ss, recv_sem=rs, device_id=d, device_id_type=MESH)
+
+    def wload(i, s):
+        return [pltpu.make_async_copy(W3.at[i, :, :, :, :, h], WT.at[s, :, :, :, :, :, pl.ds(h * 128, 128)], wsem.at[s, h]) for h in (0, 1)]
+
+    loads = [pltpu.make_async_copy(a, b, lsem.at[n]) for n, (a, b) in enumerate(
+        [(middle, ACC), (gated, R.at[0]), (gate, R.at[1]), (vals, R.at[2]), (kpre, R.at[3]), (qpre, R.at[4]), (unit, UN), (normed, NM), (wo, WO.at[0]), (po, WO.at[1])])]
+    for cp in wload(0, 0):
+        cp.start()
+    for cp in loads:
+        cp.start()
+    mats = (wg, pg, wv, pv, wk, pk, wq, pq)
+
+    def wbload(n):
+        return pltpu.make_async_copy(mats[n], WB.at[n % 2], bsem.at[n % 2])
+
+    wbload(0).start()
+    wbload(1).start()
+    LT[0] = mid[...].T
+    LT[1] = go[...].T
+    dtok[...] = jnp.zeros_like(dtok)
+    loads[0].wait()
+    pl.semaphore_wait(bar, len(peers))
+
+    def cps(k, i, hr):
+        g, s, n = lax.rem(i, NCH), lax.rem(i, 4), 3 if hr else 1
+        if k == 0:
+            return [rc(G.at[g, 1 - c, 0:n], RD.at[lax.rem(i, 2), 0:n], ds.at[i], dr.at[i], C)]
+        if k == 1:
+            o = [rc(G.at[g, c, 0:n, :, :, 1 - y, hr:64], R1.at[s, 0:n, :, :, hr:64], ys.at[i, 0], yr.at[i, 0], Y)]
+            if hr:
+                o.append(rc(G.at[g, c, 0:n, :, 1 - x, :, 0:hr], R1.at[s, 0:n, :, :, 0:hr], xs.at[i, 0], xr.at[i, 0], X))
+            return o
+        if k == 2:
+            o = [rc(G.at[g, c, 0:n, :, 1 - x, y, hr:64], R2.at[s, 0:n, :, hr:64], xs.at[i, 1], xr.at[i, 1], X)]
+            if hr:
+                o.append(rc(G.at[g, c, 0:n, :, x, 1 - y, 0:hr], R2.at[s, 0:n, :, 0:hr], ys.at[i, 1], yr.at[i, 1], Y))
+            return o
+        if k == 3:
+            return [rc(Q.at[s, 0:n, q], RZ.at[s, m, 0:n], zs.at[i, m], zr.at[i, m], dev(q, x, c, y)) for m, q in enumerate(zp)]
+
+    def ags(k, w):
+        if k == 0:
+            f = FN.at[lax.rem(w, 4)]
+            return [rc(f, O.at[w, z, x, c], az_s.at[w, n], az_r.at[w, n], dev(q, x, c, y)) for n, q in enumerate(zp)]
+        if k == 1:
+            return [rc(O.at[w, :, x, c], O.at[w, :, x, c], ax_s.at[w], ax_r.at[w], X)]
+        if k == 2:
+            return [rc(O.at[w, :, :, c], O.at[w, :, :, c], ad_s.at[w], ad_r.at[w], C)]
+
+    def flush(w):
+        return pltpu.make_async_copy(FN.at[lax.rem(w, 4)], O.at[w, z, x, c], fl.at[w])
+
+    def reduce(k, i, hr):
+        g, s, n = lax.rem(i, NCH), lax.rem(i, 4), 3 if hr else 1
+        up = lambda v: v.astype(f32)
+        if k == 1:
+            G[g, c, 0:n] = (up(G[g, c, 0:n]) + up(RD[lax.rem(i, 2), 0:n])).astype(bf)
+        if k == 2:
+            if hr:
+                G[g, c, 0:n, :, x, :, 0:hr] = (up(G[g, c, 0:n, :, x, :, 0:hr]) + up(R1[s, 0:n, :, :, 0:hr])).astype(bf)
+            G[g, c, 0:n, :, :, y, hr:64] = (up(G[g, c, 0:n, :, :, y, hr:64]) + up(R1[s, 0:n, :, :, hr:64])).astype(bf)
+        if k == 3:
+            Q[s, 0:n] = (up(G[g, c, 0:n, :, x, y]) + up(R2[s, 0:n])).astype(bf)
+        if k == 4:
+            v = up(Q[s, 0:n, z])
+            for m in range(3):
+                v = v + up(RZ[s, m, 0:n])
+            if hr:
+                sh[:, :, pl.ds(pl.multiple_of(i * 128, 128), 128)] = v
+            else:
+                FN[lax.rem(i - NCH, 4)] = v[0].astype(bf)
+
+    def arrive(k, i, hr):
+        if k > 0:
+            for cp in cps(k - 1, i, hr):
+                cp.wait_recv()
+        if k == 1:
+            for cp in cps(0, i, hr):
+                cp.wait_send()
+        if k == 4:
+            for kk in (1, 2, 3):
+                for cp in cps(kk, i, hr):
+                    cp.wait_send()
+        reduce(k, i, hr)
+
+    def leave(k, i, hr):
+        for cp in cps(k, i, hr):
+            cp.start()
+
+    def both(f, k, t):
+        i = t - RS_AT[k]
+
+        @pl.when((i >= 0) & (i < NCH))
+        def _():
+            f(k, i, HR)
+
+        @pl.when((i >= NCH) & (i < NALL))
+        def _():
+            f(k, i, 0)
+
+    def ag_arrive(k, t):
+        w = t - AG_AT[k] - NCH
+
+        @pl.when((w >= 0) & (w < NWG))
+        def _():
+            for cp in ags(k, w):
+                cp.wait_recv()
+            if k == 0:
+                for cp in ags(0, w):
+                    cp.wait_send()
+                flush(w).wait()
+
+    def ag_leave(k, t):
+        w = t - (AG_AT[k - 1] if k else RS_AT[4]) - NCH
+
+        @pl.when((w >= 0) & (w < NWG))
+        def _():
+            for cp in ags(k, w):
+                cp.start()
+            if k == 0:
+                flush(w).start()
+
+    def stages(t):
+        ag_arrive(2, t)
+        ag_arrive(1, t)
+        ag_arrive(0, t)
+        ag_leave(2, t)
+        both(arrive, 4, t)
+        ag_leave(1, t)
+        both(arrive, 3, t)
+        ag_leave(0, t)
+        both(arrive, 2, t)
+        both(leave, 3, t)
+        both(arrive, 1, t)
+        for k in (2, 1, 0):
+            both(leave, k, t)
+
+    def store(g, t, r, own):
+        r = r.astype(bf).reshape(4, 2, 2, 64, 256)
+        for cc in (0, 1):
+            G[g, cc, t, :, :, own] = r[:, :, cc, :, 0:128]
+            G[g, cc, t, :, :, 1 - own] = r[:, :, cc, :, 128:256]
+
+    def ffn(t):
+        s = lax.rem(t, 2)
+        for cp in wload(t, s):
+            cp.wait()
+
+        @pl.when(t + 1 < NCH)
+        def _():
+            for cp in wload(t + 1, 1 - s):
+                cp.start()
+
+        fv, fg, fo = [WT[s, :, n].reshape(1024, 256) for n in range(3)]
+        m, g_ = mid[...], go[...]
+        v, g, gh = dot(m, fv), dot(m, fg), dot(g_, fo)
+        hid, dv, dg = (v * g).astype(bf), (gh * g).astype(bf), (gh * v).astype(bf)
+        ACC[...] += dotnt(hid, fo)
+        dtok[...] += dotnt(dv, fv) + dotnt(dg, fg)
+        store(t, 0, dot(LT[0], dv), 0)
+        store(t, 1, dot(LT[0], dg), 0)
+        store(t, 2, dot(LT[1], hid), 0)
+
+    def ffn_tick(t, _):
+        stages(t)
+
+        def one(n, _):
+            ffn(n)
+            return 0
+
+        lax.fori_loop(jnp.maximum(2 * t - 1, 0), jnp.minimum(2 * t + 1, NCH), one, 0)
+        return 0
+
+    T = 6
+    lax.fori_loop(0, T, ffn_tick, 0)
+    stages(T)
+    for cp in loads[1:]:
+        cp.wait()
+    keep, scale_mid, scale_out, scale_in = [scal[:, n : n + 1] for n in range(4)]
+    output[...] = (ACC[...] * keep).astype(bf)
+    n2 = mid[...].astype(f32)
+    dm = dtok[...]
+    gm = go[...].astype(f32) + scale_mid * (dm - n2 * jnp.mean(dm * n2, axis=1, keepdims=True))
+    dtok[...] = gm
+    gml = gm.astype(bf)
+    LT[0] = gml.T
+    LT[1] = NM[...].T
+    for h in (0, 1):
+        cols = slice(h * 512, h * 512 + 512)
+        ACC[:, cols] = dotnt(gml, WO[h])
+    dgt, un = ACC[...], UN[...].astype(f32)
+    du = dgt * R[1].astype(f32)
+    R[1] = (dgt * un).astype(bf)
+    DMX[...] = (scale_out * (du - un * jnp.mean(du * un, axis=1, keepdims=True))).astype(bf)
+
+    def head(h):
+        return pl.ds(pl.multiple_of(h * 128, 128), 128)
+
+    def silu(v):
+        return v * jax.nn.sigmoid(v)
+
+    tau = lax.broadcasted_iota(jnp.int32, (512, 1), 0).astype(f32)
+    rho = lax.broadcasted_iota(jnp.int32, (1, 512), 1).astype(f32)
+
+    def first(h, _):
+        hs = head(h)
+        q = silu(R[4, :, hs].astype(f32)).astype(bf)
+        gf = (DMX[:, hs].astype(f32) * jnp.exp(-rates[h] * (tau + 1.0))).astype(bf)
+        GS[lax.rem(h + 4, 8)] = dottn(q, gf).astype(bf)
+        return 0
+
+    lax.fori_loop(0, 8, first, 0)
+    stages(T + 1)
+    later = rc(GS, GR, gss, gsr, Y)
+    later.start()
+    ti = lax.broadcasted_iota(jnp.int32, (512, 512), 0)
+    ri = lax.broadcasted_iota(jnp.int32, (512, 512), 1)
+
+    def pair(h, _):
+        hs = head(h)
+        qp, kp = R[4, :, hs].astype(f32), R[3, :, hs].astype(f32)
+        q, k, v, dmx = silu(qp).astype(bf), silu(kp).astype(bf), R[2, :, hs], DMX[:, hs]
+        cf, rf = jnp.exp(-rates[h] * (tau + 1.0)), jnp.exp(rates[h] * (rho + 1.0))
+        within = jnp.where(ti >= ri, cf * rf, 0.0)
+        wt = (dotnt(q, k) * within).astype(bf)
+        dsc = (dotnt(dmx, v) * within).astype(bf)
+        gf = (dmx.astype(f32) * cf).astype(bf)
+        dq = dot(dsc, k) + dotnt(gf, state[h])
+        ACC[:, hs] = dottn(dsc, q)
+        DV[:, hs] = dottn(wt, dmx)
+        sq = jax.nn.sigmoid(qp)
+        R[4, :, hs] = (dq * (sq * (1.0 + qp * (1.0 - sq)))).astype(bf)
+        return 0
+
+    stages(T + 2)
+    lax.fori_loop(0, 4, pair, 0)
+    stages(T + 3)
+    lax.fori_loop(4, 8, pair, 0)
+    stages(T + 4)
+    later.wait()
+    live = (y == 0).astype(f32)
+
+    def finish(h, _):
+        hs = head(h)
+        gin = (GR[h].astype(f32) * live).astype(bf)
+        kp = R[3, :, hs].astype(f32)
+        sk = jax.nn.sigmoid(kp)
+        k = (kp * sk).astype(bf)
+        lf = jnp.exp(-rates[h] * (511.0 - tau))
+        kl = (k.astype(f32) * lf).astype(bf)
+        dk = ACC[:, hs] + lf * dotnt(R[2, :, hs], gin)
+        R[2, :, hs] = (DV[:, hs] + dot(kl, gin)).astype(bf)
+        R[3, :, hs] = (dk * (sk * (1.0 + kp * (1.0 - sk)))).astype(bf)
+        return 0
+
+    lax.fori_loop(0, 8, finish, 0)
+    def wgrad(p):
+        j, cp = p // 4, lax.rem(p, 4)
+        lo = pl.multiple_of(cp * 128, 128)
+        rr = jnp.concatenate([R[j, :, pl.ds(lo, 128)], R[j, :, pl.ds(lo + 512, 128)]], axis=1)
+        store(lax.rem(p, NCH), 0, dot(LT[jnp.minimum(j, 1)], rr), y)
+
+    def wg_tick(t, _):
+        stages(t)
+        p = t - NCH
+        wgrad(p)
+        for n in range(8):
+            @pl.when(p == n)
+            def _():
+                wbload(n).wait()
+
+        @pl.when(p < 8)
+        def _():
+            j, h = 1 + p // 2, lax.rem(p, 2)
+            part = dotnt(R[j, :, pl.ds(pl.multiple_of(h * 512, 128), 512)], WB[h])
+            ACC[...] = jnp.where(p == 0, 0.0, ACC[...]) + part
+
+        for n in range(6):
+            @pl.when(p == n)
+            def _():
+                wbload(n + 2).start()
+
+        @pl.when(p == 8)
+        def _():
+            n1 = NM[...].astype(f32)
+            dn = ACC[...]
+            dtok[...] = dtok[...] + scale_in * (dn - n1 * jnp.mean(dn * n1, axis=1, keepdims=True))
+
+        return 0
+
+    lax.fori_loop(NCH, NCH + NWG, wg_tick, 0)
+    def tail(t, _):
+        stages(t)
+        return 0
+
+    lax.fori_loop(NALL, NALL + AG_AT[2], tail, 0)
+
+    def drain(w, _):
+        for k in (1, 2):
+            for cp in ags(k, w):
+                cp.wait_send()
+        return 0
+
+    lax.fori_loop(0, NWG, drain, 0)
+
+
+def backward_call(mid, go, rates, scal, state, *rest):
+    D, V = pltpu.SemaphoreType.DMA, pltpu.VMEM
+    A, VM = pl.BlockSpec(memory_space=pl.ANY), pl.BlockSpec(memory_space=pltpu.VMEM)
+    act = (512, 1024)
+    scratch = [V((NCH, 2, 3, 4, 2, 2, 64, 128), bf), V((2, 3, 4, 2, 2, 64, 128), bf),
+               V((4, 3, 4, 2, 64, 128), bf), V((4, 3, 4, 64, 128), bf),
+               V((4, 3, 4, 64, 128), bf), V((4, 3, 3, 64, 128), bf), V((4, 64, 128), bf), V((2, 4, 3, 2, 2, 64, 256), bf),
+               V((2, 1024, 512), bf), V(act, f32), V(act, f32), V((5,) + act, bf), V(act, bf), V(act, bf), V(act, bf),
+               V((2, 1024, 512), bf), V((2, 512, 1024), bf), V((8, 128, 128), bf), V((8, 128, 128), bf)]
+    n = NALL
+    scratch += [D(s) for s in ((2, 2), (10,), (2,), (), (), (n,), (n,), (n, 2), (n, 2), (n, 2), (n, 2), (n, 3), (n, 3),
+                               (NWG, 3), (NWG, 3), (NWG,), (NWG,), (NWG,), (NWG,), (NWG,))]
+    S = jax.ShapeDtypeStruct
+    return pl.pallas_call(
+        backward_kernel,
+        out_shape=[S(act, bf), S(act, f32), S((3, 64, 1408), f32), S((NWG, 4, 2, 2, 64, 128), bf)],
+        in_specs=[VM] * 2 + [pl.BlockSpec(memory_space=pltpu.SMEM)] + [VM] * 2 + [A] * 19,
+        out_specs=[VM] * 3 + [A],
+        scratch_shapes=scratch,
+        compiler_params=pltpu.CompilerParams(collective_id=2, has_side_effects=True, vmem_limit_bytes=67043328),
+    )(mid, go, rates, scal, state, *rest)
+def finish_kernel(o, sh, d_query, d_key, d_value, d_gate, d_out, d_f_value, d_f_gate, d_f_out):
+    for n in range(4):
+        cols = slice(n * 128, n * 128 + 128)
+        d_out[cols, :] = o[n].astype(f32).T
+        d_gate[:, cols] = o[4 + n].astype(f32)
+        d_value[:, cols] = o[8 + n].astype(f32)
+        d_key[:, cols] = o[12 + n].astype(f32)
+        d_query[:, cols] = o[16 + n].astype(f32)
+
+    @pl.when(pl.program_id(0) == 0)
+    def _():
+        d_f_value[...] = sh[0]
+        d_f_gate[...] = sh[1]
+        d_f_out[...] = sh[2].T
+
+
+def finish_call(o, sh):
+    S = jax.ShapeDtypeStruct
+    whole = lambda *s: pl.BlockSpec(s, lambda i: (0,) * len(s))
+    return pl.pallas_call(
+        finish_kernel,
+        grid=(4,),
+        out_shape=[S((1024, 512), f32)] * 4 + [S((512, 1024), f32)] + [S((64, 1408), f32)] * 2 + [S((1408, 64), f32)],
+        in_specs=[pl.BlockSpec((20, 256, 128), lambda i: (0, i, 0)), whole(3, 64, 1408)],
+        out_specs=[pl.BlockSpec((256, 512), lambda i: (i, 0))] * 4 + [pl.BlockSpec((512, 256), lambda i: (0, i))] + [whole(64, 1408)] * 2 + [whole(1408, 64)],
+        compiler_params=pltpu.CompilerParams(vmem_limit_bytes=48 << 20),
+    )(o, sh)
+
+def fast_body(tokens, lengths, decay, w_query, w_key, w_value, w_gate, w_out, f_value, f_gate, f_out, cotangent):
+    own_rows = tokens.shape[0]
+    y = lax.axis_index("head")
+    swap = [(0, 1), (1, 0)]
+    rates = jnp.concatenate([decay, lax.ppermute(decay, "head", swap)])
+    within, first_decay, last_decay, _ = decay_tables(rates)
+    positions = y * own_rows + jnp.arange(own_rows, dtype=jnp.int32)
+    keep_rows = (positions < lengths[0]).astype(f32)[:, None]
+    inputs_f = tokens.astype(f32)
+    normed, scale_in = normalize(inputs_f)
+    normed_low = normed.astype(bf)
+    W3, *parts = gather_call(prep(f_value, f_gate, f_out), wviews(w_query, w_key, w_value, w_gate, w_out))
+    pq, pk, pv, pg = [p.reshape(1024, 512) for p in parts[:4]]
+    po = parts[4].reshape(512, 1024)
+    two = lambda a, b: jnp.concatenate([matmul(normed_low, a), matmul(normed_low, b)], axis=1)
+    query_pre, keys_pre, values_pre, gate_pre = two(w_query, pq), two(w_key, pk), two(w_value, pv), two(w_gate, pg)
+    heads = lambda t: t.reshape(own_rows, 8, HD).transpose(1, 0, 2)
+    flat = lambda t: t.transpose(1, 0, 2).reshape(own_rows, 8 * HD)
+    query = heads(jax.nn.silu(query_pre).astype(bf))
+    keys = heads(jax.nn.silu(keys_pre).astype(bf))
+    values = heads(values_pre.astype(bf))
+    ein = lambda form, a, b: jnp.einsum(form, a, b, preferred_element_type=f32)
+    swapped = lambda t: lax.ppermute(jnp.concatenate([t[4:], t[:4]]).astype(bf), "head", swap)
+    keys_last = (keys.astype(f32) * last_decay[:, :, None]).astype(bf)
+    update = ein("htd,hte->hde", keys_last, values)
+    state = swapped(update)
+    state = jnp.where(y == 1, state, jnp.zeros_like(state))
+    weights = (ein("htd,hrd->htr", query, keys) * within).astype(bf)
+    mixed = flat(ein("htr,hrd->htd", weights, values) + first_decay[:, :, None] * ein("htd,hde->hte", query, state))
+    scale_out = lax.rsqrt(jnp.mean(mixed * mixed, axis=1, keepdims=True) + epsilon)
+    mixed_unit = mixed * scale_out
+    gated = (mixed_unit * gate_pre).astype(bf)
+    middle = inputs_f + matmul(gated[:, :512], w_out) + matmul(gated[:, 512:], po)
+    mid_normed, scale_mid = normalize(middle)
+    mid_low = mid_normed.astype(bf)
+    grad_out = cotangent.astype(f32) * keep_rows
+    grad_low = grad_out.astype(bf)
+    scal = jnp.concatenate([keep_rows, scale_mid, scale_out, scale_in], axis=1)
+    view = lambda p: p.reshape(1024, 512)
+    output, d_tokens, shares, grads = backward_call(
+        mid_low, grad_low, rates, scal, state, W3, middle, gate_pre.astype(bf), mixed_unit.astype(bf), gated,
+        query_pre.astype(bf), keys_pre.astype(bf), values_pre.astype(bf), normed_low,
+        w_query, w_key, w_value, w_gate, w_out, pq, pk, pv, pg, po)
+    d_query, d_key, d_value, d_gate, d_out, d_f_value, d_f_gate, d_f_out = finish_call(grads.reshape(NWG, 1024, 128), shares)
+    return (output, d_tokens, d_query, d_key, d_value, d_gate, d_out, d_f_value, d_f_gate, d_f_out)
+
+
 def solution(mesh):
     placed = (
         P(("dp", "head"), None),
@@ -288,8 +807,9 @@
         P("head", "dp"),
         P(("dp", "head"), None),
     )
+    fast = mesh.shape["dp"] == 16 and mesh.shape["head"] == 2
     return jax.shard_map(
-        body,
+        fast_body if fast else general_body,
         mesh=mesh,
         in_specs=placed,
         out_specs=(

time: 694 us -> 381 us (0.55); the launches traced: 685 us -> 381 us
  waiting for transfers between devices: 427 us -> 0.01 us
  Pallas kernels: 0 us -> 301 us
  matrix products: 147 us -> 33.3 us
  other arithmetic: 43.5 us -> 15.8 us
  local copies, waits for them, and re-layouts: 41.4 us -> 24.9 us
  between operations: 17.1 us -> 1.84 us
  blocking collectives: 7.72 us -> 0 us
    pallas_call x0 -> x3, Pallas kernels: none -> 301 us  [the longest x1 177 us: backward_call(): pl.pallas_call(backward_kernel, out_shape=[S(act, bf), S(act, f32), S((3,...]
    all_gather x7 -> x0, waiting for transfers between devices: 214 us -> none  [the longest x1 47.1 us: body(): down_full = lax.all_gather(f_out, 'dp', axis=1, tiled=True)]
    psum x1 -> x0, waiting for transfers between devices: 120 us -> none  [body(): lax.psum(matmul_left_t(gathered, d_query_pre).astype(jnp.bfloat16), 'dp')]
    reduce_scatter x5 -> x0, waiting for transfers between devices: 91.7 us -> none  [the longest x1 32.5 us: body(): lax.psum_scatter(matmul(gated, w_out).astype(jnp.bfloat16), 'head', scatt...]
    dot_general x37 -> x3, matrix products: 105 us -> 13.8 us  [fast_body(): ein = lambda form, a, b: jnp.einsum(form, a, b, preferred_element_type=f32)]
    dot_general x8 -> x10, matrix products: 41.9 us -> 19.6 us  [matmul(): return jnp.dot(left_side, right_side, preferred_element_type=jnp.float32)]
    transpose x7 -> x0, local copies, waits for them, and re-layouts: 16.3 us -> none  [the longest x3 10.1 us: from_blocks(): blocks.transpose(1, 0, 3, 2, 4)]
    convert_element_type x14 -> x7, other arithmetic: 22.3 us -> 7.26 us  [the longest x1 2.89 us: fast_body(): mixed_unit.astype(bf)]
  transfers between devices with their start and end apart: 13 -> 2, of which waited for: 11 -> 0; matrix products, arithmetic and copies ran while one was open for 11% -> 13% of each run, Pallas kernels for 0% -> 31%
where the time goes in v2:
time: 381 us
  Pallas kernels  301 us (79%)
  matrix products  33.3 us (9%)
  local copies, waits for them, and re-layouts  24.9 us (7%)
  other arithmetic  15.8 us (4%)
    pallas_call x1, Pallas kernels, backward_call(): pl.pallas_call(backward_kernel, out_shape=[S(act, bf), S(act, f32), S((3,...  177 us
    pallas_call x1, Pallas kernels, gather_call(): pl.pallas_call(gather_kernel, out_shape=outs, in_specs=[pl.BlockSpec(memo...  116 us
    dot_general x10, matrix products, matmul(): return jnp.dot(left_side, right_side, preferred_element_type=jnp.float32)  19.6 us
    dot_general x3, matrix products, fast_body(): ein = lambda form, a, b: jnp.einsum(form, a, b, preferred_element_type=f32)  13.8 us
    concatenate x6, local copies, waits for them, and re-layouts, fast_body(): jnp.concatenate([matmul(normed_low, a), matmul(normed_low, b)], axis=1)  9.31 us
    pallas_call x1, Pallas kernels, finish_call(): pl.pallas_call(finish_kernel, grid=(4,), out_shape=[S((1024, 512), f32)]...  7.64 us
  transfers between devices with their start and end apart: 2, of which 0 were waited for; matrix products, arithmetic and copies ran while one was open for 13% of the time, Pallas kernels for 31%

profile of v2, /device:TPU:1, one launch (start us, length us, event | category | flops | bytes accessed | tf_op | source)
XLA Modules:
  0.0 380.6 jit_solution(2769713773690084961)
XLA Ops:
  0.7 2.1 collective-permute-start
  2.8 0.9 subtract_compare_fusion
  3.8 1.1 subtract_select_fusion
  5.6 1.5 fusion.7
  7.8 0.7 copy.68
  8.7 1.5 convolution_convert_fusion.1
  10.3 2.0 copy.96
  12.3 2.0 fusion.34
  14.3 2.4 fusion.32
  16.7 1.0 copy.85
  17.7 1.3 copy.71
  19.0 2.3 fusion.30
  21.3 1.0 copy.83
  22.3 1.3 copy.69
  23.6 1.8 maximum_bitcast_fusion.3.s_ref
  25.4 116.3 %shard_map.195 = (bf16[11,4,3,2,2,2,64,128]{7,6,5,4,3,2,1,0:T(8,128)(2,1)}, bf16[2,2,256,512]{3,2,1,0:T(8,128)(2,1)}, bf16[2,2,256,512]{3,2,1,0:T(8,128)(2,1)}, ...) custom-call(bf16[11,3,64,128]{3,2,1,0:T(8,128)(2,1)} %maximum_bitcast_fusion.3., ...), custom_call_target="tpu_custom_call" | custom-call | tf_op jit(solution)/shard_map/pallas_call | solution.py:371
  141.7 2.8 convolution_convert_fusion
  144.4 2.0 copy.97
  146.5 2.3 fusion.33
  148.8 1.0 copy.86
  149.8 1.3 copy.72
  151.1 2.3 fusion.31
  153.4 1.0 copy.84
  154.4 1.3 copy.70
  155.8 2.4 fusion.35
  158.2 1.3 multiply_convert_fusion.2.go
  159.5 1.6 pad_maximum_fusion.4
  161.2 1.6 fusion.11
  162.9 0.6 fusion.28
  163.8 1.6 convolution_convert_fusion.2
  165.5 0.7 pad_maximum_fusion.6
  166.2 1.3 collective-permute-start.1
  167.5 7.9 %fusion = f32[8,512,128]{1,2,0:T(8,128)} fusion(f32[512,512]{1,0:T(8,128)S(1)} %copy-done.21, f32[8]{0:T(128)S(1)} %get-tuple-element.76, pred[512,512]{1,0:T(8,128)(4,1)} %subtract_compare_fusion, bf16[512,4,128]{0,2,1:T(8,128)(2,1)} %bitcast.95, bf16[512,4,128]{0,2,1:T(8,128)(2,1)} %bitcast.93, f32[512,4,128]{2,0,1:T(8,128)} %copy.70, ...), kind=kOutput, calls=%fused_computation.1 | convolution fusion | flops 1088946176 | bytes 8650784 | tf_op jit(solution)/shard_map/htr,hrd->htd/dot_general | solution.py:769
  175.5 4.2 %multiply_reduce_fusion.1 = (f32[512]{0:T(512)S(1)}, f32[512,8,128]{0,2,1:T(8,128)}) fusion(bf16[8,128,128]{2,1,0:T(8,128)(2,1)S(1)} %broadcast_select_fusion.state, f32[512,4,128]{2,0,1:T(8,128)} %copy.70, f32[512,4,128]{2,0,1:T(8,128)S(1)} %copy-done.22, f32[512,8]{0,1:T(8,128)S(1)} %multiply_exponential_fusion.1, f32[8,512,128]{1,2,0:T(8,128)} %fusion), kind=kOutput, calls=%fused_computation.22 | convolution fusion | flops 139460096 | bytes 6572032 | tf_op jit(solution)/shard_map/htd,hde->hte/dot_general | solution.py:769
  179.8 1.9 copy.98
  181.7 2.9 multiply_convert_fusion.8
  184.6 0.7 fusion.20
  185.3 0.9 copy-done.7
  186.2 0.9 multiply_reduce_fusion
  187.2 1.1 copy.87.scal
  188.2 0.3 copy-done.1
  188.5 1.1 multiply_convert_fusion.3.mid
  189.7 177.4 %shard_map.196 = (bf16[512,1024]{1,0:T(8,128)(2,1)}, f32[512,1024]{1,0:T(8,128)}, f32[3,64,1408]{2,1,0:T(8,128)}, bf16[20,4,2,2,64,128]{5,4,3,2,1,0:T(8,128)(2,1)}) custom-call(bf16[512,1024]{1,0:T(8,128)(2,1)} %multiply_convert_fusion.3.mid, bf16[512,1024]{1,0:T(8,128)(2,1)} %multiply_convert_fusion.2.go, f32[8]{0:T(128)} %get-tuple-element.77.rates, ...), custom_call_target="tpu_custom_call" | custom-call | tf_op jit(solution)/shard_map/pallas_call | solution.py:712
  367.1 1.2 copy-done
  368.3 7.6 %shard_map.197 = (f32[1024,512]{1,0:T(8,128)}, f32[1024,512]{1,0:T(8,128)}, f32[1024,512]{1,0:T(8,128)}, f32[1024,512]{1,0:T(8,128)}, f32[512,1024]{1,0:T(8,128)...) custom-call(bf16[20,1024,128]{2,1,0:T(8,128)(2,1)} %bitcast.73, f32[3,64,1408]{2,1,0:T(8,128)S(1)} %copy-done), custom_call_target="tpu_custom_call" | custom-call | tf_op jit(solution)/shard_map/pallas_call | solution.py:739
  376.0 1.0 copy.88
  377.0 2.3 copy.102
  379.3 1.3 copy.103
  (80 shorter events, 1.3 us)
Async XLA Ops:
  0.6 6.5 %copy-start.27 = (bf16[64,1408]{1,0:T(8,128)(2,1)S(1)}, bf16[64,1408]{1,0:T(8,128)(2,1)}, u32[]{:S(2)}) copy-start(bf16[64,1408]{1,0:T(8,128)(2,1)} %param.20) | copy-start | bytes 540676
  0.7 6.8 %copy-start.28 = (bf16[64,1408]{1,0:T(8,128)(2,1)S(1)}, bf16[64,1408]{1,0:T(8,128)(2,1)}, u32[]{:S(2)}) copy-start(bf16[64,1408]{1,0:T(8,128)(2,1)} %param.21) | copy-start | bytes 540676
  0.7 6.9 %copy-start.29 = (bf16[1408,64]{0,1:T(8,128)(2,1)S(1)}, bf16[1408,64]{0,1:T(8,128)(2,1)}, u32[]{:S(2)}) copy-start(bf16[1408,64]{0,1:T(8,128)(2,1)} %param.22) | copy-start | bytes 540676
  0.7 162.2 %collective-permute-start = (f32[4]{0:T(128)}, f32[4]{0:T(128)S(1)}, u32[]{:S(2)}, u32[]{:S(2)}) collective-permute-start(f32[4]{0:T(128)} %param.14), channel_id=1, source_target_pairs={{0,1},{1,0},{2,3},{3,2},{4,5},{5,4},{6,7},{7,6},{8,9},{9,8},{10,11... | collective-permute-start | bytes 56 | tf_op jit(solution)/shard_map/ppermute | solution.py:752
  4.9 3.6 copy-start.2
  7.3 1.4 copy-start.11
  8.7 3.6 copy-start.8
  12.3 2.0 copy-start.10
  14.3 146.8 %copy-start.5 = (f32[512,512]{1,0:T(8,128)}, f32[512,512]{1,0:T(8,128)S(1)}, u32[]{:S(2)}) copy-start(f32[512,512]{1,0:T(8,128)S(1)} %fusion.34) | copy-start | bytes 3145732
  25.4 116.3 %copy-start.9 = (bf16[512,1024]{1,0:T(8,128)(2,1)S(1)}, bf16[512,1024]{1,0:T(8,128)(2,1)}, u32[]{:S(2)}) copy-start(bf16[512,1024]{1,0:T(8,128)(2,1)} %copy-done.8) | copy-start | bytes 3145732
  155.7 2.4 copy-start.20
  155.7 3.8 copy-start.15
  155.8 3.8 copy-start.16
  155.8 3.8 copy-start.17
  155.8 3.8 copy-start.18
  158.2 7.2 %copy-start.6 = (f32[512,512]{1,0:T(8,128)}, f32[512,512]{1,0:T(8,128)S(1)}, u32[]{:S(2)}) copy-start(f32[512,512]{1,0:T(8,128)S(1)} %fusion.35) | copy-start | bytes 3145732
  159.5 1.6 copy-start.12
  159.5 1.6 copy-start.13
  161.2 1.7 copy-start.30
  161.2 2.4 copy-start.23
  161.2 2.4 copy-start.24
  161.2 2.4 copy-start.25
  161.2 2.6 copy-start.26
  163.8 3.7 copy-start.21
  166.2 9.3 %copy-start.22 = (f32[512,4,128]{2,0,1:T(8,128)S(1)}, f32[512,4,128]{2,0,1:T(8,128)}, u32[]{:S(2)}) copy-start(f32[512,4,128]{2,0,1:T(8,128)} %copy.69) | copy-start | bytes 3145732
  166.2 9.3 %collective-permute-start.1 = (bf16[8,128,128]{2,1,0:T(8,128)(2,1)}, bf16[8,128,128]{2,1,0:T(8,128)(2,1)S(1)}, u32[]{:S(2)}, u32[]{:S(2)}) collective-permute-start(bf16[8,128,128]{2,1,0:T(8,128)(2,1)} %pad_maximum_fusion.6), channel_id=1, source_target_pairs={{0,1},{1,0},{2,3},{3,2},{4,5},{5,4},{6,7},{7,6},{8,9},{9,8},{10,11... | collective-permute-start | bytes 786440 | tf_op jit(solution)/shard_map/ppermute | solution.py:770
  175.5 4.3 %copy-start.19 = (bf16[8,128,128]{2,1,0:T(8,128)(2,1)}, bf16[8,128,128]{2,1,0:T(8,128)(2,1)S(1)}, u32[]{:S(2)}) copy-start(bf16[8,128,128]{2,1,0:T(8,128)(2,1)S(1)} %broadcast_select_fusion.state) | copy-start | bytes 786436
  181.7 2.9 copy-start.3
  184.6 2.5 copy-start.4
  184.6 1.6 copy-start.7
  187.1 1.4 copy-start.1
  367.1 1.2 copy-start
  376.0 3.3 copy-start.14

commit v3 on v2

--- a/solution.py
+++ b/solution.py
@@ -277,7 +277,7 @@
 
 MESH = pl.DeviceIdType.MESH
 NCH = 11
-RA = 16
+RA = 24
 HR = 32
 SP = 2
 SPW = 2
@@ -307,75 +307,234 @@
     d=lax.axis_index("dp")
     return d//4, (d//2)%2, d%2, lax.axis_index("head")
 def dev(z,x,c,y): return ((z*2+x)*2+c, y)
-def gather_kernel(s_ref, wq, wk, wv, wg, wo, W3, pq, pk, pv, pg, po, zs, zr, xs, xr, ys, yr, ds, dr, wys, wyr, wzs, wzr, wxs, wxr, wds, wdr, ls):
-    z,x,c,y=place()
-    zp=[lax.rem(z+r,4) for r in (1,2,3)]
-    bar=pltpu.get_barrier_semaphore()
-    peers=[dev(q,x,c,y) for q in zp]+[dev(z,1-x,c,y),dev(z,x,1-c,y),dev(z,x,c,1-y)]
-    for p in peers: pl.semaphore_signal(bar,inc=1,device_id=p,device_id_type=MESH)
-    pl.semaphore_wait(bar,len(peers))
-    X=dev(z,1-x,c,y); Y=dev(z,x,c,1-y); C=dev(z,x,1-c,y)
-    col=pl.ds(pl.multiple_of(y*128,128),128)
-    own=[wq,wk,wv,wg,wo]; par=[pq,pk,pv,pg,po]
-    def rc(src,dst,ss,rs,d): return pltpu.make_async_remote_copy(src_ref=src,dst_ref=dst,send_sem=ss,recv_sem=rs,device_id=d,device_id_type=MESH)
-    loc=pltpu.make_async_copy(s_ref, W3.at[:,z,:,x,c,y], ls)
-    loc.start()
-    def st(k,i):
-        if k==0:
-            o=[]
-            for n,q in enumerate(zp):
-                t=W3.at[i,z,:,x,c,y]
-                o.append(rc(s_ref.at[i],t,zs.at[i,n],zr.at[i,n],dev(q,x,c,y)))
-            return o
-        if k==1:
-            a=W3.at[i,:,:,x,c,y,0:RA]; b=W3.at[i,:,:,x,c,y,RA:64]
-            return [rc(a,a,xs.at[i,0],xr.at[i,0],X), rc(b,b,ys.at[i,0],yr.at[i,0],Y)]
-        if k==2:
-            a=W3.at[i,:,:,:,c,y,0:RA]; b=W3.at[i,:,:,x,c,:,RA:64]
-            return [rc(b,b,xs.at[i,1],xr.at[i,1],X), rc(a,a,ys.at[i,1],yr.at[i,1],Y)]
-        if k==3:
-            a=W3.at[i,:,:,:,c]
-            return [rc(a,a,ds.at[i],dr.at[i],C)]
-    zb=lax.rem(z,2); ZP=dev(z+1-2*zb,x,c,y)
-    def wst(k,j):
-        if k==0: return [rc(own[j].at[zb,c],par[j].at[zb,c],wys.at[j],wyr.at[j],Y)]
-        if k==1:
-            a=par[j].at[zb,c]
-            return [rc(a,a,wxs.at[j],wxr.at[j],ZP)]
-        if k==2:
-            a=par[j].at[:,c]
-            return [rc(a,a,wds.at[j],wdr.at[j],C)]
-        return []
-    live={}
-    def go(f,tag,k,i,n):
-        if 0<=i<n:
-            if k>0:
-                for cp in live[(tag,k-1,i)]: cp.wait_recv()
-            if k<4:
-                live[(tag,k,i)]=f(k,i)
-                for cp in live[(tag,k,i)]: cp.start()
-    for t in range(NCH+4*SP):
-        for k in (4,3,2,1,0):
-            go(wst,"w",k,t-k*SPW,5)
-        if t==min(1,SP-1): loc.wait()
-        for k in (4,3,2,1,0):
-            go(st,"f",k,t-k*SP,NCH)
+def forward_kernel(tokens, cot, lengths, dec, fv, fg, fo, wq, wk, wv, wg, wo,
+                   state, scal, rates, mid, go, W3, pq, pk, pv, pg, po, middle, gate, unit, gated, qpre, kpre, vals, normed,
+                   S, WV, WO, GT, MX, BQ, BK, AG_, AU, AD, AV, AN, QB, KB, GS, GR,
+                   zs, zr, xs, xr, ys, yr, ds, dr, wys, wyr, wxs, wxr, wds, wdr, gss, gsr, rss, rsr, ls, ws, os):
+    z, x, c, y = place()
+    zp = [lax.rem(z + r, 4) for r in (1, 2, 3)]
+    X, Y, C = dev(z, 1 - x, c, y), dev(z, x, c, 1 - y), dev(z, x, 1 - c, y)
+    zb = lax.rem(z, 2)
+    ZP = dev(z + 1 - 2 * zb, x, c, y)
+    bar = pltpu.get_barrier_semaphore()
+    peers = [dev(q, x, c, y) for q in zp] + [X, Y, C]
+    for p in peers:
+        pl.semaphore_signal(bar, inc=1, device_id=p, device_id_type=MESH)
+    own, par = (wq, wk, wv, wg, wo), (pq, pk, pv, pg, po)
+
+    def rc(src, dst, ss, rs, d):
+        return pltpu.make_async_remote_copy(src_ref=src, dst_ref=dst, send_sem=ss, recv_sem=rs, device_id=d, device_id_type=MESH)
+
+    def wload(j, h):
+        src = (own if h == 0 else par)[j]
+        dst = WV.at[2 * j + h] if j < 4 else WO.at[h]
+        return pltpu.make_async_copy(src, dst, ws.at[2 * j + h])
+
+    for j in range(5):
+        wload(j, 0).start()
+    for i in range(NCH):
+        S[i, 0] = fv[:, i * 128 : i * 128 + 128]
+        S[i, 1] = fg[:, i * 128 : i * 128 + 128]
+        S[i, 2] = fo[i * 128 : i * 128 + 128, :].T
+    rates[0] = dec[...]
+    pl.semaphore_wait(bar, len(peers))
+    mine = pltpu.make_async_copy(S, W3.at[:, z, :, x, c, y], ls)
+    mine.start()
+    rate = rc(dec, rates.at[1], rss, rsr, Y)
+
+    def st(k, i):
+        if k == 0:
+            return [rc(S.at[i], W3.at[i, z, :, x, c, y], zs.at[i, n], zr.at[i, n], dev(q, x, c, y)) for n, q in enumerate(zp)]
+        if k == 1:
+            a, b = W3.at[i, :, :, x, c, y, 0:RA], W3.at[i, :, :, x, c, y, RA:64]
+            return [rc(a, a, xs.at[i, 0], xr.at[i, 0], X), rc(b, b, ys.at[i, 0], yr.at[i, 0], Y)]
+        if k == 2:
+            a, b = W3.at[i, :, :, :, c, y, 0:RA], W3.at[i, :, :, x, c, :, RA:64]
+            return [rc(b, b, xs.at[i, 1], xr.at[i, 1], X), rc(a, a, ys.at[i, 1], yr.at[i, 1], Y)]
+        a = W3.at[i, :, :, :, c]
+        return [rc(a, a, ds.at[i], dr.at[i], C)]
+
+    def quarter(r):
+        n = r.shape[0] // 4
+        return lambda a, b: r.at[pl.ds(pl.multiple_of((2 * a + b) * n, 128), n)]
+
+    def wst(k, j):
+        if k == 0:
+            return [rc(quarter(own[j])(zb, c), quarter(par[j])(zb, c), wys.at[j], wyr.at[j], Y)]
+        if k == 1:
+            a = quarter(par[j])(zb, c)
+            return [rc(a, a, wxs.at[j], wxr.at[j], ZP)]
+        return [rc(quarter(par[j])(b, c), quarter(par[j])(b, c), wds.at[j, b], wdr.at[j, b], C) for b in (0, 1)]
+
+    live = {}
+
+    def go_on(f, tag, k, i, n, last):
+        if 0 <= i < n:
+            if k > 0:
+                for cp in live[(tag, k - 1, i)]:
+                    cp.wait_recv()
+            if k < last:
+                live[(tag, k, i)] = f(k, i)
+                for cp in live[(tag, k, i)]:
+                    cp.start()
+
+    def tick(t):
+        for k in (3, 2, 1, 0):
+            go_on(wst, 0, k, t - k * SPW, 5, 3)
+        if t == 1:
+            mine.wait()
+        for k in (4, 3, 2, 1, 0):
+            go_on(st, 1, k, t - k * SP, NCH, 4)
+
+    outs = []
+
+    def put(src, dst):
+        cp = pltpu.make_async_copy(src, dst, os.at[len(outs)])
+        cp.start()
+        outs.append(cp)
+
+    def head(h):
+        return pl.ds(pl.multiple_of(h * 128, 128), 128)
+
+    tau = lax.broadcasted_iota(jnp.int32, (512, 1), 0).astype(f32)
+    rho = lax.broadcasted_iota(jnp.int32, (1, 512), 1).astype(f32)
+
+    def rate_of(h):
+        return rates[h // 4, pl.ds(lax.rem(h, 4), 1), 0:1]
+
+    def norm_rows():
+        v = tokens[...].astype(f32)
+        f = lax.rsqrt(jnp.mean(v * v, axis=1, keepdims=True) + epsilon)
+        scal[:, 3:4] = f
+        AN[...] = (v * f).astype(bf)
+        put(AN, normed)
+        pos = lax.broadcasted_iota(jnp.int32, (512, 1), 0) + y * 512
+        keep = (pos < lengths[0]).astype(f32)
+        scal[:, 0:1] = keep
+        go[...] = (cot[...].astype(f32) * keep).astype(bf)
+
+    def project(j, h):
+        cols = slice(h * 512, h * 512 + 512)
+        v = dot(AN[...], WV[2 * j + h])
+        if j == 0:
+            BQ[:, cols] = v.astype(bf)
+            QB[:, cols] = (v * jax.nn.sigmoid(v)).astype(bf)
+        if j == 1:
+            BK[:, cols] = v.astype(bf)
+            KB[:, cols] = (v * jax.nn.sigmoid(v)).astype(bf)
+        if j == 2:
+            AV[:, cols] = v.astype(bf)
+        if j == 3:
+            GT[:, cols] = v
+            AG_[:, cols] = v.astype(bf)
+
+    def project_own(*js):
+        for j in js:
+            wload(j, 0).wait()
+            project(j, 0)
+
+    def project_part(j):
+        wload(j, 1).wait()
+        project(j, 1)
+        put(*((BQ, qpre), (BK, kpre), (AV, vals), (AG_, gate))[j])
+
+    def update(h, _):
+        hs = head(h)
+        kl = (KB[:, hs].astype(f32) * jnp.exp(-rate_of(h) * (511.0 - tau))).astype(bf)
+        GS[lax.rem(h + 4, 8)] = dottn(kl, AV[:, hs]).astype(bf)
+        return 0
+
+    hand = rc(GS, GR, gss, gsr, Y)
+    ti = lax.broadcasted_iota(jnp.int32, (512, 512), 0)
+    ri = lax.broadcasted_iota(jnp.int32, (512, 512), 1)
+
+    def inner(h, _):
+        hs = head(h)
+        r = rate_of(h)
+        within = jnp.where(ti >= ri, jnp.exp(-r * (tau + 1.0)) * jnp.exp(r * (rho + 1.0)), 0.0)
+        MX[:, hs] = dot((dotnt(QB[:, hs], KB[:, hs]) * within).astype(bf), AV[:, hs])
+        return 0
+
+    alive = (y == 1).astype(f32)
+
+    def outer(h, _):
+        hs = head(h)
+        s = (GR[h].astype(f32) * alive).astype(bf)
+        state[h] = s
+        MX[:, hs] = MX[:, hs] + jnp.exp(-rate_of(h) * (tau + 1.0)) * dot(QB[:, hs], s)
+        return 0
+
+    def gating():
+        m = MX[...]
+        f = lax.rsqrt(jnp.mean(m * m, axis=1, keepdims=True) + epsilon)
+        scal[:, 2:3] = f
+        u = m * f
+        AU[...] = u.astype(bf)
+        put(AU, unit)
+        AD[...] = (u * GT[...]).astype(bf)
+        put(AD, gated)
+
+    def middle_rows():
+        wload(4, 0).wait()
+        wload(4, 1).wait()
+        m = tokens[...].astype(f32) + dot(AD[:, 0:512], WO[0]) + dot(AD[:, 512:1024], WO[1])
+        f = lax.rsqrt(jnp.mean(m * m, axis=1, keepdims=True) + epsilon)
+        scal[:, 1:2] = f
+        MX[...] = m
+        put(MX, middle)
+        mid[...] = (m * f).astype(bf)
+
+    loops = lambda f, a, b: lax.fori_loop(a, b, f, 0)
+    W = 3 * SPW
+    for t in range(NCH + 4 * SP):
+        tick(t)
+        if t == 0:
+            rate.start()
+            norm_rows()
+        if t == 1:
+            project_own(0, 1)
+        if t == 2:
+            project_own(2, 3)
+        if W <= t < W + 5:
+            wload(t - W, 1).start()
+        if W + 1 <= t < W + 5:
+            project_part(t - W - 1)
+        if t == W + 3:
+            rate.wait()
+            loops(update, 0, 8)
+            hand.start()
+        if t == W + 4:
+            loops(inner, 0, 8)
+        if t == W + 6:
+            hand.wait()
+            loops(outer, 0, 8)
+            gating()
+            middle_rows()
     for cps in live.values():
-        for cp in cps: cp.wait_send()
-def gather_call(s, ws):
-    D=pltpu.SemaphoreType.DMA
-    bf=jnp.bfloat16
-    outs=[jax.ShapeDtypeStruct((NCH,4,3,2,2,2,64,128),bf)]+[jax.ShapeDtypeStruct((2,2,256,512),bf)]*4+[jax.ShapeDtypeStruct((2,2,128,1024),bf)]
-    A=pl.BlockSpec(memory_space=pl.ANY)
-    sem=[(NCH,3),(NCH,3),(NCH,2),(NCH,2),(NCH,2),(NCH,2),(NCH,),(NCH,),(5,),(5,),(5,3),(5,3),(5,),(5,),(5,),(5,)]
-    return pl.pallas_call(gather_kernel,out_shape=outs,in_specs=[pl.BlockSpec(memory_space=pltpu.VMEM)]+[A]*5,out_specs=[A]*6,
-        scratch_shapes=[D(v) for v in sem]+[D(())],
-        compiler_params=pltpu.CompilerParams(collective_id=1,has_side_effects=True,vmem_limit_bytes=60<<20))(s,*ws)
-def prep(fv,fg,fo):
-    s=jnp.stack([fv,fg,fo.T])
-    return s.reshape(3,64,NCH,128).transpose(2,0,1,3)
-def wviews(wq,wk,wv,wg,wo):
-    return [w.reshape(2,2,256,512) for w in (wq,wk,wv,wg)]+[wo.reshape(2,2,128,1024)]
+        for cp in cps:
+            cp.wait_send()
+    for cp in outs:
+        cp.wait()
+
+
+def forward_call(*ins):
+    D, V, S = pltpu.SemaphoreType.DMA, pltpu.VMEM, jax.ShapeDtypeStruct
+    A, VM = pl.BlockSpec(memory_space=pl.ANY), pl.BlockSpec(memory_space=pltpu.VMEM)
+    act, w = (512, 1024), (1024, 512)
+    outs = [S((8, 128, 128), bf), S((512, 4), f32), S((2, 8, 128), f32), S(act, bf), S(act, bf),
+            S((NCH, 4, 3, 2, 2, 2, 64, 128), bf)] + [S(w, bf)] * 4 + [S(act, bf), S(act, f32)] + [S(act, bf)] * 7
+    scratch = [V((NCH, 3, 64, 128), bf), V((8,) + w, bf), V((2,) + act, bf), V(act, f32), V(act, f32)] + [V(act, bf)] * 9
+    scratch += [V((8, 128, 128), bf)] * 2
+    n = (NCH,)
+    scratch += [D(s) for s in ((NCH, 3), (NCH, 3), (NCH, 2), (NCH, 2), (NCH, 2), (NCH, 2), n, n, (5,), (5,), (5,), (5,), (5, 2), (5, 2), (), (), (), (), (), (10,), (8,))]
+    return pl.pallas_call(
+        forward_kernel,
+        out_shape=outs,
+        in_specs=[VM, VM, pl.BlockSpec(memory_space=pltpu.SMEM)] + [VM] * 4 + [A] * 5,
+        out_specs=[VM] * 5 + [A] * 14,
+        scratch_shapes=scratch,
+        compiler_params=pltpu.CompilerParams(collective_id=1, has_side_effects=True, vmem_limit_bytes=67043328),
+    )(*ins)
 def backward_kernel(mid, go, rates, scal, state, W3, middle, gate, unit, gated, qpre, kpre, vals, normed, wq, wk, wv, wg, wo, pq, pk, pv, pg, po,
                     output, dtok, sh, O,
                     G, RD, R1, R2, Q, RZ, FN, WT, LT, ACC, DV, R, UN, NM, DMX, WB, WO, GS, GR,
@@ -591,13 +750,16 @@
     def silu(v):
         return v * jax.nn.sigmoid(v)
 
+    def rate_of(h):
+        return rates[h // 4, pl.ds(lax.rem(h, 4), 1), 0:1]
+
     tau = lax.broadcasted_iota(jnp.int32, (512, 1), 0).astype(f32)
     rho = lax.broadcasted_iota(jnp.int32, (1, 512), 1).astype(f32)
 
     def first(h, _):
         hs = head(h)
         q = silu(R[4, :, hs].astype(f32)).astype(bf)
-        gf = (DMX[:, hs].astype(f32) * jnp.exp(-rates[h] * (tau + 1.0))).astype(bf)
+        gf = (DMX[:, hs].astype(f32) * jnp.exp(-rate_of(h) * (tau + 1.0))).astype(bf)
         GS[lax.rem(h + 4, 8)] = dottn(q, gf).astype(bf)
         return 0
 
@@ -612,7 +774,7 @@
         hs = head(h)
         qp, kp = R[4, :, hs].astype(f32), R[3, :, hs].astype(f32)
         q, k, v, dmx = silu(qp).astype(bf), silu(kp).astype(bf), R[2, :, hs], DMX[:, hs]
-        cf, rf = jnp.exp(-rates[h] * (tau + 1.0)), jnp.exp(rates[h] * (rho + 1.0))
+        cf, rf = jnp.exp(-rate_of(h) * (tau + 1.0)), jnp.exp(rate_of(h) * (rho + 1.0))
         within = jnp.where(ti >= ri, cf * rf, 0.0)
         wt = (dotnt(q, k) * within).astype(bf)
         dsc = (dotnt(dmx, v) * within).astype(bf)
@@ -638,7 +800,7 @@
         kp = R[3, :, hs].astype(f32)
         sk = jax.nn.sigmoid(kp)
         k = (kp * sk).astype(bf)
-        lf = jnp.exp(-rates[h] * (511.0 - tau))
+        lf = jnp.exp(-rate_of(h) * (511.0 - tau))
         kl = (k.astype(f32) * lf).astype(bf)
         dk = ACC[:, hs] + lf * dotnt(R[2, :, hs], gin)
         R[2, :, hs] = (DV[:, hs] + dot(kl, gin)).astype(bf)
@@ -712,7 +874,7 @@
     return pl.pallas_call(
         backward_kernel,
         out_shape=[S(act, bf), S(act, f32), S((3, 64, 1408), f32), S((NWG, 4, 2, 2, 64, 128), bf)],
-        in_specs=[VM] * 2 + [pl.BlockSpec(memory_space=pltpu.SMEM)] + [VM] * 2 + [A] * 19,
+        in_specs=[VM] * 5 + [A] * 19,
         out_specs=[VM] * 3 + [A],
         scratch_shapes=scratch,
         compiler_params=pltpu.CompilerParams(collective_id=2, has_side_effects=True, vmem_limit_bytes=67043328),
@@ -746,48 +908,11 @@
     )(o, sh)
 
 def fast_body(tokens, lengths, decay, w_query, w_key, w_value, w_gate, w_out, f_value, f_gate, f_out, cotangent):
-    own_rows = tokens.shape[0]
-    y = lax.axis_index("head")
-    swap = [(0, 1), (1, 0)]
-    rates = jnp.concatenate([decay, lax.ppermute(decay, "head", swap)])
-    within, first_decay, last_decay, _ = decay_tables(rates)
-    positions = y * own_rows + jnp.arange(own_rows, dtype=jnp.int32)
-    keep_rows = (positions < lengths[0]).astype(f32)[:, None]
-    inputs_f = tokens.astype(f32)
-    normed, scale_in = normalize(inputs_f)
-    normed_low = normed.astype(bf)
-    W3, *parts = gather_call(prep(f_value, f_gate, f_out), wviews(w_query, w_key, w_value, w_gate, w_out))
-    pq, pk, pv, pg = [p.reshape(1024, 512) for p in parts[:4]]
-    po = parts[4].reshape(512, 1024)
-    two = lambda a, b: jnp.concatenate([matmul(normed_low, a), matmul(normed_low, b)], axis=1)
-    query_pre, keys_pre, values_pre, gate_pre = two(w_query, pq), two(w_key, pk), two(w_value, pv), two(w_gate, pg)
-    heads = lambda t: t.reshape(own_rows, 8, HD).transpose(1, 0, 2)
-    flat = lambda t: t.transpose(1, 0, 2).reshape(own_rows, 8 * HD)
-    query = heads(jax.nn.silu(query_pre).astype(bf))
-    keys = heads(jax.nn.silu(keys_pre).astype(bf))
-    values = heads(values_pre.astype(bf))
-    ein = lambda form, a, b: jnp.einsum(form, a, b, preferred_element_type=f32)
-    swapped = lambda t: lax.ppermute(jnp.concatenate([t[4:], t[:4]]).astype(bf), "head", swap)
-    keys_last = (keys.astype(f32) * last_decay[:, :, None]).astype(bf)
-    update = ein("htd,hte->hde", keys_last, values)
-    state = swapped(update)
-    state = jnp.where(y == 1, state, jnp.zeros_like(state))
-    weights = (ein("htd,hrd->htr", query, keys) * within).astype(bf)
-    mixed = flat(ein("htr,hrd->htd", weights, values) + first_decay[:, :, None] * ein("htd,hde->hte", query, state))
-    scale_out = lax.rsqrt(jnp.mean(mixed * mixed, axis=1, keepdims=True) + epsilon)
-    mixed_unit = mixed * scale_out
-    gated = (mixed_unit * gate_pre).astype(bf)
-    middle = inputs_f + matmul(gated[:, :512], w_out) + matmul(gated[:, 512:], po)
-    mid_normed, scale_mid = normalize(middle)
-    mid_low = mid_normed.astype(bf)
-    grad_out = cotangent.astype(f32) * keep_rows
-    grad_low = grad_out.astype(bf)
-    scal = jnp.concatenate([keep_rows, scale_mid, scale_out, scale_in], axis=1)
-    view = lambda p: p.reshape(1024, 512)
-    output, d_tokens, shares, grads = backward_call(
-        mid_low, grad_low, rates, scal, state, W3, middle, gate_pre.astype(bf), mixed_unit.astype(bf), gated,
-        query_pre.astype(bf), keys_pre.astype(bf), values_pre.astype(bf), normed_low,
-        w_query, w_key, w_value, w_gate, w_out, pq, pk, pv, pg, po)
+    dec = jnp.concatenate([jnp.broadcast_to(decay[:, None], (4, 128)), jnp.zeros((4, 128), f32)])
+    weights = (w_query, w_key, w_value, w_gate, w_out)
+    state, scal, rates, mid, go, W3, pq, pk, pv, pg, po, middle, *acts = forward_call(
+        tokens, cotangent, lengths, dec, f_value, f_gate, f_out, *weights)
+    output, d_tokens, shares, grads = backward_call(mid, go, rates, scal, state, W3, middle, *acts, *weights, pq, pk, pv, pg, po)
     d_query, d_key, d_value, d_gate, d_out, d_f_value, d_f_gate, d_f_out = finish_call(grads.reshape(NWG, 1024, 128), shares)
     return (output, d_tokens, d_query, d_key, d_value, d_gate, d_out, d_f_value, d_f_gate, d_f_out)
 

time: 381 us -> 310 us (0.81)
  matrix products: 33.3 us -> 0 us
  local copies, waits for them, and re-layouts: 24.9 us -> 8.96 us
  other arithmetic: 15.8 us -> 0 us
    dot_general x13 -> x0, matrix products: 33.3 us -> none  [the longest x10 19.6 us: matmul(): return jnp.dot(left_side, right_side, preferred_element_type=jnp.float32)]
    concatenate x7 -> x2, local copies, waits for them, and re-layouts: 10.4 us -> 1.32 us  [fast_body(): jnp.concatenate([jnp.broadcast_to(decay[:, None], (4, 128)), jnp.zeros((4...]
    convert_element_type x8 -> x0, other arithmetic: 7.26 us -> none  [the longest x1 2.89 us: fast_body(): mixed_unit.astype(bf)]
    dot_general x4 -> x0, local copies, waits for them, and re-layouts: 4.04 us -> none  [matmul(): return jnp.dot(left_side, right_side, preferred_element_type=jnp.float32)]
    unnamed x65 -> x8, local copies, waits for them, and re-layouts: 7.35 us -> 7.63 us
  transfers between devices with their start and end apart: 2 -> 0, of which waited for: 0 -> 0; matrix products, arithmetic and copies ran while one was open for 13% -> 0% of each run, Pallas kernels for 31% -> 0%
where the time goes in v3:
time: 310 us
  Pallas kernels  300 us (97%)
  local copies, waits for them, and re-layouts  8.96 us (3%)
    pallas_call x1, Pallas kernels, backward_call(): pl.pallas_call(backward_kernel, out_shape=[S(act, bf), S(act, f32), S((3,...  178 us
    pallas_call x1, Pallas kernels, forward_call(): pl.pallas_call(forward_kernel, out_shape=outs, in_specs=[VM, VM, pl.Block...  114 us
    pallas_call x1, Pallas kernels, finish_call(): pl.pallas_call(finish_kernel, grid=(4,), out_shape=[S((1024, 512), f32)]...  7.64 us
    unnamed x8, local copies, waits for them, and re-layouts  7.63 us

profile of v3, /device:TPU:1, one launch (start us, length us, event | category | flops | bytes accessed | tf_op | source)
XLA Modules:
  0.0 310.1 jit_solution(9068563765829262471)
XLA Ops:
  1.3 0.7 concatenate.5
  1.9 0.7 concatenate.6.dec
  2.6 1.8 copy.22.fo
  4.4 114.3 %shard_map.195 = (bf16[8,128,128]{2,1,0:T(8,128)(2,1)}, f32[512,4]{1,0:T(8,128)}, f32[2,8,128]{2,1,0:T(8,128)}, bf16[512,1024]{1,0:T(8,128)(2,1)}, bf16[512,1024...) custom-call(bf16[512,1024]{1,0:T(8,128)(2,1)} %tokens.1, ...), custom_call_target="tpu_custom_call" | custom-call | tf_op jit(solution)/shard_map/pallas_call | solution.py:530
  118.8 177.8 %shard_map.196 = (bf16[512,1024]{1,0:T(8,128)(2,1)}, f32[512,1024]{1,0:T(8,128)}, f32[3,64,1408]{2,1,0:T(8,128)}, bf16[20,4,2,2,64,128]{5,4,3,2,1,0:T(8,128)(2,1)}) custom-call(bf16[512,1024]{1,0:T(8,128)(2,1)} %get-tuple-element.41.mid, bf16[512,1024]{1,0:T(8,128)(2,1)} %get-tuple-element.42.go, f32[2,8,128]{2,1,0:T(8,128)} %get-tuple-element.43.rates, ...), custom_call_target="tpu_custom_call" | custom-call | tf_op jit(solution)/shard_map/pallas_call | solution.py:874
  296.6 0.0 copy-start
  296.6 1.2 copy-done
  297.9 7.6 %shard_map.197 = (f32[1024,512]{1,0:T(8,128)}, f32[1024,512]{1,0:T(8,128)}, f32[1024,512]{1,0:T(8,128)}, f32[1024,512]{1,0:T(8,128)}, f32[512,1024]{1,0:T(8,128)...) custom-call(bf16[20,1024,128]{2,1,0:T(8,128)(2,1)} %bitcast.1, f32[3,64,1408]{2,1,0:T(8,128)S(1)} %copy-done), custom_call_target="tpu_custom_call" | custom-call | tf_op jit(solution)/shard_map/pallas_call | solution.py:901
  305.5 0.0 copy-start.1
  305.5 1.0 copy.23
  306.5 2.3 copy.27
  308.8 0.0 copy-done.1
  308.8 1.3 copy.28
Async XLA Ops:
  296.6 1.2 copy-start
  305.5 3.3 %copy-start.1 = (f32[512,1024]{1,0:T(8,128)S(1)}, f32[512,1024]{1,0:T(8,128)}, u32[]{:S(2)}) copy-start(f32[512,1024]{1,0:T(8,128)} %get-tuple-element.93) | copy-start | bytes 6291460

commit v4 on v3

--- a/solution.py
+++ b/solution.py
@@ -281,6 +281,8 @@
 HR = 32
 SP = 2
 SPW = 2
+NEAR = 2
+MEET = 13
 NWG = 20
 NALL = NCH + NWG
 RS_AT = (1, 2, 4, 6, 8)
@@ -307,10 +309,11 @@
     d=lax.axis_index("dp")
     return d//4, (d//2)%2, d%2, lax.axis_index("head")
 def dev(z,x,c,y): return ((z*2+x)*2+c, y)
-def forward_kernel(tokens, cot, lengths, dec, fv, fg, fo, wq, wk, wv, wg, wo,
-                   state, scal, rates, mid, go, W3, pq, pk, pv, pg, po, middle, gate, unit, gated, qpre, kpre, vals, normed,
-                   S, WV, WO, GT, MX, BQ, BK, AG_, AU, AD, AV, AN, QB, KB, GS, GR,
-                   zs, zr, xs, xr, ys, yr, ds, dr, wys, wyr, wxs, wxr, wds, wdr, gss, gsr, rss, rsr, ls, ws, os):
+def layer_kernel(tokens, cot, lengths, dec, fv, fg, fo, wq, wk, wv, wg, wo,
+                 output, dtok, sh, O, W3, pq, pk, pv, pg, po,
+                 S, WV, WO, G, RD, R1, R2, Q, RZ, FN, WT, LT, ACC, DV, R, UN, NM, DMX, mid, go, scal, rates, state, GS, GR, GS2, GR2,
+                 zs, zr, xs, xr, ys, yr, nxs, nxr, nys, nyr, ds, dr, wys, wyr, wxs, wxr, wds, wdr, gss, gsr, rss, rsr, ls, ws,
+                 wsem, bsem, g2s, g2r, e_s, e_r, fx_s, fx_r, fy_s, fy_r, fz_s, fz_r, az_s, az_r, ax_s, ax_r, ad_s, ad_r, fl):
     z, x, c, y = place()
     zp = [lax.rem(z + r, 4) for r in (1, 2, 3)]
     X, Y, C = dev(z, 1 - x, c, y), dev(z, x, c, 1 - y), dev(z, x, 1 - c, y)
@@ -327,7 +330,7 @@
 
     def wload(j, h):
         src = (own if h == 0 else par)[j]
-        dst = WV.at[2 * j + h] if j < 4 else WO.at[h]
+        dst = WV.at[j] if j < 4 else WO.at[h]
         return pltpu.make_async_copy(src, dst, ws.at[2 * j + h])
 
     for j in range(5):
@@ -335,24 +338,40 @@
     for i in range(NCH):
         S[i, 0] = fv[:, i * 128 : i * 128 + 128]
         S[i, 1] = fg[:, i * 128 : i * 128 + 128]
-        S[i, 2] = fo[i * 128 : i * 128 + 128, :].T
+        S[i, 2] = fo[:, i * 128 : i * 128 + 128]
     rates[0] = dec[...]
+    dtok[...] = jnp.zeros_like(dtok)
     pl.semaphore_wait(bar, len(peers))
     mine = pltpu.make_async_copy(S, W3.at[:, z, :, x, c, y], ls)
     mine.start()
     rate = rc(dec, rates.at[1], rss, rsr, Y)
 
+    far = [lax.rem(z + r, 4) for r in (3, 2, 1)]
+
     def st(k, i):
         if k == 0:
             return [rc(S.at[i], W3.at[i, z, :, x, c, y], zs.at[i, n], zr.at[i, n], dev(q, x, c, y)) for n, q in enumerate(zp)]
         if k == 1:
-            a, b = W3.at[i, :, :, x, c, y, 0:RA], W3.at[i, :, :, x, c, y, RA:64]
-            return [rc(a, a, xs.at[i, 0], xr.at[i, 0], X), rc(b, b, ys.at[i, 0], yr.at[i, 0], Y)]
+            o = []
+            for n, q in enumerate(far):
+                a, b = W3.at[i, q, :, x, c, y, 0:RA], W3.at[i, q, :, x, c, y, RA:64]
+                o += [rc(a, a, xs.at[i, 0, n], xr.at[i, 0, n], X), rc(b, b, ys.at[i, 0, n], yr.at[i, 0, n], Y)]
+            return o
         if k == 2:
-            a, b = W3.at[i, :, :, :, c, y, 0:RA], W3.at[i, :, :, x, c, :, RA:64]
-            return [rc(b, b, xs.at[i, 1], xr.at[i, 1], X), rc(a, a, ys.at[i, 1], yr.at[i, 1], Y)]
+            o = []
+            for n, q in enumerate(far):
+                a, b = W3.at[i, q, :, :, c, y, 0:RA], W3.at[i, q, :, x, c, :, RA:64]
+                o += [rc(b, b, xs.at[i, 1, n], xr.at[i, 1, n], X), rc(a, a, ys.at[i, 1, n], yr.at[i, 1, n], Y)]
+            return o
         a = W3.at[i, :, :, :, c]
         return [rc(a, a, ds.at[i], dr.at[i], C)]
+
+    def near(k):
+        if k == 0:
+            return [rc(S.at[:, :, 0:RA], W3.at[:, z, :, x, c, y, 0:RA], nxs.at[0], nxr.at[0], X),
+                    rc(S.at[:, :, RA:64], W3.at[:, z, :, x, c, y, RA:64], nys.at[0], nyr.at[0], Y)]
+        a, b = W3.at[:, z, :, :, c, y, 0:RA], W3.at[:, z, :, x, c, :, RA:64]
+        return [rc(b, b, nxs.at[1], nxr.at[1], X), rc(a, a, nys.at[1], nyr.at[1], Y)]
 
     def quarter(r):
         n = r.shape[0] // 4
@@ -366,32 +385,56 @@
             return [rc(a, a, wxs.at[j], wxr.at[j], ZP)]
         return [rc(quarter(par[j])(b, c), quarter(par[j])(b, c), wds.at[j, b], wdr.at[j, b], C) for b in (0, 1)]
 
-    live = {}
-
-    def go_on(f, tag, k, i, n, last):
-        if 0 <= i < n:
-            if k > 0:
-                for cp in live[(tag, k - 1, i)]:
-                    cp.wait_recv()
-            if k < last:
-                live[(tag, k, i)] = f(k, i)
-                for cp in live[(tag, k, i)]:
-                    cp.start()
+    def near_step(k):
+        if k == 1:
+            mine.wait()
+        if k > 0:
+            for cp in near(k - 1):
+                cp.wait_recv()
+        if k < 2:
+            for cp in near(k):
+                cp.start()
+
+    def weight_step(k, j):
+        if k > 0:
+            for cp in wst(k - 1, j):
+                cp.wait_recv()
+        if k < 3:
+            for cp in wst(k, j):
+                cp.start()
+
+    def gather_step(k, i):
+        came = st(k - 1, i) if k > 0 else []
+        new = st(k, i) if k < 4 else []
+        parts = 3 if k in (1, 2) else 1
+        for m in range(parts):
+            for cp in came[m * len(came) // parts : (m + 1) * len(came) // parts]:
+                cp.wait_recv()
+            for cp in new[m * len(new) // parts : (m + 1) * len(new) // parts]:
+                cp.start()
+
+    def gather_tick(t):
+        for k in (4, 3, 2, 1, 0):
+            i = t - k * SP
+
+            @pl.when((i >= 0) & (i < NCH))
+            def _():
+                gather_step(k, i)
 
     def tick(t):
+        if t == 0:
+            near_step(0)
         for k in (3, 2, 1, 0):
-            go_on(wst, 0, k, t - k * SPW, 5, 3)
-        if t == 1:
-            mine.wait()
-        for k in (4, 3, 2, 1, 0):
-            go_on(st, 1, k, t - k * SP, NCH, 4)
-
-    outs = []
-
-    def put(src, dst):
-        cp = pltpu.make_async_copy(src, dst, os.at[len(outs)])
-        cp.start()
-        outs.append(cp)
+            if 0 <= t - k * SPW < 5:
+                weight_step(k, t - k * SPW)
+        if t == NEAR:
+            near_step(1)
+        if t == 3 * SP:
+            near_step(2)
+        gather_tick(t)
+
+    def silu(v):
+        return v * jax.nn.sigmoid(v)
 
     def head(h):
         return pl.ds(pl.multiple_of(h * 128, 128), 128)
@@ -406,27 +449,27 @@
         v = tokens[...].astype(f32)
         f = lax.rsqrt(jnp.mean(v * v, axis=1, keepdims=True) + epsilon)
         scal[:, 3:4] = f
-        AN[...] = (v * f).astype(bf)
-        put(AN, normed)
+        NM[...] = (v * f).astype(bf)
         pos = lax.broadcasted_iota(jnp.int32, (512, 1), 0) + y * 512
         keep = (pos < lengths[0]).astype(f32)
         scal[:, 0:1] = keep
         go[...] = (cot[...].astype(f32) * keep).astype(bf)
+        LT[1] = go[...].T
 
     def project(j, h):
         cols = slice(h * 512, h * 512 + 512)
-        v = dot(AN[...], WV[2 * j + h])
+        v = dot(NM[...], WV[j])
         if j == 0:
-            BQ[:, cols] = v.astype(bf)
-            QB[:, cols] = (v * jax.nn.sigmoid(v)).astype(bf)
+            R[4, :, cols] = v.astype(bf)
+            DMX[:, cols] = (v * jax.nn.sigmoid(v)).astype(bf)
         if j == 1:
-            BK[:, cols] = v.astype(bf)
-            KB[:, cols] = (v * jax.nn.sigmoid(v)).astype(bf)
+            R[3, :, cols] = v.astype(bf)
+            UN[:, cols] = (v * jax.nn.sigmoid(v)).astype(bf)
         if j == 2:
-            AV[:, cols] = v.astype(bf)
+            R[2, :, cols] = v.astype(bf)
         if j == 3:
-            GT[:, cols] = v
-            AG_[:, cols] = v.astype(bf)
+            DV[:, cols] = v
+            R[1, :, cols] = v.astype(bf)
 
     def project_own(*js):
         for j in js:
@@ -436,12 +479,11 @@
     def project_part(j):
         wload(j, 1).wait()
         project(j, 1)
-        put(*((BQ, qpre), (BK, kpre), (AV, vals), (AG_, gate))[j])
 
     def update(h, _):
         hs = head(h)
-        kl = (KB[:, hs].astype(f32) * jnp.exp(-rate_of(h) * (511.0 - tau))).astype(bf)
-        GS[lax.rem(h + 4, 8)] = dottn(kl, AV[:, hs]).astype(bf)
+        kl = (UN[:, hs].astype(f32) * jnp.exp(-rate_of(h) * (511.0 - tau))).astype(bf)
+        GS[lax.rem(h + 4, 8)] = dottn(kl, R[2, :, hs]).astype(bf)
         return 0
 
     hand = rc(GS, GR, gss, gsr, Y)
@@ -452,7 +494,7 @@
         hs = head(h)
         r = rate_of(h)
         within = jnp.where(ti >= ri, jnp.exp(-r * (tau + 1.0)) * jnp.exp(r * (rho + 1.0)), 0.0)
-        MX[:, hs] = dot((dotnt(QB[:, hs], KB[:, hs]) * within).astype(bf), AV[:, hs])
+        ACC[:, hs] = dot((dotnt(DMX[:, hs], UN[:, hs]) * within).astype(bf), R[2, :, hs])
         return 0
 
     alive = (y == 1).astype(f32)
@@ -461,32 +503,184 @@
         hs = head(h)
         s = (GR[h].astype(f32) * alive).astype(bf)
         state[h] = s
-        MX[:, hs] = MX[:, hs] + jnp.exp(-rate_of(h) * (tau + 1.0)) * dot(QB[:, hs], s)
+        ACC[:, hs] = ACC[:, hs] + jnp.exp(-rate_of(h) * (tau + 1.0)) * dot(DMX[:, hs], s)
         return 0
 
     def gating():
-        m = MX[...]
+        m = ACC[...]
         f = lax.rsqrt(jnp.mean(m * m, axis=1, keepdims=True) + epsilon)
         scal[:, 2:3] = f
         u = m * f
-        AU[...] = u.astype(bf)
-        put(AU, unit)
-        AD[...] = (u * GT[...]).astype(bf)
-        put(AD, gated)
+        UN[...] = u.astype(bf)
+        R[0] = (u * DV[...]).astype(bf)
 
     def middle_rows():
         wload(4, 0).wait()
         wload(4, 1).wait()
-        m = tokens[...].astype(f32) + dot(AD[:, 0:512], WO[0]) + dot(AD[:, 512:1024], WO[1])
+        m = tokens[...].astype(f32) + dot(R[0, :, 0:512], WO[0]) + dot(R[0, :, 512:1024], WO[1])
         f = lax.rsqrt(jnp.mean(m * m, axis=1, keepdims=True) + epsilon)
         scal[:, 1:2] = f
-        MX[...] = m
-        put(MX, middle)
+        ACC[...] = m
         mid[...] = (m * f).astype(bf)
-
+        LT[0] = mid[...].T
+
+    def tload(i, s):
+        return [pltpu.make_async_copy(W3.at[i, :, :, :, :, h], WT.at[s, :, :, :, :, :, pl.ds(h * 128, 128)], wsem.at[s, h]) for h in (0, 1)]
+
+    def cps(k, i, hr):
+        g, s, n = lax.rem(i, NCH), lax.rem(i, 4), 3 if hr else 1
+        if k == 0:
+            return [rc(G.at[g, 1 - c, 0:n], RD.at[lax.rem(i, 2), 0:n], e_s.at[i], e_r.at[i], C)]
+        if k == 1:
+            o = [rc(G.at[g, c, 0:n, :, :, 1 - y, hr:64], R1.at[s, 0:n, :, :, hr:64], fy_s.at[i, 0], fy_r.at[i, 0], Y)]
+            if hr:
+                o.append(rc(G.at[g, c, 0:n, :, 1 - x, :, 0:hr], R1.at[s, 0:n, :, :, 0:hr], fx_s.at[i, 0], fx_r.at[i, 0], X))
+            return o
+        if k == 2:
+            o = [rc(G.at[g, c, 0:n, :, 1 - x, y, hr:64], R2.at[s, 0:n, :, hr:64], fx_s.at[i, 1], fx_r.at[i, 1], X)]
+            if hr:
+                o.append(rc(G.at[g, c, 0:n, :, x, 1 - y, 0:hr], R2.at[s, 0:n, :, 0:hr], fy_s.at[i, 1], fy_r.at[i, 1], Y))
+            return o
+        if k == 3:
+            return [rc(Q.at[s, 0:n, q], RZ.at[s, m, 0:n], fz_s.at[i, m], fz_r.at[i, m], dev(q, x, c, y)) for m, q in enumerate(zp)]
+
+    def ags(k, w):
+        if k == 0:
+            f = FN.at[lax.rem(w, 4)]
+            return [rc(f, O.at[w, z, x, c], az_s.at[w, n], az_r.at[w, n], dev(q, x, c, y)) for n, q in enumerate(zp)]
+        if k == 1:
+            return [rc(O.at[w, :, x, c], O.at[w, :, x, c], ax_s.at[w], ax_r.at[w], X)]
+        if k == 2:
+            return [rc(O.at[w, :, :, c], O.at[w, :, :, c], ad_s.at[w], ad_r.at[w], C)]
+
+    def flush(w):
+        return pltpu.make_async_copy(FN.at[lax.rem(w, 4)], O.at[w, z, x, c], fl.at[w])
+
+    def reduce(k, i, hr):
+        g, s, n = lax.rem(i, NCH), lax.rem(i, 4), 3 if hr else 1
+        up = lambda v: v.astype(f32)
+        if k == 1:
+            G[g, c, 0:n] = (up(G[g, c, 0:n]) + up(RD[lax.rem(i, 2), 0:n])).astype(bf)
+        if k == 2:
+            if hr:
+                G[g, c, 0:n, :, x, :, 0:hr] = (up(G[g, c, 0:n, :, x, :, 0:hr]) + up(R1[s, 0:n, :, :, 0:hr])).astype(bf)
+            G[g, c, 0:n, :, :, y, hr:64] = (up(G[g, c, 0:n, :, :, y, hr:64]) + up(R1[s, 0:n, :, :, hr:64])).astype(bf)
+        if k == 3:
+            Q[s, 0:n] = (up(G[g, c, 0:n, :, x, y]) + up(R2[s, 0:n])).astype(bf)
+        if k == 4:
+            v = up(Q[s, 0:n, z])
+            for m in range(3):
+                v = v + up(RZ[s, m, 0:n])
+            if hr:
+                sh[:, :, pl.ds(pl.multiple_of(i * 128, 128), 128)] = v
+            else:
+                FN[lax.rem(i - NCH, 4)] = v[0].astype(bf)
+
+    def arrive(k, i, hr):
+        if k > 0:
+            for cp in cps(k - 1, i, hr):
+                cp.wait_recv()
+        if k == 1:
+            for cp in cps(0, i, hr):
+                cp.wait_send()
+        if k == 4:
+            for kk in (1, 2, 3):
+                for cp in cps(kk, i, hr):
+                    cp.wait_send()
+        reduce(k, i, hr)
+
+    def leave(k, i, hr):
+        for cp in cps(k, i, hr):
+            cp.start()
+
+    def both(f, k, t):
+        i = t - RS_AT[k]
+
+        @pl.when((i >= 0) & (i < NCH))
+        def _():
+            f(k, i, HR)
+
+        @pl.when((i >= NCH) & (i < NALL))
+        def _():
+            f(k, i, 0)
+
+    def ag_arrive(k, t):
+        w = t - AG_AT[k] - NCH
+
+        @pl.when((w >= 0) & (w < NWG))
+        def _():
+            for cp in ags(k, w):
+                cp.wait_recv()
+            if k == 0:
+                for cp in ags(0, w):
+                    cp.wait_send()
+                flush(w).wait()
+
+    def ag_leave(k, t):
+        w = t - (AG_AT[k - 1] if k else RS_AT[4]) - NCH
+
+        @pl.when((w >= 0) & (w < NWG))
+        def _():
+            for cp in ags(k, w):
+                cp.start()
+            if k == 0:
+                flush(w).start()
+
+    def stages(t):
+        ag_arrive(2, t)
+        ag_arrive(1, t)
+        ag_arrive(0, t)
+        ag_leave(2, t)
+        both(arrive, 4, t)
+        ag_leave(1, t)
+        both(arrive, 3, t)
+        ag_leave(0, t)
+        both(arrive, 2, t)
+        both(leave, 3, t)
+        both(arrive, 1, t)
+        for k in (2, 1, 0):
+            both(leave, k, t)
+
+    def store(g, t, r, own):
+        r = r.astype(bf).reshape(4, 2, 2, 64, 256)
+        for cc in (0, 1):
+            G[g, cc, t, :, :, own] = r[:, :, cc, :, 0:128]
+            G[g, cc, t, :, :, 1 - own] = r[:, :, cc, :, 128:256]
+
+    def ffn(t):
+        s = lax.rem(t, 2)
+        for cp in tload(t, s):
+            cp.wait()
+
+        @pl.when(t + 1 < NCH)
+        def _():
+            for cp in tload(t + 1, 1 - s):
+                cp.start()
+
+        fv, fg, fo = [WT[s, :, n].reshape(1024, 256) for n in range(3)]
+        m, g_ = mid[...], go[...]
+        v, g, gh = dot(m, fv), dot(m, fg), dot(g_, fo)
+        hid, dv, dg = (v * g).astype(bf), (gh * g).astype(bf), (gh * v).astype(bf)
+        ACC[...] += dotnt(hid, fo)
+        dtok[...] += dotnt(dv, fv) + dotnt(dg, fg)
+        store(t, 0, dot(LT[0], dv), 0)
+        store(t, 1, dot(LT[0], dg), 0)
+        store(t, 2, dot(LT[1], hid), 0)
+
+    def ffn_tick(t, _):
+        stages(t)
+
+        def one(n, _):
+            ffn(n)
+            return 0
+
+        lax.fori_loop(jnp.maximum(t, 2 * t - 7), jnp.maximum(t + 1, 2 * t - 5), one, 0)
+        return 0
+
+    T = 9
     loops = lambda f, a, b: lax.fori_loop(a, b, f, 0)
     W = 3 * SPW
-    for t in range(NCH + 4 * SP):
+    for t in range(MEET):
         tick(t)
         if t == 0:
             rate.start()
@@ -510,223 +704,16 @@
             loops(outer, 0, 8)
             gating()
             middle_rows()
-    for cps in live.values():
-        for cp in cps:
-            cp.wait_send()
-    for cp in outs:
-        cp.wait()
-
-
-def forward_call(*ins):
-    D, V, S = pltpu.SemaphoreType.DMA, pltpu.VMEM, jax.ShapeDtypeStruct
-    A, VM = pl.BlockSpec(memory_space=pl.ANY), pl.BlockSpec(memory_space=pltpu.VMEM)
-    act, w = (512, 1024), (1024, 512)
-    outs = [S((8, 128, 128), bf), S((512, 4), f32), S((2, 8, 128), f32), S(act, bf), S(act, bf),
-            S((NCH, 4, 3, 2, 2, 2, 64, 128), bf)] + [S(w, bf)] * 4 + [S(act, bf), S(act, f32)] + [S(act, bf)] * 7
-    scratch = [V((NCH, 3, 64, 128), bf), V((8,) + w, bf), V((2,) + act, bf), V(act, f32), V(act, f32)] + [V(act, bf)] * 9
-    scratch += [V((8, 128, 128), bf)] * 2
-    n = (NCH,)
-    scratch += [D(s) for s in ((NCH, 3), (NCH, 3), (NCH, 2), (NCH, 2), (NCH, 2), (NCH, 2), n, n, (5,), (5,), (5,), (5,), (5, 2), (5, 2), (), (), (), (), (), (10,), (8,))]
-    return pl.pallas_call(
-        forward_kernel,
-        out_shape=outs,
-        in_specs=[VM, VM, pl.BlockSpec(memory_space=pltpu.SMEM)] + [VM] * 4 + [A] * 5,
-        out_specs=[VM] * 5 + [A] * 14,
-        scratch_shapes=scratch,
-        compiler_params=pltpu.CompilerParams(collective_id=1, has_side_effects=True, vmem_limit_bytes=67043328),
-    )(*ins)
-def backward_kernel(mid, go, rates, scal, state, W3, middle, gate, unit, gated, qpre, kpre, vals, normed, wq, wk, wv, wg, wo, pq, pk, pv, pg, po,
-                    output, dtok, sh, O,
-                    G, RD, R1, R2, Q, RZ, FN, WT, LT, ACC, DV, R, UN, NM, DMX, WB, WO, GS, GR,
-                    wsem, lsem, bsem, gss, gsr, ds, dr, xs, xr, ys, yr, zs, zr, az_s, az_r, ax_s, ax_r, ad_s, ad_r, fl):
-    z, x, c, y = place()
-    zp = [lax.rem(z + r, 4) for r in (1, 2, 3)]
-    X, Y, C = dev(z, 1 - x, c, y), dev(z, x, c, 1 - y), dev(z, x, 1 - c, y)
-    bar = pltpu.get_barrier_semaphore()
-    peers = [dev(q, x, c, y) for q in zp] + [X, Y, C]
-    for p in peers:
-        pl.semaphore_signal(bar, inc=1, device_id=p, device_id_type=MESH)
-
-    def rc(src, dst, ss, rs, d):
-        return pltpu.make_async_remote_copy(src_ref=src, dst_ref=dst, send_sem=ss, recv_sem=rs, device_id=d, device_id_type=MESH)
-
-    def wload(i, s):
-        return [pltpu.make_async_copy(W3.at[i, :, :, :, :, h], WT.at[s, :, :, :, :, :, pl.ds(h * 128, 128)], wsem.at[s, h]) for h in (0, 1)]
-
-    loads = [pltpu.make_async_copy(a, b, lsem.at[n]) for n, (a, b) in enumerate(
-        [(middle, ACC), (gated, R.at[0]), (gate, R.at[1]), (vals, R.at[2]), (kpre, R.at[3]), (qpre, R.at[4]), (unit, UN), (normed, NM), (wo, WO.at[0]), (po, WO.at[1])])]
-    for cp in wload(0, 0):
-        cp.start()
-    for cp in loads:
-        cp.start()
-    mats = (wg, pg, wv, pv, wk, pk, wq, pq)
-
-    def wbload(n):
-        return pltpu.make_async_copy(mats[n], WB.at[n % 2], bsem.at[n % 2])
-
-    wbload(0).start()
-    wbload(1).start()
-    LT[0] = mid[...].T
-    LT[1] = go[...].T
-    dtok[...] = jnp.zeros_like(dtok)
-    loads[0].wait()
-    pl.semaphore_wait(bar, len(peers))
-
-    def cps(k, i, hr):
-        g, s, n = lax.rem(i, NCH), lax.rem(i, 4), 3 if hr else 1
-        if k == 0:
-            return [rc(G.at[g, 1 - c, 0:n], RD.at[lax.rem(i, 2), 0:n], ds.at[i], dr.at[i], C)]
-        if k == 1:
-            o = [rc(G.at[g, c, 0:n, :, :, 1 - y, hr:64], R1.at[s, 0:n, :, :, hr:64], ys.at[i, 0], yr.at[i, 0], Y)]
-            if hr:
-                o.append(rc(G.at[g, c, 0:n, :, 1 - x, :, 0:hr], R1.at[s, 0:n, :, :, 0:hr], xs.at[i, 0], xr.at[i, 0], X))
-            return o
-        if k == 2:
-            o = [rc(G.at[g, c, 0:n, :, 1 - x, y, hr:64], R2.at[s, 0:n, :, hr:64], xs.at[i, 1], xr.at[i, 1], X)]
-            if hr:
-                o.append(rc(G.at[g, c, 0:n, :, x, 1 - y, 0:hr], R2.at[s, 0:n, :, 0:hr], ys.at[i, 1], yr.at[i, 1], Y))
-            return o
-        if k == 3:
-            return [rc(Q.at[s, 0:n, q], RZ.at[s, m, 0:n], zs.at[i, m], zr.at[i, m], dev(q, x, c, y)) for m, q in enumerate(zp)]
-
-    def ags(k, w):
-        if k == 0:
-            f = FN.at[lax.rem(w, 4)]
-            return [rc(f, O.at[w, z, x, c], az_s.at[w, n], az_r.at[w, n], dev(q, x, c, y)) for n, q in enumerate(zp)]
-        if k == 1:
-            return [rc(O.at[w, :, x, c], O.at[w, :, x, c], ax_s.at[w], ax_r.at[w], X)]
-        if k == 2:
-            return [rc(O.at[w, :, :, c], O.at[w, :, :, c], ad_s.at[w], ad_r.at[w], C)]
-
-    def flush(w):
-        return pltpu.make_async_copy(FN.at[lax.rem(w, 4)], O.at[w, z, x, c], fl.at[w])
-
-    def reduce(k, i, hr):
-        g, s, n = lax.rem(i, NCH), lax.rem(i, 4), 3 if hr else 1
-        up = lambda v: v.astype(f32)
-        if k == 1:
-            G[g, c, 0:n] = (up(G[g, c, 0:n]) + up(RD[lax.rem(i, 2), 0:n])).astype(bf)
-        if k == 2:
-            if hr:
-                G[g, c, 0:n, :, x, :, 0:hr] = (up(G[g, c, 0:n, :, x, :, 0:hr]) + up(R1[s, 0:n, :, :, 0:hr])).astype(bf)
-            G[g, c, 0:n, :, :, y, hr:64] = (up(G[g, c, 0:n, :, :, y, hr:64]) + up(R1[s, 0:n, :, :, hr:64])).astype(bf)
-        if k == 3:
-            Q[s, 0:n] = (up(G[g, c, 0:n, :, x, y]) + up(R2[s, 0:n])).astype(bf)
-        if k == 4:
-            v = up(Q[s, 0:n, z])
-            for m in range(3):
-                v = v + up(RZ[s, m, 0:n])
-            if hr:
-                sh[:, :, pl.ds(pl.multiple_of(i * 128, 128), 128)] = v
-            else:
-                FN[lax.rem(i - NCH, 4)] = v[0].astype(bf)
-
-    def arrive(k, i, hr):
-        if k > 0:
-            for cp in cps(k - 1, i, hr):
-                cp.wait_recv()
-        if k == 1:
-            for cp in cps(0, i, hr):
-                cp.wait_send()
-        if k == 4:
-            for kk in (1, 2, 3):
-                for cp in cps(kk, i, hr):
-                    cp.wait_send()
-        reduce(k, i, hr)
-
-    def leave(k, i, hr):
-        for cp in cps(k, i, hr):
-            cp.start()
-
-    def both(f, k, t):
-        i = t - RS_AT[k]
-
-        @pl.when((i >= 0) & (i < NCH))
-        def _():
-            f(k, i, HR)
-
-        @pl.when((i >= NCH) & (i < NALL))
-        def _():
-            f(k, i, 0)
-
-    def ag_arrive(k, t):
-        w = t - AG_AT[k] - NCH
-
-        @pl.when((w >= 0) & (w < NWG))
-        def _():
-            for cp in ags(k, w):
-                cp.wait_recv()
-            if k == 0:
-                for cp in ags(0, w):
-                    cp.wait_send()
-                flush(w).wait()
-
-    def ag_leave(k, t):
-        w = t - (AG_AT[k - 1] if k else RS_AT[4]) - NCH
-
-        @pl.when((w >= 0) & (w < NWG))
-        def _():
-            for cp in ags(k, w):
+            for cp in tload(0, 0):
                 cp.start()
-            if k == 0:
-                flush(w).start()
-
-    def stages(t):
-        ag_arrive(2, t)
-        ag_arrive(1, t)
-        ag_arrive(0, t)
-        ag_leave(2, t)
-        both(arrive, 4, t)
-        ag_leave(1, t)
-        both(arrive, 3, t)
-        ag_leave(0, t)
-        both(arrive, 2, t)
-        both(leave, 3, t)
-        both(arrive, 1, t)
-        for k in (2, 1, 0):
-            both(leave, k, t)
-
-    def store(g, t, r, own):
-        r = r.astype(bf).reshape(4, 2, 2, 64, 256)
-        for cc in (0, 1):
-            G[g, cc, t, :, :, own] = r[:, :, cc, :, 0:128]
-            G[g, cc, t, :, :, 1 - own] = r[:, :, cc, :, 128:256]
-
-    def ffn(t):
-        s = lax.rem(t, 2)
-        for cp in wload(t, s):
-            cp.wait()
-
-        @pl.when(t + 1 < NCH)
-        def _():
-            for cp in wload(t + 1, 1 - s):
-                cp.start()
-
-        fv, fg, fo = [WT[s, :, n].reshape(1024, 256) for n in range(3)]
-        m, g_ = mid[...], go[...]
-        v, g, gh = dot(m, fv), dot(m, fg), dot(g_, fo)
-        hid, dv, dg = (v * g).astype(bf), (gh * g).astype(bf), (gh * v).astype(bf)
-        ACC[...] += dotnt(hid, fo)
-        dtok[...] += dotnt(dv, fv) + dotnt(dg, fg)
-        store(t, 0, dot(LT[0], dv), 0)
-        store(t, 1, dot(LT[0], dg), 0)
-        store(t, 2, dot(LT[1], hid), 0)
-
-    def ffn_tick(t, _):
-        stages(t)
-
-        def one(n, _):
-            ffn(n)
-            return 0
-
-        lax.fori_loop(jnp.maximum(2 * t - 1, 0), jnp.minimum(2 * t + 1, NCH), one, 0)
-        return 0
-
-    T = 6
-    lax.fori_loop(0, T, ffn_tick, 0)
+
+    def meet_tick(t, _):
+        gather_tick(t)
+        return ffn_tick(t - MEET, 0)
+
+    lax.fori_loop(MEET, NCH + 4 * SP, meet_tick, 0)
+    lax.fori_loop(NCH + 4 * SP - MEET, T, ffn_tick, 0)
     stages(T)
-    for cp in loads[1:]:
-        cp.wait()
     keep, scale_mid, scale_out, scale_in = [scal[:, n : n + 1] for n in range(4)]
     output[...] = (ACC[...] * keep).astype(bf)
     n2 = mid[...].astype(f32)
@@ -739,37 +726,22 @@
     for h in (0, 1):
         cols = slice(h * 512, h * 512 + 512)
         ACC[:, cols] = dotnt(gml, WO[h])
+    stages(T + 1)
     dgt, un = ACC[...], UN[...].astype(f32)
     du = dgt * R[1].astype(f32)
     R[1] = (dgt * un).astype(bf)
     DMX[...] = (scale_out * (du - un * jnp.mean(du * un, axis=1, keepdims=True))).astype(bf)
 
-    def head(h):
-        return pl.ds(pl.multiple_of(h * 128, 128), 128)
-
-    def silu(v):
-        return v * jax.nn.sigmoid(v)
-
-    def rate_of(h):
-        return rates[h // 4, pl.ds(lax.rem(h, 4), 1), 0:1]
-
-    tau = lax.broadcasted_iota(jnp.int32, (512, 1), 0).astype(f32)
-    rho = lax.broadcasted_iota(jnp.int32, (1, 512), 1).astype(f32)
-
     def first(h, _):
         hs = head(h)
         q = silu(R[4, :, hs].astype(f32)).astype(bf)
         gf = (DMX[:, hs].astype(f32) * jnp.exp(-rate_of(h) * (tau + 1.0))).astype(bf)
-        GS[lax.rem(h + 4, 8)] = dottn(q, gf).astype(bf)
+        GS2[lax.rem(h + 4, 8)] = dottn(q, gf).astype(bf)
         return 0
 
     lax.fori_loop(0, 8, first, 0)
-    stages(T + 1)
-    later = rc(GS, GR, gss, gsr, Y)
+    later = rc(GS2, GR2, g2s, g2r, Y)
     later.start()
-    ti = lax.broadcasted_iota(jnp.int32, (512, 512), 0)
-    ri = lax.broadcasted_iota(jnp.int32, (512, 512), 1)
-
     def pair(h, _):
         hs = head(h)
         qp, kp = R[4, :, hs].astype(f32), R[3, :, hs].astype(f32)
@@ -786,17 +758,11 @@
         R[4, :, hs] = (dq * (sq * (1.0 + qp * (1.0 - sq)))).astype(bf)
         return 0
 
-    stages(T + 2)
-    lax.fori_loop(0, 4, pair, 0)
-    stages(T + 3)
-    lax.fori_loop(4, 8, pair, 0)
-    stages(T + 4)
-    later.wait()
     live = (y == 0).astype(f32)
 
     def finish(h, _):
         hs = head(h)
-        gin = (GR[h].astype(f32) * live).astype(bf)
+        gin = (GR2[h].astype(f32) * live).astype(bf)
         kp = R[3, :, hs].astype(f32)
         sk = jax.nn.sigmoid(kp)
         k = (kp * sk).astype(bf)
@@ -807,7 +773,6 @@
         R[3, :, hs] = (dk * (sk * (1.0 + kp * (1.0 - sk)))).astype(bf)
         return 0
 
-    lax.fori_loop(0, 8, finish, 0)
     def wgrad(p):
         j, cp = p // 4, lax.rem(p, 4)
         lo = pl.multiple_of(cp * 128, 128)
@@ -818,23 +783,34 @@
         stages(t)
         p = t - NCH
         wgrad(p)
+
+        @pl.when(p < 8)
+        def _():
+            pair(p, 0)
+
+        @pl.when(p == 7)
+        def _():
+            later.wait()
+            lax.fori_loop(0, 8, finish, 0)
+
         for n in range(8):
-            @pl.when(p == n)
+            @pl.when(p == n + 8)
             def _():
                 wbload(n).wait()
 
-        @pl.when(p < 8)
+        @pl.when((p >= 8) & (p < 16))
         def _():
-            j, h = 1 + p // 2, lax.rem(p, 2)
-            part = dotnt(R[j, :, pl.ds(pl.multiple_of(h * 512, 128), 512)], WB[h])
-            ACC[...] = jnp.where(p == 0, 0.0, ACC[...]) + part
+            n = p - 8
+            j, h = 1 + n // 2, lax.rem(n, 2)
+            part = dotnt(R[j, :, pl.ds(pl.multiple_of(h * 512, 128), 512)], WV[h])
+            ACC[...] = jnp.where(n == 0, 0.0, ACC[...]) + part
 
         for n in range(6):
-            @pl.when(p == n)
+            @pl.when(p == n + 8)
             def _():
                 wbload(n + 2).start()
 
-        @pl.when(p == 8)
+        @pl.when(p == 16)
         def _():
             n1 = NM[...].astype(f32)
             dn = ACC[...]
@@ -842,6 +818,13 @@
 
         return 0
 
+    mats = (wg, pg, wv, pv, wk, pk, wq, pq)
+
+    def wbload(n):
+        return pltpu.make_async_copy(mats[n], WV.at[n % 2], bsem.at[n % 2])
+
+    wbload(0).start()
+    wbload(1).start()
     lax.fori_loop(NCH, NCH + NWG, wg_tick, 0)
     def tail(t, _):
         stages(t)
@@ -857,29 +840,48 @@
 
     lax.fori_loop(0, NWG, drain, 0)
 
-
-def backward_call(mid, go, rates, scal, state, *rest):
-    D, V = pltpu.SemaphoreType.DMA, pltpu.VMEM
+    def drain_gather(i, _):
+        for k in range(4):
+            for cp in st(k, i):
+                cp.wait_send()
+        return 0
+
+    lax.fori_loop(0, NCH, drain_gather, 0)
+    for k in (0, 1):
+        for cp in near(k):
+            cp.wait_send()
+    for j in range(5):
+        for k in range(3):
+            for cp in wst(k, j):
+                cp.wait_send()
+
+
+def layer_call(*ins):
+    D, V, S = pltpu.SemaphoreType.DMA, pltpu.VMEM, jax.ShapeDtypeStruct
     A, VM = pl.BlockSpec(memory_space=pl.ANY), pl.BlockSpec(memory_space=pltpu.VMEM)
-    act = (512, 1024)
-    scratch = [V((NCH, 2, 3, 4, 2, 2, 64, 128), bf), V((2, 3, 4, 2, 2, 64, 128), bf),
-               V((4, 3, 4, 2, 64, 128), bf), V((4, 3, 4, 64, 128), bf),
+    act, w = (512, 1024), (1024, 512)
+    outs = [S(act, bf), S(act, f32), S((3, 64, 1408), f32), S((NWG, 4, 2, 2, 64, 128), bf), S((NCH, 4, 3, 2, 2, 2, 64, 128), bf)] + [S(w, bf)] * 4 + [S(act, bf)]
+    scratch = [V((NCH, 3, 64, 128), bf), V((4,) + w, bf), V((2,) + act, bf),
+               V((NCH, 2, 3, 4, 2, 2, 64, 128), bf), V((2, 3, 4, 2, 2, 64, 128), bf), V((4, 3, 4, 2, 64, 128), bf), V((4, 3, 4, 64, 128), bf),
                V((4, 3, 4, 64, 128), bf), V((4, 3, 3, 64, 128), bf), V((4, 64, 128), bf), V((2, 4, 3, 2, 2, 64, 256), bf),
-               V((2, 1024, 512), bf), V(act, f32), V(act, f32), V((5,) + act, bf), V(act, bf), V(act, bf), V(act, bf),
-               V((2, 1024, 512), bf), V((2, 512, 1024), bf), V((8, 128, 128), bf), V((8, 128, 128), bf)]
-    n = NALL
-    scratch += [D(s) for s in ((2, 2), (10,), (2,), (), (), (n,), (n,), (n, 2), (n, 2), (n, 2), (n, 2), (n, 3), (n, 3),
-                               (NWG, 3), (NWG, 3), (NWG,), (NWG,), (NWG,), (NWG,), (NWG,))]
-    S = jax.ShapeDtypeStruct
+               V((2,) + w, bf), V(act, f32), V(act, f32), V((5,) + act, bf), V(act, bf), V(act, bf), V(act, bf), V(act, bf), V(act, bf),
+               V((512, 4), f32), V((2, 8, 128), f32)] + [V((8, 128, 128), bf)] * 5
+    n, m, a = (NCH,), (NALL,), (NWG,)
+    scratch += [D(s) for s in ((NCH, 3), (NCH, 3), (NCH, 2, 3), (NCH, 2, 3), (NCH, 2, 3), (NCH, 2, 3), (2,), (2,), (2,), (2,), n, n,
+                               (5,), (5,), (5,), (5,), (5, 2), (5, 2), (), (), (), (), (), (10,),
+                               (2, 2), (2,), (), (), m, m, (NALL, 2), (NALL, 2), (NALL, 2), (NALL, 2), (NALL, 3), (NALL, 3),
+                               (NWG, 3), (NWG, 3), a, a, a, a, a)]
     return pl.pallas_call(
-        backward_kernel,
-        out_shape=[S(act, bf), S(act, f32), S((3, 64, 1408), f32), S((NWG, 4, 2, 2, 64, 128), bf)],
-        in_specs=[VM] * 5 + [A] * 19,
-        out_specs=[VM] * 3 + [A],
+        layer_kernel,
+        out_shape=outs,
+        in_specs=[VM, VM, pl.BlockSpec(memory_space=pltpu.SMEM)] + [VM] * 4 + [A] * 5,
+        out_specs=[VM] * 3 + [A] * 7,
         scratch_shapes=scratch,
-        compiler_params=pltpu.CompilerParams(collective_id=2, has_side_effects=True, vmem_limit_bytes=67043328),
-    )(mid, go, rates, scal, state, *rest)
-def finish_kernel(o, sh, d_query, d_key, d_value, d_gate, d_out, d_f_value, d_f_gate, d_f_out):
+        compiler_params=pltpu.CompilerParams(collective_id=1, has_side_effects=True, vmem_limit_bytes=67043328),
+    )(*ins)
+def finish_kernel(o, sh, out, dtok, output, d_tokens, d_query, d_key, d_value, d_gate, d_out, d_f_value, d_f_gate, d_f_out):
+    output[...] = out[...]
+    d_tokens[...] = dtok[...]
     for n in range(4):
         cols = slice(n * 128, n * 128 + 128)
         d_out[cols, :] = o[n].astype(f32).T
@@ -892,29 +894,27 @@
     def _():
         d_f_value[...] = sh[0]
         d_f_gate[...] = sh[1]
-        d_f_out[...] = sh[2].T
-
-
-def finish_call(o, sh):
+        d_f_out[...] = sh[2]
+
+
+def finish_call(o, sh, out, dtok):
     S = jax.ShapeDtypeStruct
     whole = lambda *s: pl.BlockSpec(s, lambda i: (0,) * len(s))
     return pl.pallas_call(
         finish_kernel,
         grid=(4,),
-        out_shape=[S((1024, 512), f32)] * 4 + [S((512, 1024), f32)] + [S((64, 1408), f32)] * 2 + [S((1408, 64), f32)],
-        in_specs=[pl.BlockSpec((20, 256, 128), lambda i: (0, i, 0)), whole(3, 64, 1408)],
-        out_specs=[pl.BlockSpec((256, 512), lambda i: (i, 0))] * 4 + [pl.BlockSpec((512, 256), lambda i: (0, i))] + [whole(64, 1408)] * 2 + [whole(1408, 64)],
-        compiler_params=pltpu.CompilerParams(vmem_limit_bytes=48 << 20),
-    )(o, sh)
+        out_shape=[S((512, 1024), bf), S((512, 1024), f32)] + [S((1024, 512), f32)] * 4 + [S((512, 1024), f32)] + [S((64, 1408), f32)] * 3,
+        in_specs=[pl.BlockSpec((20, 256, 128), lambda i: (0, i, 0)), whole(3, 64, 1408)] + [pl.BlockSpec((128, 1024), lambda i: (i, 0))] * 2,
+        out_specs=[pl.BlockSpec((128, 1024), lambda i: (i, 0))] * 2 + [pl.BlockSpec((256, 512), lambda i: (i, 0))] * 4 + [pl.BlockSpec((512, 256), lambda i: (0, i))] + [whole(64, 1408)] * 3,
+        compiler_params=pltpu.CompilerParams(vmem_limit_bytes=67043328),
+    )(o, sh, out, dtok)
 
 def fast_body(tokens, lengths, decay, w_query, w_key, w_value, w_gate, w_out, f_value, f_gate, f_out, cotangent):
     dec = jnp.concatenate([jnp.broadcast_to(decay[:, None], (4, 128)), jnp.zeros((4, 128), f32)])
     weights = (w_query, w_key, w_value, w_gate, w_out)
-    state, scal, rates, mid, go, W3, pq, pk, pv, pg, po, middle, *acts = forward_call(
-        tokens, cotangent, lengths, dec, f_value, f_gate, f_out, *weights)
-    output, d_tokens, shares, grads = backward_call(mid, go, rates, scal, state, W3, middle, *acts, *weights, pq, pk, pv, pg, po)
-    d_query, d_key, d_value, d_gate, d_out, d_f_value, d_f_gate, d_f_out = finish_call(grads.reshape(NWG, 1024, 128), shares)
-    return (output, d_tokens, d_query, d_key, d_value, d_gate, d_out, d_f_value, d_f_gate, d_f_out)
+    output, d_tokens, shares, grads, *_ = layer_call(tokens, cotangent, lengths, dec, f_value, f_gate, f_out.T, *weights)
+    *results, d_f_out = finish_call(grads.reshape(NWG, 1024, 128), shares, output, d_tokens)
+    return (*results, d_f_out.T)
 
 
 def solution(mesh):

time: 310 us -> 285 us (0.919)
  Pallas kernels: 300 us -> 282 us
  local copies, waits for them, and re-layouts: 8.96 us -> 1.32 us
    pallas_call x3 -> x2, Pallas kernels: 300 us -> 282 us  [the longest x1 272 us: layer_call(): pl.pallas_call(layer_kernel, out_shape=outs, in_specs=[VM, VM, pl.BlockSp...]
    unnamed x8 -> x0, local copies, waits for them, and re-layouts: 7.63 us -> none
where the time goes in v4:
time: 285 us
  Pallas kernels  282 us (99%)
    pallas_call x1, Pallas kernels, layer_call(): pl.pallas_call(layer_kernel, out_shape=outs, in_specs=[VM, VM, pl.BlockSp...  272 us
    pallas_call x1, Pallas kernels, finish_call(): pl.pallas_call(finish_kernel, grid=(4,), out_shape=[S((512, 1024), bf), S...  9.79 us

profile of v4, /device:TPU:1, one launch (start us, length us, event | category | flops | bytes accessed | tf_op | source)
XLA Modules:
  0.0 285.0 jit_solution(10461785525683800938)
XLA Ops:
  1.3 0.7 concatenate.5
  1.9 0.7 concatenate.6.dec
  2.6 272.4 %shard_map.195 = (bf16[512,1024]{1,0:T(8,128)(2,1)}, f32[512,1024]{1,0:T(8,128)}, f32[3,64,1408]{2,1,0:T(8,128)}, bf16[20,4,2,2,64,128]{5,4,3,2,1,0:T(8,128)(2,1...) custom-call(bf16[512,1024]{1,0:T(8,128)(2,1)} %tokens.1, ...), custom_call_target="tpu_custom_call" | custom-call | tf_op jit(solution)/shard_map/pallas_call | solution.py:874
  275.0 9.8 %shard_map.196 = (bf16[512,1024]{1,0:T(8,128)(2,1)}, f32[512,1024]{1,0:T(8,128)}, f32[1024,512]{1,0:T(8,128)}, f32[1024,512]{1,0:T(8,128)}, f32[1024,512]{1,0:T(...) custom-call(bf16[20,1024,128]{2,1,0:T(8,128)(2,1)} %bitcast.3, ...), custom_call_target="tpu_custom_call" | custom-call | tf_op jit(solution)/shard_map/pallas_call | solution.py:903

commit v5 on v4

--- a/solution.py
+++ b/solution.py
@@ -277,14 +277,19 @@
 
 MESH = pl.DeviceIdType.MESH
 NCH = 11
-RA = 24
+RA = 16
 HR = 32
 SP = 2
-SPW = 2
 NEAR = 2
-MEET = 13
+MEET = 10
+W_AT = (0, 2, 4, 5)
+HAND = 4
+SLOTS = 4
+SLOT1 = 4
+NF = NCH
 NWG = 20
 NALL = NCH + NWG
+
 RS_AT = (1, 2, 4, 6, 8)
 AG_AT = (10, 12, 14)
 TN = (((0,), (0,)), ((), ()))
@@ -310,10 +315,10 @@
     return d//4, (d//2)%2, d%2, lax.axis_index("head")
 def dev(z,x,c,y): return ((z*2+x)*2+c, y)
 def layer_kernel(tokens, cot, lengths, dec, fv, fg, fo, wq, wk, wv, wg, wo,
-                 output, dtok, sh, O, W3, pq, pk, pv, pg, po,
-                 S, WV, WO, G, RD, R1, R2, Q, RZ, FN, WT, LT, ACC, DV, R, UN, NM, DMX, mid, go, scal, rates, state, GS, GR, GS2, GR2,
+                 output, d_tokens, shares, O, W3, pq, pk, pv, pg, po,
+                 S, WV, WO, G, RD, R1, R2, Q, RZ, FN, WT, LT, ACC, DV, R, UN, NM, DMX, mid, go, scal, rates, state, GS, GR, GS2, GR2, TK, OUT, dtok, sh,
                  zs, zr, xs, xr, ys, yr, nxs, nxr, nys, nyr, ds, dr, wys, wyr, wxs, wxr, wds, wdr, gss, gsr, rss, rsr, ls, ws,
-                 wsem, bsem, g2s, g2r, e_s, e_r, fx_s, fx_r, fy_s, fy_r, fz_s, fz_r, az_s, az_r, ax_s, ax_r, ad_s, ad_r, fl):
+                 wsem, bsem, g2s, g2r, e_s, e_r, fx_s, fx_r, fy_s, fy_r, fz_s, fz_r, az_s, az_r, ax_s, ax_r, ad_s, ad_r, fl, io):
     z, x, c, y = place()
     zp = [lax.rem(z + r, 4) for r in (1, 2, 3)]
     X, Y, C = dev(z, 1 - x, c, y), dev(z, x, c, 1 - y), dev(z, x, 1 - c, y)
@@ -323,7 +328,11 @@
     peers = [dev(q, x, c, y) for q in zp] + [X, Y, C]
     for p in peers:
         pl.semaphore_signal(bar, inc=1, device_id=p, device_id_type=MESH)
-    own, par = (wq, wk, wv, wg, wo), (pq, pk, pv, pg, po)
+    ins = [pltpu.make_async_copy(tokens, TK, io.at[0]), pltpu.make_async_copy(cot, go, io.at[1])]
+    for cp in ins:
+        cp.start()
+    outs = [pltpu.make_async_copy(a, b, io.at[2 + n]) for n, (a, b) in enumerate(((OUT, output), (dtok, d_tokens), (sh, shares)))]
+    own, par = (wk, wv, wq, wg, wo), (pk, pv, pq, pg, po)
 
     def rc(src, dst, ss, rs, d):
         return pltpu.make_async_remote_copy(src_ref=src, dst_ref=dst, send_sem=ss, recv_sem=rs, device_id=d, device_id_type=MESH)
@@ -339,12 +348,13 @@
         S[i, 0] = fv[:, i * 128 : i * 128 + 128]
         S[i, 1] = fg[:, i * 128 : i * 128 + 128]
         S[i, 2] = fo[:, i * 128 : i * 128 + 128]
-    rates[0] = dec[...]
+    for h in range(4):
+        rates[0, h : h + 1, :] = jnp.full((1, 128), dec[h], f32)
     dtok[...] = jnp.zeros_like(dtok)
     pl.semaphore_wait(bar, len(peers))
     mine = pltpu.make_async_copy(S, W3.at[:, z, :, x, c, y], ls)
     mine.start()
-    rate = rc(dec, rates.at[1], rss, rsr, Y)
+    rate = rc(rates.at[0], rates.at[1], rss, rsr, Y)
 
     far = [lax.rem(z + r, 4) for r in (3, 2, 1)]
 
@@ -424,11 +434,11 @@
     def tick(t):
         if t == 0:
             near_step(0)
-        for k in (3, 2, 1, 0):
-            if 0 <= t - k * SPW < 5:
-                weight_step(k, t - k * SPW)
         if t == NEAR:
             near_step(1)
+        for k in (3, 2, 1, 0):
+            if 0 <= t - W_AT[k] < 5:
+                weight_step(k, t - W_AT[k])
         if t == 3 * SP:
             near_step(2)
         gather_tick(t)
@@ -446,26 +456,28 @@
         return rates[h // 4, pl.ds(lax.rem(h, 4), 1), 0:1]
 
     def norm_rows():
-        v = tokens[...].astype(f32)
+        for cp in ins:
+            cp.wait()
+        v = TK[...].astype(f32)
         f = lax.rsqrt(jnp.mean(v * v, axis=1, keepdims=True) + epsilon)
         scal[:, 3:4] = f
         NM[...] = (v * f).astype(bf)
         pos = lax.broadcasted_iota(jnp.int32, (512, 1), 0) + y * 512
         keep = (pos < lengths[0]).astype(f32)
         scal[:, 0:1] = keep
-        go[...] = (cot[...].astype(f32) * keep).astype(bf)
+        go[...] = (go[...].astype(f32) * keep).astype(bf)
         LT[1] = go[...].T
 
     def project(j, h):
         cols = slice(h * 512, h * 512 + 512)
         v = dot(NM[...], WV[j])
-        if j == 0:
+        if j == 2:
             R[4, :, cols] = v.astype(bf)
             DMX[:, cols] = (v * jax.nn.sigmoid(v)).astype(bf)
-        if j == 1:
+        if j == 0:
             R[3, :, cols] = v.astype(bf)
             UN[:, cols] = (v * jax.nn.sigmoid(v)).astype(bf)
-        if j == 2:
+        if j == 1:
             R[2, :, cols] = v.astype(bf)
         if j == 3:
             DV[:, cols] = v
@@ -517,7 +529,7 @@
     def middle_rows():
         wload(4, 0).wait()
         wload(4, 1).wait()
-        m = tokens[...].astype(f32) + dot(R[0, :, 0:512], WO[0]) + dot(R[0, :, 512:1024], WO[1])
+        m = TK[...].astype(f32) + dot(R[0, :, 0:512], WO[0]) + dot(R[0, :, 512:1024], WO[1])
         f = lax.rsqrt(jnp.mean(m * m, axis=1, keepdims=True) + epsilon)
         scal[:, 1:2] = f
         ACC[...] = m
@@ -527,22 +539,30 @@
     def tload(i, s):
         return [pltpu.make_async_copy(W3.at[i, :, :, :, :, h], WT.at[s, :, :, :, :, :, pl.ds(h * 128, 128)], wsem.at[s, h]) for h in (0, 1)]
 
-    def cps(k, i, hr):
-        g, s, n = lax.rem(i, NCH), lax.rem(i, 4), 3 if hr else 1
+    def where(i, m):
+        if m == 0:
+            return i, slice(0, 3), 3, HR
+        if m == 2:
+            return i - NWG, slice(0, 3), 3, HR
+        e = i - NF
+        return e // 3, pl.ds(lax.rem(e, 3), 1), 1, 0
+
+    def cps(k, i, m):
+        (g, ts, n, hr), s, s1, sq = where(i, m), lax.rem(i, SLOTS), lax.rem(i, SLOT1), lax.rem(i, 4)
         if k == 0:
-            return [rc(G.at[g, 1 - c, 0:n], RD.at[lax.rem(i, 2), 0:n], e_s.at[i], e_r.at[i], C)]
+            return [rc(G.at[g, 1 - c, ts], RD.at[lax.rem(i, 2), 0:n], e_s.at[i], e_r.at[i], C)]
         if k == 1:
-            o = [rc(G.at[g, c, 0:n, :, :, 1 - y, hr:64], R1.at[s, 0:n, :, :, hr:64], fy_s.at[i, 0], fy_r.at[i, 0], Y)]
+            o = [rc(G.at[g, c, ts, :, :, 1 - y, hr:64], R1.at[s1, 0:n, :, :, hr:64], fy_s.at[i, 0], fy_r.at[i, 0], Y)]
             if hr:
-                o.append(rc(G.at[g, c, 0:n, :, 1 - x, :, 0:hr], R1.at[s, 0:n, :, :, 0:hr], fx_s.at[i, 0], fx_r.at[i, 0], X))
+                o.append(rc(G.at[g, c, ts, :, 1 - x, :, 0:hr], R1.at[s1, 0:n, :, :, 0:hr], fx_s.at[i, 0], fx_r.at[i, 0], X))
             return o
         if k == 2:
-            o = [rc(G.at[g, c, 0:n, :, 1 - x, y, hr:64], R2.at[s, 0:n, :, hr:64], fx_s.at[i, 1], fx_r.at[i, 1], X)]
+            o = [rc(G.at[g, c, ts, :, 1 - x, y, hr:64], R2.at[s, 0:n, :, hr:64], fx_s.at[i, 1], fx_r.at[i, 1], X)]
             if hr:
-                o.append(rc(G.at[g, c, 0:n, :, x, 1 - y, 0:hr], R2.at[s, 0:n, :, 0:hr], fy_s.at[i, 1], fy_r.at[i, 1], Y))
+                o.append(rc(G.at[g, c, ts, :, x, 1 - y, 0:hr], R2.at[s, 0:n, :, 0:hr], fy_s.at[i, 1], fy_r.at[i, 1], Y))
             return o
         if k == 3:
-            return [rc(Q.at[s, 0:n, q], RZ.at[s, m, 0:n], fz_s.at[i, m], fz_r.at[i, m], dev(q, x, c, y)) for m, q in enumerate(zp)]
+            return [rc(Q.at[sq, 0:n, q], RZ.at[s, u, 0:n], fz_s.at[i, u], fz_r.at[i, u], dev(q, x, c, y)) for u, q in enumerate(zp)]
 
     def ags(k, w):
         if k == 0:
@@ -556,56 +576,54 @@
     def flush(w):
         return pltpu.make_async_copy(FN.at[lax.rem(w, 4)], O.at[w, z, x, c], fl.at[w])
 
-    def reduce(k, i, hr):
-        g, s, n = lax.rem(i, NCH), lax.rem(i, 4), 3 if hr else 1
+    def reduce(k, i, m):
+        (g, ts, n, hr), s, s1, sq = where(i, m), lax.rem(i, SLOTS), lax.rem(i, SLOT1), lax.rem(i, 4)
         up = lambda v: v.astype(f32)
         if k == 1:
-            G[g, c, 0:n] = (up(G[g, c, 0:n]) + up(RD[lax.rem(i, 2), 0:n])).astype(bf)
+            G[g, c, ts] = (up(G[g, c, ts]) + up(RD[lax.rem(i, 2), 0:n])).astype(bf)
         if k == 2:
             if hr:
-                G[g, c, 0:n, :, x, :, 0:hr] = (up(G[g, c, 0:n, :, x, :, 0:hr]) + up(R1[s, 0:n, :, :, 0:hr])).astype(bf)
-            G[g, c, 0:n, :, :, y, hr:64] = (up(G[g, c, 0:n, :, :, y, hr:64]) + up(R1[s, 0:n, :, :, hr:64])).astype(bf)
+                G[g, c, ts, :, x, :, 0:hr] = (up(G[g, c, ts, :, x, :, 0:hr]) + up(R1[s1, 0:n, :, :, 0:hr])).astype(bf)
+            G[g, c, ts, :, :, y, hr:64] = (up(G[g, c, ts, :, :, y, hr:64]) + up(R1[s1, 0:n, :, :, hr:64])).astype(bf)
         if k == 3:
-            Q[s, 0:n] = (up(G[g, c, 0:n, :, x, y]) + up(R2[s, 0:n])).astype(bf)
+            Q[sq, 0:n] = (up(G[g, c, ts, :, x, y]) + up(R2[s, 0:n])).astype(bf)
         if k == 4:
-            v = up(Q[s, 0:n, z])
-            for m in range(3):
-                v = v + up(RZ[s, m, 0:n])
-            if hr:
-                sh[:, :, pl.ds(pl.multiple_of(i * 128, 128), 128)] = v
+            v = up(Q[sq, 0:n, z])
+            for u in range(3):
+                v = v + up(RZ[s, u, 0:n])
+            if m == 1:
+                FN[lax.rem(i - NF, 4)] = v[0].astype(bf)
             else:
-                FN[lax.rem(i - NCH, 4)] = v[0].astype(bf)
-
-    def arrive(k, i, hr):
+                sh[ts, :, pl.ds(pl.multiple_of(g * 128, 128), 128)] = v
+
+    def arrive(k, i, m):
         if k > 0:
-            for cp in cps(k - 1, i, hr):
+            for cp in cps(k - 1, i, m):
                 cp.wait_recv()
         if k == 1:
-            for cp in cps(0, i, hr):
+            for cp in cps(0, i, m):
                 cp.wait_send()
         if k == 4:
             for kk in (1, 2, 3):
-                for cp in cps(kk, i, hr):
+                for cp in cps(kk, i, m):
                     cp.wait_send()
-        reduce(k, i, hr)
-
-    def leave(k, i, hr):
-        for cp in cps(k, i, hr):
+        reduce(k, i, m)
+
+    def leave(k, i, m):
+        for cp in cps(k, i, m):
             cp.start()
 
     def both(f, k, t):
         i = t - RS_AT[k]
 
-        @pl.when((i >= 0) & (i < NCH))
-        def _():
-            f(k, i, HR)
-
-        @pl.when((i >= NCH) & (i < NALL))
-        def _():
-            f(k, i, 0)
+        for m, lo, hi in ((0, 0, NF), (1, NF, NF + NWG), (2, NF + NWG, NALL)):
+
+            @pl.when((i >= lo) & (i < hi))
+            def _(m=m):
+                f(k, i, m)
 
     def ag_arrive(k, t):
-        w = t - AG_AT[k] - NCH
+        w = t - AG_AT[k] - NF
 
         @pl.when((w >= 0) & (w < NWG))
         def _():
@@ -617,7 +635,7 @@
                 flush(w).wait()
 
     def ag_leave(k, t):
-        w = t - (AG_AT[k - 1] if k else RS_AT[4]) - NCH
+        w = t - (AG_AT[k - 1] if k else RS_AT[4]) - NF
 
         @pl.when((w >= 0) & (w < NWG))
         def _():
@@ -679,7 +697,7 @@
 
     T = 9
     loops = lambda f, a, b: lax.fori_loop(a, b, f, 0)
-    W = 3 * SPW
+    W = W_AT[3]
     for t in range(MEET):
         tick(t)
         if t == 0:
@@ -693,13 +711,13 @@
             wload(t - W, 1).start()
         if W + 1 <= t < W + 5:
             project_part(t - W - 1)
-        if t == W + 3:
+        if t == W + 2:
             rate.wait()
             loops(update, 0, 8)
             hand.start()
-        if t == W + 4:
+        if t == W + 3:
             loops(inner, 0, 8)
-        if t == W + 6:
+        if t == W + HAND:
             hand.wait()
             loops(outer, 0, 8)
             gating()
@@ -715,7 +733,8 @@
     lax.fori_loop(NCH + 4 * SP - MEET, T, ffn_tick, 0)
     stages(T)
     keep, scale_mid, scale_out, scale_in = [scal[:, n : n + 1] for n in range(4)]
-    output[...] = (ACC[...] * keep).astype(bf)
+    OUT[...] = (ACC[...] * keep).astype(bf)
+    outs[0].start()
     n2 = mid[...].astype(f32)
     dm = dtok[...]
     gm = go[...].astype(f32) + scale_mid * (dm - n2 * jnp.mean(dm * n2, axis=1, keepdims=True))
@@ -777,11 +796,11 @@
         j, cp = p // 4, lax.rem(p, 4)
         lo = pl.multiple_of(cp * 128, 128)
         rr = jnp.concatenate([R[j, :, pl.ds(lo, 128)], R[j, :, pl.ds(lo + 512, 128)]], axis=1)
-        store(lax.rem(p, NCH), 0, dot(LT[jnp.minimum(j, 1)], rr), y)
+        store(p // 3, lax.rem(p, 3), dot(LT[jnp.minimum(j, 1)], rr), y)
 
     def wg_tick(t, _):
         stages(t)
-        p = t - NCH
+        p = t - NF
         wgrad(p)
 
         @pl.when(p < 8)
@@ -815,6 +834,7 @@
             n1 = NM[...].astype(f32)
             dn = ACC[...]
             dtok[...] = dtok[...] + scale_in * (dn - n1 * jnp.mean(dn * n1, axis=1, keepdims=True))
+            outs[1].start()
 
         return 0
 
@@ -825,12 +845,12 @@
 
     wbload(0).start()
     wbload(1).start()
-    lax.fori_loop(NCH, NCH + NWG, wg_tick, 0)
+    lax.fori_loop(NF, NF + NWG, wg_tick, 0)
     def tail(t, _):
         stages(t)
         return 0
 
-    lax.fori_loop(NALL, NALL + AG_AT[2], tail, 0)
+    lax.fori_loop(NF + NWG, NF + NWG + AG_AT[2], tail, 0)
 
     def drain(w, _):
         for k in (1, 2):
@@ -839,6 +859,8 @@
         return 0
 
     lax.fori_loop(0, NWG, drain, 0)
+
+    outs[2].start()
 
     def drain_gather(i, _):
         for k in range(4):
@@ -854,6 +876,8 @@
         for k in range(3):
             for cp in wst(k, j):
                 cp.wait_send()
+    for cp in outs:
+        cp.wait()
 
 
 def layer_call(*ins):
@@ -862,20 +886,20 @@
     act, w = (512, 1024), (1024, 512)
     outs = [S(act, bf), S(act, f32), S((3, 64, 1408), f32), S((NWG, 4, 2, 2, 64, 128), bf), S((NCH, 4, 3, 2, 2, 2, 64, 128), bf)] + [S(w, bf)] * 4 + [S(act, bf)]
     scratch = [V((NCH, 3, 64, 128), bf), V((4,) + w, bf), V((2,) + act, bf),
-               V((NCH, 2, 3, 4, 2, 2, 64, 128), bf), V((2, 3, 4, 2, 2, 64, 128), bf), V((4, 3, 4, 2, 64, 128), bf), V((4, 3, 4, 64, 128), bf),
-               V((4, 3, 4, 64, 128), bf), V((4, 3, 3, 64, 128), bf), V((4, 64, 128), bf), V((2, 4, 3, 2, 2, 64, 256), bf),
+               V((NCH, 2, 3, 4, 2, 2, 64, 128), bf), V((2, 3, 4, 2, 2, 64, 128), bf), V((SLOT1, 3, 4, 2, 64, 128), bf), V((SLOTS, 3, 4, 64, 128), bf),
+               V((4, 3, 4, 64, 128), bf), V((SLOTS, 3, 3, 64, 128), bf), V((4, 64, 128), bf), V((2, 4, 3, 2, 2, 64, 256), bf),
                V((2,) + w, bf), V(act, f32), V(act, f32), V((5,) + act, bf), V(act, bf), V(act, bf), V(act, bf), V(act, bf), V(act, bf),
-               V((512, 4), f32), V((2, 8, 128), f32)] + [V((8, 128, 128), bf)] * 5
+               V((512, 4), f32), V((2, 8, 128), f32)] + [V((8, 128, 128), bf)] * 5 + [V(act, bf), V(act, bf), V(act, f32), V((3, 64, 1408), f32)]
     n, m, a = (NCH,), (NALL,), (NWG,)
     scratch += [D(s) for s in ((NCH, 3), (NCH, 3), (NCH, 2, 3), (NCH, 2, 3), (NCH, 2, 3), (NCH, 2, 3), (2,), (2,), (2,), (2,), n, n,
                                (5,), (5,), (5,), (5,), (5, 2), (5, 2), (), (), (), (), (), (10,),
                                (2, 2), (2,), (), (), m, m, (NALL, 2), (NALL, 2), (NALL, 2), (NALL, 2), (NALL, 3), (NALL, 3),
-                               (NWG, 3), (NWG, 3), a, a, a, a, a)]
+                               (NWG, 3), (NWG, 3), a, a, a, a, a, (5,))]
     return pl.pallas_call(
         layer_kernel,
         out_shape=outs,
-        in_specs=[VM, VM, pl.BlockSpec(memory_space=pltpu.SMEM)] + [VM] * 4 + [A] * 5,
-        out_specs=[VM] * 3 + [A] * 7,
+        in_specs=[A, A] + [pl.BlockSpec(memory_space=pltpu.SMEM)] * 2 + [VM] * 3 + [A] * 5,
+        out_specs=[A] * 10,
         scratch_shapes=scratch,
         compiler_params=pltpu.CompilerParams(collective_id=1, has_side_effects=True, vmem_limit_bytes=67043328),
     )(*ins)
@@ -910,9 +934,8 @@
     )(o, sh, out, dtok)
 
 def fast_body(tokens, lengths, decay, w_query, w_key, w_value, w_gate, w_out, f_value, f_gate, f_out, cotangent):
-    dec = jnp.concatenate([jnp.broadcast_to(decay[:, None], (4, 128)), jnp.zeros((4, 128), f32)])
     weights = (w_query, w_key, w_value, w_gate, w_out)
-    output, d_tokens, shares, grads, *_ = layer_call(tokens, cotangent, lengths, dec, f_value, f_gate, f_out.T, *weights)
+    output, d_tokens, shares, grads, *_ = layer_call(tokens, cotangent, lengths, decay, f_value, f_gate, f_out.T, *weights)
     *results, d_f_out = finish_call(grads.reshape(NWG, 1024, 128), shares, output, d_tokens)
     return (*results, d_f_out.T)
 

time: 285 us -> 278 us (0.975)
  Pallas kernels: 282 us -> 277 us
    pallas_call x1, Pallas kernels: 272 us -> 267 us  [layer_call(): pl.pallas_call(layer_kernel, out_shape=outs, in_specs=[A, A] + [pl.BlockS...]
where the time goes in v5:
time: 278 us
  Pallas kernels  277 us (100%)
    pallas_call x1, Pallas kernels, layer_call(): pl.pallas_call(layer_kernel, out_shape=outs, in_specs=[A, A] + [pl.BlockS...  267 us
    pallas_call x1, Pallas kernels, finish_call(): pl.pallas_call(finish_kernel, grid=(4,), out_shape=[S((512, 1024), bf), S...  9.79 us

profile of v5, /device:TPU:1, one launch (start us, length us, event | category | flops | bytes accessed | tf_op | source)
XLA Modules:
  0.0 278.1 jit_solution(1102304047889821577)
XLA Ops:
  1.3 266.9 %shard_map.195 = (bf16[512,1024]{1,0:T(8,128)(2,1)}, f32[512,1024]{1,0:T(8,128)}, f32[3,64,1408]{2,1,0:T(8,128)}, bf16[20,4,2,2,64,128]{5,4,3,2,1,0:T(8,128)(2,1...) custom-call(bf16[512,1024]{1,0:T(8,128)(2,1)} %tokens.1, ...), custom_call_target="tpu_custom_call" | custom-call | tf_op jit(solution)/shard_map/pallas_call | solution.py:898
  268.2 9.8 %shard_map.196 = (bf16[512,1024]{1,0:T(8,128)(2,1)}, f32[512,1024]{1,0:T(8,128)}, f32[1024,512]{1,0:T(8,128)}, f32[1024,512]{1,0:T(8,128)}, f32[1024,512]{1,0:T(...) custom-call(bf16[20,1024,128]{2,1,0:T(8,128)(2,1)} %bitcast.3, ...), custom_call_target="tpu_custom_call" | custom-call | tf_op jit(solution)/shard_map/pallas_call | solution.py:927

commit v6 on v5

--- a/solution.py
+++ b/solution.py
@@ -284,14 +284,15 @@
 MEET = 10
 W_AT = (0, 2, 4, 5)
 HAND = 4
+RN = 16
 SLOTS = 4
-SLOT1 = 4
+SLOT1 = 6
 NF = NCH
 NWG = 20
 NALL = NCH + NWG
 
-RS_AT = (1, 2, 4, 6, 8)
-AG_AT = (10, 12, 14)
+RS_AT = (1, 2, 5, 7, 9)
+AG_AT = (11, 13, 15)
 TN = (((0,), (0,)), ((), ()))
 bf = jnp.bfloat16
 f32 = jnp.float32
@@ -378,9 +379,9 @@
 
     def near(k):
         if k == 0:
-            return [rc(S.at[:, :, 0:RA], W3.at[:, z, :, x, c, y, 0:RA], nxs.at[0], nxr.at[0], X),
-                    rc(S.at[:, :, RA:64], W3.at[:, z, :, x, c, y, RA:64], nys.at[0], nyr.at[0], Y)]
-        a, b = W3.at[:, z, :, :, c, y, 0:RA], W3.at[:, z, :, x, c, :, RA:64]
+            return [rc(S.at[:, :, 0:RN], W3.at[:, z, :, x, c, y, 0:RN], nxs.at[0], nxr.at[0], X),
+                    rc(S.at[:, :, RN:64], W3.at[:, z, :, x, c, y, RN:64], nys.at[0], nyr.at[0], Y)]
+        a, b = W3.at[:, z, :, :, c, y, 0:RN], W3.at[:, z, :, x, c, :, RN:64]
         return [rc(b, b, nxs.at[1], nxr.at[1], X), rc(a, a, nys.at[1], nyr.at[1], Y)]
 
     def quarter(r):
@@ -926,10 +927,10 @@
     whole = lambda *s: pl.BlockSpec(s, lambda i: (0,) * len(s))
     return pl.pallas_call(
         finish_kernel,
-        grid=(4,),
+        grid=(2,),
         out_shape=[S((512, 1024), bf), S((512, 1024), f32)] + [S((1024, 512), f32)] * 4 + [S((512, 1024), f32)] + [S((64, 1408), f32)] * 3,
-        in_specs=[pl.BlockSpec((20, 256, 128), lambda i: (0, i, 0)), whole(3, 64, 1408)] + [pl.BlockSpec((128, 1024), lambda i: (i, 0))] * 2,
-        out_specs=[pl.BlockSpec((128, 1024), lambda i: (i, 0))] * 2 + [pl.BlockSpec((256, 512), lambda i: (i, 0))] * 4 + [pl.BlockSpec((512, 256), lambda i: (0, i))] + [whole(64, 1408)] * 3,
+        in_specs=[pl.BlockSpec((20, 512, 128), lambda i: (0, i, 0)), whole(3, 64, 1408)] + [pl.BlockSpec((256, 1024), lambda i: (i, 0))] * 2,
+        out_specs=[pl.BlockSpec((256, 1024), lambda i: (i, 0))] * 2 + [pl.BlockSpec((512, 512), lambda i: (i, 0))] * 4 + [pl.BlockSpec((512, 512), lambda i: (0, i))] + [whole(64, 1408)] * 3,
         compiler_params=pltpu.CompilerParams(vmem_limit_bytes=67043328),
     )(o, sh, out, dtok)
 

time: 278 us -> 275 us (0.989)
  Pallas kernels: 277 us -> 273 us
where the time goes in v6:
time: 275 us
  Pallas kernels  273 us (99%)
    pallas_call x1, Pallas kernels, layer_call(): pl.pallas_call(layer_kernel, out_shape=outs, in_specs=[A, A] + [pl.BlockS...  265 us
    pallas_call x1, Pallas kernels, finish_call(): pl.pallas_call(finish_kernel, grid=(2,), out_shape=[S((512, 1024), bf), S...  8.62 us

profile of v6, /device:TPU:1, one launch (start us, length us, event | category | flops | bytes accessed | tf_op | source)
XLA Modules:
  0.0 275.0 jit_solution(16896581975999927632)
XLA Ops:
  1.3 264.9 %shard_map.195 = (bf16[512,1024]{1,0:T(8,128)(2,1)}, f32[512,1024]{1,0:T(8,128)}, f32[3,64,1408]{2,1,0:T(8,128)}, bf16[20,4,2,2,64,128]{5,4,3,2,1,0:T(8,128)(2,1...) custom-call(bf16[512,1024]{1,0:T(8,128)(2,1)} %tokens.1, ...), custom_call_target="tpu_custom_call" | custom-call | tf_op jit(solution)/shard_map/pallas_call | solution.py:899
  266.2 8.6 %shard_map.196 = (bf16[512,1024]{1,0:T(8,128)(2,1)}, f32[512,1024]{1,0:T(8,128)}, f32[1024,512]{1,0:T(8,128)}, f32[1024,512]{1,0:T(8,128)}, f32[1024,512]{1,0:T(...) custom-call(bf16[20,1024,128]{2,1,0:T(8,128)(2,1)} %bitcast.3, ...), custom_call_target="tpu_custom_call" | custom-call | tf_op jit(solution)/shard_map/pallas_call | solution.py:928
